TPU v7x, 32 devices: a whole 2x2x4 slice. The times are simulated.
32 devices in a mesh: gossip: 4 (over z), fsdp: 2 (over y), tensor: 4 (over x, core).
Axes of the slice: x: 2, y: 2, z: 4, core: 2. Of those that a mesh axis runs over, the one named last changes fastest.
Arguments:
- hidden: bfloat16 [4, 4, 256, 4096], P('gossip', 'fsdp', None, 'tensor'), may hold values from -6 to 6
- cotangent: bfloat16 [4, 4, 256, 4096], P('gossip', 'fsdp', None, 'tensor'), may hold values from -6 to 6
- documents: int32 [4, 4, 256], P('gossip', 'fsdp'), may hold values from 0 to 7, never falling along the last dimension, each value on 1 to 128 neighbouring positions
- q_weight: float32 [4, 4096, 2048], P('gossip', 'fsdp', 'tensor'), may hold values from -0.09375 to 0.09375
- k_weight: float32 [4, 4096, 512], P('gossip', 'fsdp', 'tensor'), may hold values from -0.09375 to 0.09375
- v_weight: float32 [4, 4096, 512], P('gossip', 'fsdp', 'tensor'), may hold values from -0.09375 to 0.09375
- o_weight: float32 [4, 4096, 2048], P('gossip', 'fsdp', 'tensor'), may hold values from -0.125 to 0.125
- edge_weight: float32 [4], P('gossip'), may hold values from 0.1 to 0.45
Outputs:
- new_q_weight: float32 [4, 4096, 2048], P('gossip', 'fsdp', 'tensor')
- new_k_weight: float32 [4, 4096, 512], P('gossip', 'fsdp', 'tensor')
- new_v_weight: float32 [4, 4096, 512], P('gossip', 'fsdp', 'tensor')
- new_o_weight: float32 [4, 4096, 2048], P('gossip', 'fsdp', 'tensor')
Inputs may be any that keep to these rules, and one draw needn't show every extreme that they name: `documents`: document ids never fall along a sequence; each document spans 1 to 128 positions, and some document spans exactly 128.
All inputs are finite; a program needn't handle non-finite values.
Results may differ from a plain program's by a relative error of at most 0.007.
Values may be sent and summed in bfloat16 or wider, within the bound.
No kernel may reach another device: no remote copies, remote signals or barrier semaphores. Data moves between devices by JAX's collectives and lax.ppermute only.
A program may use at most 128 MiB of HBM per device.

v0:
```python
import math

import jax
import jax.numpy as jnp
from jax import lax
from jax.sharding import PartitionSpec as P

HD = 128


rope_theta = 500000.0
learn_rate = 0.001
norm_eps = 1e-05


def passed_along(shard, axis, by):
    count = lax.axis_size(axis)
    return lax.ppermute(shard, axis, [(i, (i + by) % count) for i in range(count)])


def contract(form, left, right):
    return jnp.einsum(form, left, right, preferred_element_type=jnp.float32)


def rope_tables(length, head_size):
    half_dim = head_size // 2
    positions = jnp.arange(length, dtype=jnp.float32)
    freqs = jnp.exp(
        jnp.arange(half_dim, dtype=jnp.float32) * (-2.0 / head_size * math.log(rope_theta))
    )
    angles = positions[:, None] * freqs[None, :]
    return (jnp.cos(angles), jnp.sin(angles))


def rotate(values, cosine, sine_table):
    half_dim = values.shape[-1] // 2
    first_half = values[..., :half_dim]
    second_half = values[..., half_dim:]
    return jnp.concatenate(
        [
            first_half * cosine - second_half * sine_table,
            second_half * cosine + first_half * sine_table,
        ],
        -1,
    )


def unrotate(values, cosine, sine_table):
    half_dim = values.shape[-1] // 2
    first_half = values[..., :half_dim]
    second_half = values[..., half_dim:]
    return jnp.concatenate(
        [
            first_half * cosine + second_half * sine_table,
            second_half * cosine - first_half * sine_table,
        ],
        -1,
    )


def attention_grads(proj, d_ctx, documents, heads_q, heads_k):
    seq_count, length = documents.shape
    group_size = heads_q // heads_k
    q_cols = heads_q * HD
    kv_cols = heads_k * HD
    cosine, sine_table = rope_tables(length, HD)
    cos_query = cosine[None, :, None, None, :]
    sin_query = sine_table[None, :, None, None, :]
    cos_key = cosine[None, :, None, :]
    sin_key = sine_table[None, :, None, :]
    query = rotate(
        proj[..., :q_cols].reshape(seq_count, length, heads_k, group_size, HD), cos_query, sin_query
    ).astype(jnp.bfloat16)
    key_rot = rotate(
        proj[..., q_cols : q_cols + kv_cols].reshape(seq_count, length, heads_k, HD),
        cos_key,
        sin_key,
    ).astype(jnp.bfloat16)
    value_b = (
        proj[..., q_cols + kv_cols :].reshape(seq_count, length, heads_k, HD).astype(jnp.bfloat16)
    )
    d_out = d_ctx.reshape(seq_count, length, heads_k, group_size, HD).astype(jnp.bfloat16)
    score_scale = 1.0 / math.sqrt(HD)
    scores = contract("bqhgd,bkhd->bhgqk", query, key_rot) * score_scale
    positions = jnp.arange(length)
    causal = positions[:, None] >= positions[None, :]
    same_doc = documents[:, :, None] == documents[:, None, :]
    allowed = (causal[None] & same_doc)[:, None, None, :, :]
    exp_scores = jnp.where(allowed, jnp.exp(scores), 0.0)
    probs_f = exp_scores / jnp.sum(exp_scores, -1, keepdims=True)
    probs_b = probs_f.astype(jnp.bfloat16)
    context = contract("bhgqk,bkhd->bqhgd", probs_b, value_b).astype(jnp.bfloat16)
    d_probs = contract("bqhgd,bkhd->bhgqk", d_out, value_b)
    d_value = contract("bhgqk,bqhgd->bkhd", probs_b, d_out).astype(jnp.bfloat16)
    delta_sum = jnp.sum(probs_f * d_probs, -1, keepdims=True)
    d_scores = (probs_f * (d_probs - delta_sum) * score_scale).astype(jnp.bfloat16)
    d_query = contract("bhgqk,bkhd->bqhgd", d_scores, key_rot)
    d_key = contract("bhgqk,bqhgd->bkhd", d_scores, query)
    d_query = unrotate(d_query, cos_query, sin_query).astype(jnp.bfloat16)
    d_key = unrotate(d_key, cos_key, sin_key).astype(jnp.bfloat16)
    d_proj = jnp.concatenate(
        [
            d_query.reshape(seq_count, length, q_cols),
            d_key.reshape(seq_count, length, kv_cols),
            d_value.reshape(seq_count, length, kv_cols),
        ],
        -1,
    )
    return (d_proj, context.reshape(seq_count, length, q_cols))


def mix_three(center, from_low, from_high, c_low, c_high):
    return center + c_low * (from_low - center) + c_high * (from_high - center)


def body(hidden, cotangent, documents, q_weight, k_weight, v_weight, o_weight, edge_weight):
    full_hidden, full_cotan = (
        lax.all_gather(hidden, "tensor", axis=3, tiled=True),
        lax.all_gather(cotangent, "tensor", axis=3, tiled=True),
    )
    seq_count, length, model_width = full_hidden.shape[1:]
    token_rows = seq_count * length
    hidden_f = full_hidden[0].reshape(token_rows, model_width).astype(jnp.float32)
    normed = (
        hidden_f * lax.rsqrt(jnp.mean(hidden_f * hidden_f, -1, keepdims=True) + norm_eps)
    ).astype(jnp.bfloat16)
    cotan_rows = full_cotan[0].reshape(token_rows, model_width)
    q_cols = q_weight.shape[2]
    kv_cols = k_weight.shape[2]
    proj_cols = q_cols + 2 * kv_cols
    packed = jnp.concatenate([q_weight[0], k_weight[0], v_weight[0], o_weight[0]], 1).astype(
        jnp.bfloat16
    )
    block_rows = lax.all_gather(packed, "fsdp", axis=0, tiled=True)
    left = normed
    right = cotan_rows
    proj = jnp.dot(left, block_rows[:, :proj_cols], preferred_element_type=jnp.float32)
    d_ctx = jnp.dot(right, block_rows[:, proj_cols:], preferred_element_type=jnp.float32)
    d_proj, context = attention_grads(
        proj.reshape(seq_count, length, proj_cols),
        d_ctx.reshape(seq_count, length, q_cols),
        documents[0],
        q_cols // HD,
        kv_cols // HD,
    )
    d_proj = d_proj.reshape(token_rows, proj_cols)
    context = context.reshape(token_rows, q_cols)
    contract_rows = (((0,), (0,)), ((), ()))
    left = normed
    right = cotan_rows
    first_part = lax.dot_general(left, d_proj, contract_rows, preferred_element_type=jnp.float32)
    second_part = lax.dot_general(right, context, contract_rows, preferred_element_type=jnp.float32)
    gradients = lax.psum_scatter(
        jnp.concatenate([first_part, second_part], 1).astype(jnp.bfloat16),
        "fsdp",
        scatter_dimension=0,
        tiled=True,
    ).astype(jnp.float32)
    grad_q = gradients[None, :, :q_cols]
    grad_k = gradients[None, :, q_cols : q_cols + kv_cols]
    grad_v = gradients[None, :, q_cols + kv_cols : proj_cols]
    grad_o = gradients[None, :, proj_cols:]
    c_high = edge_weight[0]
    new_q = q_weight - learn_rate * grad_q
    new_k = k_weight - learn_rate * grad_k
    new_v = v_weight - learn_rate * grad_v
    new_o = o_weight - learn_rate * grad_o
    from_low = passed_along((new_q, new_k, new_v, new_o, edge_weight), "gossip", 1)
    from_high = passed_along((new_q, new_k, new_v, new_o), "gossip", -1)
    c_low = from_low[4][0]
    return (
        mix_three(new_q, from_low[0], from_high[0], c_low, c_high),
        mix_three(new_k, from_low[1], from_high[1], c_low, c_high),
        mix_three(new_v, from_low[2], from_high[2], c_low, c_high),
        mix_three(new_o, from_low[3], from_high[3], c_low, c_high),
    )


def solution(mesh):
    return jax.shard_map(
        body,
        mesh=mesh,
        in_specs=(
            P("gossip", "fsdp", None, "tensor"),
            P("gossip", "fsdp", None, "tensor"),
            P("gossip", "fsdp", None),
            P("gossip", "fsdp", "tensor"),
            P("gossip", "fsdp", "tensor"),
            P("gossip", "fsdp", "tensor"),
            P("gossip", "fsdp", "tensor"),
            P("gossip"),
        ),
        out_specs=(
            P("gossip", "fsdp", "tensor"),
            P("gossip", "fsdp", "tensor"),
            P("gossip", "fsdp", "tensor"),
            P("gossip", "fsdp", "tensor"),
        ),
        check_vma=False,
    )
```

profile of v0, /device:TPU:0, one launch (start us, length us, event | category | flops | bytes accessed | tf_op | source)
XLA Modules:
  0.0 878.4 jit_solution(919153522589254380)
XLA Ops:
  7.2 0.7 all-gather.4.cloned.1.call-update
  7.9 1.7 convert_bitcast_fusion.2
  9.6 4.0 convert_bitcast_fusion
  13.6 2.8 pad_maximum_fusion.1
  16.5 0.7 all-gather.8.cloned.1.call-update
  17.9 28.8 %all-gather.4.cloned.1.call-done = bf16[1,2,256,4096]{3,2,1,0:T(8,128)(2,1)} async-done(((bf16[1,2,256,1024]{3,2,1,0:T(8,128)(2,1)}), bf16[1,2,256,4096]{3,2,1,0:T(8,128)(2,1)}) %all-gather.4.cloned.1.call-update) | async-done | bytes 4194320 | tf_op jit(solution)/shard_map/all_gather | solution.py:118
  46.8 3.2 multiply_reduce_fusion
  50.2 3.4 fusion.1
  53.6 124.3 %all-gather.6.cloned.1.call-done = bf16[4096,1280]{1,0:T(8,128)(2,1)} async-done(((bf16[2048,1280]{1,0:T(8,128)(2,1)}), bf16[4096,1280]{1,0:T(8,128)(2,1)}) %all-gather.6.cloned.1.call-update) | async-done | bytes 10485776 | tf_op jit(solution)/shard_map/all_gather | solution.py:134
  177.9 7.3 fusion.2
  185.2 1.1 copy-done.9
  186.9 1.7 slice_bitcast_fusion.2
  189.2 24.8 %all-gather.8.cloned.1.call-done = bf16[1,2,256,4096]{3,2,1,0:T(8,128)(2,1)} async-done(((bf16[1,2,256,1024]{3,2,1,0:T(8,128)(2,1)}), bf16[1,2,256,4096]{3,2,1,0:T(8,128)(2,1)}) %all-gather.8.cloned.1.call-update) | async-done | bytes 4194320 | tf_op jit(solution)/shard_map/all_gather | solution.py:119
  214.0 6.7 fusion.23
  220.7 1.2 convert_element_type.97
  222.3 0.9 fusion.18
  223.2 1.7 fusion.13
  224.8 0.7 fusion.28
  226.7 0.7 fusion.27
  227.4 1.6 fusion.22
  230.9 5.0 fusion.3
  235.9 4.3 convolution_convert_fusion
  240.2 9.6 %pad_maximum_fusion = bf16[4096,1280]{0,1:T(8,128)(2,1)} fusion(bf16[4096,512]{0,1:T(8,128)(2,1)S(1)} %fusion.3, bf16[4096,768]{0,1:T(8,128)(2,1)S(1)} %convolution_convert_fusion), kind=kLoop, calls=%fused_computation | loop fusion | flops 20971520 | bytes 20971520 | tf_op jit(solution)/shard_map/concatenate | solution.py:154
  249.8 5.3 copy.49
  255.2 6.0 copy.52
  261.2 1.3 copy.50
  262.5 1.3 copy.51
  263.8 108.0 %reduce-scatter.2.cloned.1.call-done = bf16[2048,1280]{0,1:T(8,128)(2,1)} async-done(((bf16[4096,1280]{0,1:T(8,128)(2,1)}), bf16[2048,1280]{0,1:T(8,128)(2,1)}) %reduce-scatter.2.cloned.1.call-update) | async-done | bytes 5242896 | tf_op jit(solution)/shard_map/reduce_scatter | solution.py:153
  371.8 4.0 convert_element_type.107
  375.9 4.0 copy-done
  380.3 1.5 collective-permute-start.5
  382.1 10.4 %fusion.6 = (f32[1,2048,512]{1,2,0:T(8,128)}, f32[1,2048,512]{1,2,0:T(8,128)}) fusion(f32[1,2048,512]{1,2,0:T(8,128)} %copy.52, f32[2048,1280]{0,1:T(8,128)} %copy-done, f32[1,2048,512]{1,2,0:T(8,128)S(1)} %copy-done.2), kind=kLoop, calls=%fused_computation.14 | loop fusion | flops 4194304 | bytes 25165824 | tf_op jit(solution)/shard_map/sub | solution.py:167
  392.5 1.5 collective-permute-start.7
  394.0 2.3 collective-permute-start.8
  396.3 1.5 collective-permute-start.6
  398.3 210.9 %collective-permute-done = f32[1]{0:T(128)} collective-permute-done((f32[1]{0:T(128)}, f32[1]{0:T(128)}, u32[]{:S(2)}, u32[]{:S(2)}) %collective-permute-start) | collective-permute-done | bytes 36 | tf_op jit(solution)/shard_map/ppermute | solution.py:18
  609.3 3.8 collective-permute-start.2
  613.1 202.5 %collective-permute-done.3 = f32[1,2048,128]{1,2,0:T(8,128)S(1)} collective-permute-done((f32[1,2048,128]{1,2,0:T(8,128)S(1)}, f32[1,2048,128]{1,2,0:T(8,128)S(1)}, u32[]{:S(2)}, u32[]{:S(2)}) %collective-permute-start.3) | collective-permute-done | bytes 1048608 | tf_op jit(solution)/shard_map/ppermute | solution.py:18
  815.6 1.0 copy-done.10
  817.2 2.2 multiply_add_fusion.2
  819.4 1.3 copy.55
  820.7 18.3 %collective-permute-done.4 = f32[1,2048,128]{1,2,0:T(8,128)} collective-permute-done((f32[1,2048,128]{1,2,0:T(8,128)S(1)}, f32[1,2048,128]{1,2,0:T(8,128)}, u32[]{:S(2)}, u32[]{:S(2)}) %collective-permute-start.4) | collective-permute-done | bytes 1048608 | tf_op jit(solution)/shard_map/ppermute | solution.py:18
  839.0 2.5 multiply_add_fusion.3
  841.5 1.3 copy.54
  842.8 9.2 %multiply_add_fusion = f32[1,2048,512]{1,2,0:T(8,128)} fusion(f32[1,2048,512]{1,2,0:T(8,128)} %collective-permute-done.8, f32[1,2048,512]{1,2,0:T(8,128)} %get-tuple-element.12, f32[1,2048,512]{1,2,0:T(8,128)} %collective-permute-done.7, f32[]{:T(128)} %bitcast.169, f32[]{:T(128)} %bitcast.46), kind=kLoop, calls=%fused_computation.21 | loop fusion | flops 6291456 | bytes 16777224 | tf_op jit(solution)/shard_map/add | solution.py:113
  852.0 5.3 copy.56
  857.3 9.2 %multiply_add_fusion.1 = f32[1,2048,512]{1,2,0:T(8,128)} fusion(f32[1,2048,512]{1,2,0:T(8,128)} %collective-permute-done.2, f32[1,2048,512]{1,2,0:T(8,128)} %get-tuple-element.13, f32[1,2048,512]{1,2,0:T(8,128)} %collective-permute-done.1, f32[]{:T(128)} %bitcast.167, f32[]{:T(128)} %bitcast.46), kind=kLoop, calls=%fused_computation.22 | loop fusion | flops 6291456 | bytes 16777224 | tf_op jit(solution)/shard_map/add | solution.py:113
  866.6 5.3 copy.53
  (58 shorter events, 6.8 us)
Async XLA Ops:
  7.2 39.6 %all-gather.4.cloned.1.call-start = ((), (), s32[]{:S(2)}) async-start(), calls=%async_computation.1 | async-start | bytes 5242880 | tf_op jit(solution)/shard_map/all_gather | solution.py:118
  7.9 170.0 %all-gather.6.cloned.1.call-start = ((), (), s32[]{:S(2)}) async-start(), calls=%async_computation.2 | async-start | bytes 15728640 | tf_op jit(solution)/shard_map/all_gather | solution.py:134
  16.4 0.9 copy-start.11
  16.4 197.5 %all-gather.8.cloned.1.call-start = ((), (), s32[]{:S(2)}) async-start(), calls=%async_computation.3 | async-start | bytes 5242880 | tf_op jit(solution)/shard_map/all_gather | solution.py:119
  17.2 354.7 %reduce-scatter.2.cloned.1.call-start = ((), (), s32[]{:S(2)}) async-start(), calls=%async_computation.4 | async-start | bytes 15728640 | tf_op jit(solution)/shard_map/reduce_scatter | solution.py:153
  46.8 3.4 copy-start.1
  185.2 1.1 copy-start.9
  214.0 7.9 copy-start.8
  230.9 5.0 copy-start.3
  255.2 6.0 copy-start.4
  255.2 7.3 copy-start.5
  371.8 8.1 copy-start.6
  371.8 8.1 copy-start.7
  375.9 4.0 copy-start
  379.9 2.2 copy-start.2
  380.3 229.0 %collective-permute-start.5 = (f32[1,2048,128]{1,2,0:T(8,128)S(1)}, f32[1,2048,128]{1,2,0:T(8,128)}, u32[]{:S(2)}, u32[]{:S(2)}) collective-permute-start(f32[1,2048,128]{1,2,0:T(8,128)S(1)} %get-tuple-element.14), channel_id=1, source_target_pairs={{0,8},{8,16},{16,24},{24,0},{1,9},{9,17},{17,25},{25,1},{2,10},{10... | collective-permute-start | bytes 3145736 | tf_op jit(solution)/shard_map/ppermute | solution.py:18
  392.5 450.3 %collective-permute-start.7 = (f32[1,2048,512]{1,2,0:T(8,128)}, f32[1,2048,512]{1,2,0:T(8,128)}, u32[]{:S(2)}, u32[]{:S(2)}) collective-permute-start(f32[1,2048,512]{1,2,0:T(8,128)} %get-tuple-element.12), channel_id=1, source_target_pairs={{0,8},{8,16},{16,24},{24,0},{1,9},{9,17},{17,25},{25,1},{2,10},{10... | collective-permute-start | bytes 12582920 | tf_op jit(solution)/shard_map/ppermute | solution.py:18
  394.0 448.8 %collective-permute-start.8 = (f32[1,2048,512]{1,2,0:T(8,128)}, f32[1,2048,512]{1,2,0:T(8,128)}, u32[]{:S(2)}, u32[]{:S(2)}) collective-permute-start(f32[1,2048,512]{1,2,0:T(8,128)} %get-tuple-element.12), channel_id=1, source_target_pairs={{0,24},{8,0},{16,8},{24,16},{1,25},{9,1},{17,9},{25,17},{2,26},{10... | collective-permute-start | bytes 12582920 | tf_op jit(solution)/shard_map/ppermute | solution.py:18
  396.3 216.8 %collective-permute-start.6 = (f32[1,2048,128]{1,2,0:T(8,128)S(1)}, f32[1,2048,128]{1,2,0:T(8,128)S(1)}, u32[]{:S(2)}, u32[]{:S(2)}) collective-permute-start(f32[1,2048,128]{1,2,0:T(8,128)S(1)} %get-tuple-element.14), channel_id=1, source_target_pairs={{0,24},{8,0},{16,8},{24,16},{1,25},{9,1},{17,9},{25,17},{2,26},{10... | collective-permute-start | bytes 3145736 | tf_op jit(solution)/shard_map/ppermute | solution.py:18
  397.8 211.4 %collective-permute-start = (f32[1]{0:T(128)}, f32[1]{0:T(128)}, u32[]{:S(2)}, u32[]{:S(2)}) collective-permute-start(f32[1]{0:T(128)} %param.15), channel_id=1, source_target_pairs={{0,8},{8,16},{16,24},{24,0},{1,9},{9,17},{17,25},{25,1},{2,10},{10... | collective-permute-start | bytes 20 | tf_op jit(solution)/shard_map/ppermute | solution.py:18
  609.3 248.1 %collective-permute-start.1 = (f32[1,2048,512]{1,2,0:T(8,128)}, f32[1,2048,512]{1,2,0:T(8,128)}, u32[]{:S(2)}, u32[]{:S(2)}) collective-permute-start(f32[1,2048,512]{1,2,0:T(8,128)} %get-tuple-element.13), channel_id=1, source_target_pairs={{0,8},{8,16},{16,24},{24,0},{1,9},{9,17},{17,25},{25,1},{2,10},{10... | collective-permute-start | bytes 12582920 | tf_op jit(solution)/shard_map/ppermute | solution.py:18
  609.3 248.1 %collective-permute-start.2 = (f32[1,2048,512]{1,2,0:T(8,128)}, f32[1,2048,512]{1,2,0:T(8,128)}, u32[]{:S(2)}, u32[]{:S(2)}) collective-permute-start(f32[1,2048,512]{1,2,0:T(8,128)} %get-tuple-element.13), channel_id=1, source_target_pairs={{0,24},{8,0},{16,8},{24,16},{1,25},{9,1},{17,9},{25,17},{2,26},{10... | collective-permute-start | bytes 12582920 | tf_op jit(solution)/shard_map/ppermute | solution.py:18
  613.1 202.5 %collective-permute-start.3 = (f32[1,2048,128]{1,2,0:T(8,128)S(1)}, f32[1,2048,128]{1,2,0:T(8,128)S(1)}, u32[]{:S(2)}, u32[]{:S(2)}) collective-permute-start(f32[1,2048,128]{1,2,0:T(8,128)S(1)} %get-tuple-element.15), channel_id=1, source_target_pairs={{0,8},{8,16},{16,24},{24,0},{1,9},{9,17},{17,25},{25,1},{2,10},{10... | collective-permute-start | bytes 3145736 | tf_op jit(solution)/shard_map/ppermute | solution.py:18
  815.6 1.0 copy-start.10
  816.6 22.5 %collective-permute-start.4 = (f32[1,2048,128]{1,2,0:T(8,128)S(1)}, f32[1,2048,128]{1,2,0:T(8,128)}, u32[]{:S(2)}, u32[]{:S(2)}) collective-permute-start(f32[1,2048,128]{1,2,0:T(8,128)S(1)} %get-tuple-element.15), channel_id=1, source_target_pairs={{0,24},{8,0},{16,8},{24,16},{1,25},{9,1},{17,9},{25,17},{2,26},{10... | collective-permute-start | bytes 3145736 | tf_op jit(solution)/shard_map/ppermute | solution.py:18
Sparse Core Ops, SparseCore 0:
  9.6 37.1 all-gather.3
  48.3 129.5 all-gather.5
  179.4 34.4 all-gather.7
  249.9 121.8 reduce-scatter.1
where the time goes:
time: 879 us; the launch traced here: 878 us
  waiting for transfers between devices  719 us (82%)
  other arithmetic  65.3 us (7%)
  local copies, waits for them, and re-layouts  38.7 us (4%)
  matrix products  29.3 us (3%)
  between operations  14.7 us (2%)
  starting transfers between devices  11.4 us (1%)
    ppermute x9, waiting for transfers between devices, passed_along(): lax.ppermute(shard, axis, [(i, (i + by) % count) for i in range(count)])  432 us
    all_gather x1, waiting for transfers between devices, body(): block_rows = lax.all_gather(packed, 'fsdp', axis=0, tiled=True)  124 us
    reduce_scatter x1, waiting for transfers between devices, body(): lax.psum_scatter(jnp.concatenate([first_part, second_part], 1).astype(jnp...  108 us
    unnamed x34, local copies, waits for them, and re-layouts  33.9 us
    all_gather x1, waiting for transfers between devices, body(): lax.all_gather(hidden, 'tensor', axis=3, tiled=True)  28.8 us
    all_gather x1, waiting for transfers between devices, body(): lax.all_gather(cotangent, 'tensor', axis=3, tiled=True)  24.8 us
    add x4, other arithmetic, mix_three(): return center + c_low * (from_low - center) + c_high * (from_high - center)  23 us
  transfers between devices with their start and end apart: 13, of which 7 were waited for; matrix products, arithmetic and copies ran while one was open for 8% of the time, Pallas kernels for 0%

commit v1 on v0

v1 whole, which is shorter than its diff:
```python
import functools
import math

import jax
import jax.numpy as jnp
from jax import lax
from jax.experimental import pallas as pl
from jax.experimental.pallas import tpu as pltpu
from jax.sharding import PartitionSpec as P

HD = 128
F32 = jnp.float32
BF16 = jnp.bfloat16
BLOCK = 256

rope_theta = 500000.0
learn_rate = 0.001
norm_eps = 1e-05

NN = (((1,), (0,)), ((), ()))
NT = (((1,), (1,)), ((), ()))
TN = (((0,), (0,)), ((), ()))


def mm(left, right, form=NN):
    return lax.dot_general(left, right, form, preferred_element_type=F32)


def cost(flops, bytes_accessed, transcendentals=0):
    return pl.CostEstimate(
        flops=int(flops), bytes_accessed=int(bytes_accessed), transcendentals=int(transcendentals)
    )


def params(count):
    return pltpu.CompilerParams(
        dimension_semantics=("arbitrary",) * count, vmem_limit_bytes=40 * 1024 * 1024
    )


def passed_along(shard, axis, by):
    count = lax.axis_size(axis)
    return lax.ppermute(shard, axis, [(i, (i + by) % count) for i in range(count)])


def rope_tables(length, head_size):
    half_dim = head_size // 2
    positions = jnp.arange(length, dtype=F32)
    freqs = jnp.exp(jnp.arange(half_dim, dtype=F32) * (-2.0 / head_size * math.log(rope_theta)))
    angles = positions[:, None] * freqs[None, :]
    cosine, sine = jnp.cos(angles), jnp.sin(angles)
    return jnp.concatenate([cosine, cosine], 1), jnp.concatenate([-sine, sine], 1)


def after(value, *others):
    return lax.optimization_barrier((value, *others))[0]


def spread(shard, fsdp_count, tensor_count):
    share = tensor_count // fsdp_count
    near, far = [], []
    for g in range(fsdp_count):
        for t in range(tensor_count):
            x, lane = divmod(t, share)
            source = g * tensor_count + t
            across = x * tensor_count + (1 - x) * share + lane
            if x == g:
                near.append((source, across))
            else:
                near.append((source, x * tensor_count + t))
                far.append((source, across))
    axes = ("fsdp", "tensor")
    return lax.ppermute(shard, axes, near), lax.ppermute(shard, axes, far)


def swapped(block, tensor_count):
    return lax.ppermute(block, "tensor", [(t, t ^ 1) for t in range(tensor_count)])


def parity_halves(par_ref, w_ref, rows):
    par = par_ref[0]
    return (
        w_ref[pl.ds(pl.multiple_of(par * rows, rows), rows), :],
        w_ref[pl.ds(pl.multiple_of((1 - par) * rows, rows), rows), :],
    )


def project_kernel(par_ref, *refs):
    *pieces, w_ref, own_ref, oth_ref, sent_ref = refs
    _, tokens, rows = pieces[0].shape
    w_mine, w_theirs = parity_halves(par_ref, w_ref, rows)
    for part in range(len(pieces) // 2):
        mine, theirs = pieces[2 * part : 2 * part + 2]
        at = pl.ds(part * tokens, tokens)
        other = mm(mine[1], w_mine) + mm(theirs[1], w_theirs)
        sent_ref[at, :] = other.astype(BF16)
        oth_ref[at, :] = other
        own_ref[at, :] = mm(mine[0], w_mine) + mm(theirs[0], w_theirs)


def project(par, pieces, weight, at, cols):
    parts = len(pieces) // 2
    _, tokens, rows = pieces[0].shape
    if parts == 1:
        steps, unit = 2, cols
        piece = pl.BlockSpec((2, tokens // steps, rows), lambda i, p: (0, i, 0))
        whole = pl.BlockSpec((2 * rows, cols), lambda i, p: (0, at))
        out = pl.BlockSpec((tokens // steps, cols), lambda i, p: (i, 0))
    else:
        unit = 2 * HD
        steps = cols // unit
        piece = pl.BlockSpec((2, tokens, rows), lambda i, p: (0, 0, 0))
        whole = pl.BlockSpec((2 * rows, unit), lambda i, p: (0, at * steps + i))
        out = pl.BlockSpec((parts * tokens, unit), lambda i, p: (0, i))
    tokens = tokens * parts
    return pl.pallas_call(
        project_kernel,
        grid_spec=pltpu.PrefetchScalarGridSpec(
            num_scalar_prefetch=1,
            grid=(steps,),
            in_specs=[piece] * len(pieces) + [whole],
            out_specs=[out] * 3,
        ),
        out_shape=[jax.ShapeDtypeStruct((tokens, cols), kind) for kind in (F32, F32, BF16)],
        compiler_params=params(1),
        cost_estimate=cost(8 * tokens * rows * cols, 8 * tokens * rows + 10 * tokens * cols),
        name="project",
    )(par, *pieces, weight)


def rotated(values, cos, sin):
    return values * cos + pltpu.roll(values, HD // 2, 1) * sin


def unrotated(values, cos, sin):
    return values * cos - pltpu.roll(values, HD // 2, 1) * sin


def probabilities(query, key, mask):
    scores = mm(query, key, NT) * (1.0 / math.sqrt(HD))
    exp_scores = jnp.where(mask, jnp.exp(scores), 0.0)
    return exp_scores / jnp.sum(exp_scores, -1, keepdims=True)


def first_kernel(own, oth, cos, sin, mask, q_ref, k_ref, v_ref, ctx_ref):
    proj = own[...] + oth[...].astype(F32)
    key = rotated(proj[:, :HD], cos[...], sin[...]).astype(BF16)
    value = proj[:, HD : 2 * HD].astype(BF16)
    query = rotated(proj[:, 2 * HD :], cos[...], sin[...]).astype(BF16)
    probs = probabilities(query, key, mask[0] > 0.5)
    ctx_ref[...] = mm(probs.astype(BF16), value).astype(BF16)
    q_ref[...] = query
    k_ref[...] = key
    v_ref[...] = value


def rest_kernel(heads, own, oth, cos, sin, mask, k_ref, v_ref, q_ref, ctx_ref):
    key, value = k_ref[...], v_ref[...]
    allowed = mask[0] > 0.5
    for head in range(heads):
        cols = slice(head * HD, (head + 1) * HD)
        proj = own[:, cols] + oth[:, cols].astype(F32)
        query = rotated(proj, cos[...], sin[...]).astype(BF16)
        probs = probabilities(query, key, allowed)
        ctx_ref[:, cols] = mm(probs.astype(BF16), value).astype(BF16)
        q_ref[:, cols] = query


def back_kernel(
    heads, own, oth, cos, sin, mask, q0_ref, q_ref, k_ref, v_ref, out_ref
):
    key, value = k_ref[...], v_ref[...]
    allowed = mask[0] > 0.5
    d_key = jnp.zeros(key.shape, F32)
    d_value = jnp.zeros(key.shape, F32)
    for head in range(heads):
        cols = slice(head * HD, (head + 1) * HD)
        query = q0_ref[...] if head == 0 else q_ref[:, (head - 1) * HD : head * HD]
        d_out = (own[:, cols] + oth[:, cols].astype(F32)).astype(BF16)
        probs = probabilities(query, key, allowed)
        d_probs = mm(d_out, value, NT)
        d_value += mm(probs.astype(BF16), d_out, TN)
        delta = jnp.sum(probs * d_probs, -1, keepdims=True)
        d_scores = (probs * (d_probs - delta) * (1.0 / math.sqrt(HD))).astype(BF16)
        d_query = unrotated(mm(d_scores, key), cos[...], sin[...])
        out_ref[:, (head + 2) * HD : (head + 3) * HD] = d_query.astype(BF16)
        d_key += mm(d_scores, query, TN)
    out_ref[:, :HD] = unrotated(d_key, cos[...], sin[...]).astype(BF16)
    out_ref[:, HD : 2 * HD] = d_value.astype(BF16)


def per_sequence(kernel, arrays, *, tables, mask, outs, name, work):
    length = tables[0].shape[0]
    seqs = mask.shape[0]

    def by_rows(cols, at=0):
        return pl.BlockSpec((length, cols), lambda s: (s, at))

    arrays = [a if isinstance(a, tuple) else (a, a.shape[1], 0) for a in arrays]
    specs = [by_rows(cols, at) for _, cols, at in arrays]
    table = pl.BlockSpec((length, HD), lambda s: (0, 0))
    values = [a for a, _, _ in arrays]
    return pl.pallas_call(
        kernel,
        grid=(seqs,),
        in_specs=specs[:2]
        + [table, table, pl.BlockSpec((1, length, length), lambda s: (s, 0, 0))]
        + specs[2:],
        out_specs=[by_rows(cols) for cols in outs],
        out_shape=[jax.ShapeDtypeStruct((seqs * length, cols), BF16) for cols in outs],
        compiler_params=params(1),
        cost_estimate=cost(
            seqs * work * length * length * HD,
            4 * seqs * length * sum(outs),
            seqs * length * length,
        ),
        name=name,
    )(*values[:2], *tables, mask, *values[2:])


def step_kernel(par_ref, *refs):
    *pieces, dy_own, dy_oth, w_mine, w_theirs, u_ref, sent_ref = refs
    cols = u_ref.shape[2]
    tokens = pieces[0].shape[1]
    at = pl.ds(pl.multiple_of(pl.program_id(1) * cols, cols), cols)
    for place, weight in ((0, w_mine), (1, w_theirs)):
        grad = 0.0
        for group, dy in ((0, dy_own), (1, dy_oth)):
            term = 0.0
            for part in range(len(pieces) // 2):
                rows = pl.ds(part * tokens, tokens)
                term += mm(pieces[2 * part + place][group], dy[rows, at], TN)
            grad += term.astype(BF16).astype(F32)
        updated = weight[...] - learn_rate * grad
        u_ref[place] = updated
        sent_ref[place] = updated.astype(BF16)


def step_weights(par, pieces, d_own, d_oth, weight, first_col, unit, blocks=None):
    _, part_tokens, rows = pieces[0].shape
    tokens, cols = d_own.shape
    total = rows // BLOCK
    begin, end = blocks or (0, total)
    count = end - begin
    at = first_col // unit
    piece = pl.BlockSpec((2, part_tokens, BLOCK), lambda j, k, p: (0, 0, begin + j))
    whole = pl.BlockSpec((tokens, cols), lambda j, k, p: (0, 0))
    out = pl.BlockSpec((2, BLOCK, unit), lambda j, k, p: (0, j, k))
    mine = lambda j, k, p: (p[0] * total + begin + j, at + k)
    theirs = lambda j, k, p: ((1 - p[0]) * total + begin + j, at + k)
    return pl.pallas_call(
        step_kernel,
        grid_spec=pltpu.PrefetchScalarGridSpec(
            num_scalar_prefetch=1,
            grid=(count, cols // unit),
            in_specs=[piece] * len(pieces)
            + [whole, whole]
            + [pl.BlockSpec((BLOCK, unit), mine), pl.BlockSpec((BLOCK, unit), theirs)],
            out_specs=[out, out],
        ),
        out_shape=[
            jax.ShapeDtypeStruct((2, count * BLOCK, cols), F32),
            jax.ShapeDtypeStruct((2, count * BLOCK, cols), BF16),
        ],
        compiler_params=params(2),
        cost_estimate=cost(8 * tokens * count * BLOCK * cols, count * BLOCK * (8 * tokens + 20 * cols)),
        name="step_weights",
    )(par, *pieces, d_own, d_oth, weight, weight)


def mix_kernel(par_ref, coef, u_ref, low_ref, high_ref, *outs):
    updated = u_ref[0]
    out_ref = outs[-1]
    out_ref[...] = (
        updated
        + coef[0] * (low_ref[0].astype(F32) - updated)
        + coef[1] * (high_ref[0].astype(F32) - updated)
    )


def mix(par, coef, chunk, rows, cols, width, to_col, begin, buffer=None):
    count = chunk[0].shape[1]
    block = min(2 * BLOCK, count)
    total, first, to = rows // block, begin * BLOCK // block, to_col // cols
    source = pl.BlockSpec((1, block, cols), lambda i, j, p: (i, j, 0))
    place = pl.BlockSpec(
        (block, cols), lambda i, j, p: ((p[0] + i * (1 - 2 * p[0])) * total + first + j, to)
    )
    extra = [] if buffer is None else [buffer]
    return pl.pallas_call(
        mix_kernel,
        grid_spec=pltpu.PrefetchScalarGridSpec(
            num_scalar_prefetch=1,
            grid=(2, count // block),
            in_specs=[pl.BlockSpec(memory_space=pltpu.SMEM), source, source, source]
            + [pl.BlockSpec(memory_space=pl.ANY)] * len(extra),
            out_specs=place,
        ),
        out_shape=jax.ShapeDtypeStruct((2 * rows, width), F32),
        input_output_aliases={5: 0} if extra else {},
        compiler_params=params(2),
        cost_estimate=cost(10 * count * cols, 24 * count * cols),
        name="mix",
    )(par, coef, *chunk, *extra)


def body(fsdp_count, tensor_count, hidden, cotangent, documents, q_w, k_w, v_w, o_w, edge_weight):
    _, seqs, length, shard_cols = hidden.shape
    tokens = seqs * length
    model_width = shard_cols * tensor_count
    q_cols = q_w.shape[2]
    heads = q_cols // HD
    tensor_at, fsdp_at = lax.axis_index("tensor"), lax.axis_index("fsdp")
    share = tensor_count // fsdp_count
    home = tensor_at // share == fsdp_at
    par = (tensor_at % share).astype(jnp.int32).reshape(1)
    other = functools.partial(passed_along, axis="fsdp", by=1)
    flip = lambda block: swapped(block, tensor_count)
    far_flip = lambda block: lax.ppermute(
        block, "tensor", [(t, (t + share) % tensor_count) for t in range(tensor_count)]
    )

    shard = hidden[0].reshape(tokens, shard_cols)
    cotan = cotangent[0].reshape(tokens, shard_cols)
    h_near, h_far = spread(shard, fsdp_count, tensor_count)

    coef = jnp.concatenate([passed_along(edge_weight, "gossip", 1), edge_weight])

    wide = shard.astype(F32)
    squares = jnp.sum(wide * wide, -1)
    got = flip(squares)
    wq, wk, wv = after((q_w[0], k_w[0], v_w[0]), squares)
    squares = squares + got
    got_x = far_flip(squares)
    docs = documents[0].astype(F32)
    got_y = other(jnp.concatenate([squares, docs.reshape(tokens)]))
    got_xy = lax.ppermute(
        squares,
        ("fsdp", "tensor"),
        [
            (g * tensor_count + t, (1 - g) * tensor_count + (t + share) % tensor_count)
            for g in range(fsdp_count)
            for t in range(tensor_count)
        ],
    )
    w_proj = jnp.concatenate(after((wk, wv, wq), squares), 1).astype(BF16)
    w_out = after(o_w[0], squares).astype(BF16)
    tables = rope_tables(length, HD)
    positions = jnp.arange(length)
    causal = (positions[:, None] >= positions[None, :])[None]

    def mask_of(docs):
        docs = after(docs, squares)
        return (causal & (docs[:, :, None] == docs[:, None, :])).astype(F32)

    mask = mask_of(docs)
    got_x, coef, w_proj, w_out, mask, *tables = lax.optimization_barrier(
        (got_x, coef, w_proj, w_out, mask, *tables)
    )
    inv_own = lax.rsqrt((squares + got_x) / model_width + norm_eps)
    inv_oth = lax.rsqrt((got_y[:tokens] + got_xy) / model_width + norm_eps)

    def pieces_of(part, near, far, scale_own=None, scale_oth=None):
        own = jnp.where(home, part, near)
        oth = jnp.where(home, near, far)
        if scale_own is not None:
            own = (own.astype(F32) * scale_own[:, None]).astype(BF16)
            oth = (oth.astype(F32) * scale_oth[:, None]).astype(BF16)
        mine = lax.optimization_barrier(jnp.stack([own, oth]))
        return mine, flip(mine)

    c_near, c_far = spread(after(cotan, h_near, h_far), fsdp_count, tensor_count)
    h_pieces = pieces_of(shard, h_near, h_far, inv_own, inv_oth)
    first_cols, rest_cols = 3 * HD, q_cols - HD
    first_own, first_oth, first_sent = project(par, h_pieces, w_proj, 0, first_cols)
    first_sent = jnp.concatenate([first_sent, first_own.astype(BF16)], 1)
    first_got = other(first_sent)
    rest_own, rest_oth, rest_sent = project(par, after(h_pieces, first_sent), w_proj, 1, rest_cols)
    rest_sent = jnp.concatenate([rest_sent, rest_own.astype(BF16)], 1)
    mask_oth = mask_of(after(got_y[tokens:], rest_sent).reshape(docs.shape))
    c_near, c_far = after((c_near, c_far), rest_sent, mask_oth)
    c_pieces = pieces_of(cotan, c_near, c_far)
    first_got = after(first_got, c_pieces[0])
    first = functools.partial(
        per_sequence, first_kernel, tables=tables, outs=(HD,) * 4, name="first_head", work=4
    )
    q0, key, value, ctx0 = first((first_own, (first_got, first_cols, 0)), mask=mask)
    q0_oth, key_oth, value_oth, ctx0_oth = first(
        (first_oth, (first_got, first_cols, 1)), mask=mask_oth
    )
    rest_got = other(after(rest_sent, first_got))

    def shared(pair, *gates):
        updated, sent = pair
        sent = after(sent, *gates) if gates else sent
        return updated, passed_along(sent, "gossip", 1), passed_along(sent, "gossip", -1)

    o_step = functools.partial(step_weights, par, c_pieces)
    blocks = shard_cols // BLOCK
    z1 = shared(o_step(ctx0, ctx0_oth, o_w[0], 0, HD, (0, blocks // 2)))
    z2 = shared(o_step(after(ctx0, z1[0]), ctx0_oth, o_w[0], 0, HD, (blocks // 2, blocks)))
    d_own, d_oth, d_sent = project(par, after(c_pieces, z2[0]), w_out, 0, q_cols)
    d_sent = jnp.concatenate([d_sent, d_own.astype(BF16)], 1)
    rest_got = after(rest_got, d_sent, *z1[1:])
    d_got = other(after(d_sent, rest_got))
    rest = functools.partial(
        per_sequence,
        functools.partial(rest_kernel, heads - 1),
        tables=tables,
        outs=(rest_cols,) * 2,
        name="rest_heads",
        work=4 * (heads - 1),
    )
    q_rest, ctx_rest = rest((rest_own, (rest_got, rest_cols, 0), key, value), mask=mask)
    q_rest_oth, ctx_rest_oth = rest(
        (rest_oth, (rest_got, rest_cols, 1), key_oth, value_oth), mask=mask_oth
    )
    chunks = [z1, z2]
    for i in range(heads - 1):
        at = slice(i * HD, (i + 1) * HD)
        d_ctx = after(ctx_rest[:, at], chunks[-1][0])
        chunks.append(shared(o_step(d_ctx, ctx_rest_oth[:, at], o_w[0], (i + 1) * HD, HD)))
    d_got = after(d_got, chunks[-1][0])
    back = functools.partial(
        per_sequence,
        functools.partial(back_kernel, heads),
        tables=tables,
        outs=(q_cols + 2 * HD,),
        name="attention_back",
        work=14 * heads,
    )
    d_proj = back((d_own, (d_got, q_cols, 0), q0, q_rest, key, value), mask=mask)[0]
    d_proj_oth = back(
        (d_oth, (d_got, q_cols, 1), q0_oth, q_rest_oth, key_oth, value_oth), mask=mask_oth
    )[0]
    h_step = functools.partial(step_weights, par, h_pieces)
    half = q_cols // 2
    for weight, first_col, begin, cols in (
        (k_w[0], 0, 0, HD),
        (v_w[0], 0, HD, HD),
        (q_w[0], 0, 2 * HD, half),
        (q_w[0], half, 2 * HD + half, half),
    ):
        at = slice(begin, begin + cols)
        d_own = after(d_proj[:, at], chunks[-1][0])
        chunks.append(shared(h_step(d_own, d_proj_oth[:, at], weight, first_col, cols)))

    outs = {}
    last = coef
    for chunk, (name, cols, width, first_col) in zip(
        chunks,
        [("o", HD, q_cols, max(i, 0) * HD) for i in range(-1, heads)]
        + [("k", HD, HD, 0), ("v", HD, HD, 0), ("q", half, q_cols, 0), ("q", half, q_cols, half)],
    ):
        chunk = (chunk[0], *after(chunk[1:], last))
        begin = blocks // 2 if chunk[0].shape[1] < shard_cols and name in outs else 0
        last = outs[name] = mix(
            par, coef, chunk, shard_cols, cols, width, first_col, begin, outs.get(name)
        )
    return tuple(outs[name][None] for name in "qkvo")


def solution(mesh):
    fsdp_count, tensor_count = mesh.shape["fsdp"], mesh.shape["tensor"]
    assert fsdp_count == 2 and tensor_count == 2 * fsdp_count
    activations = P("gossip", "fsdp", None, "tensor")
    weights = P("gossip", "fsdp", "tensor")
    return jax.shard_map(
        functools.partial(body, fsdp_count, tensor_count),
        mesh=mesh,
        in_specs=(activations, activations, P("gossip", "fsdp", None))
        + (weights,) * 4
        + (P("gossip"),),
        out_specs=(weights,) * 4,
        check_vma=False,
    )
```

time: 879 us -> 329 us (0.37)
  waiting for transfers between devices: 719 us -> 157 us
  Pallas kernels: 0 us -> 75.6 us
  starting transfers between devices: 11.4 us -> 63.6 us
  other arithmetic: 65.3 us -> 15.6 us
  matrix products: 29.3 us -> 0 us
  local copies, waits for them, and re-layouts: 38.7 us -> 14.9 us
  between operations: 14.7 us -> 2.01 us
    ppermute x9 -> x23, waiting for transfers between devices: 432 us -> 147 us  [passed_along(): lax.ppermute(shard, axis, [(i, (i + by) % count) for i in range(count)])]
    all_gather x3 -> x0, waiting for transfers between devices: 178 us -> none  [the longest x1 124 us: body(): block_rows = lax.all_gather(packed, 'fsdp', axis=0, tiled=True)]
    reduce_scatter x1 -> x0, waiting for transfers between devices: 108 us -> none  [body(): lax.psum_scatter(jnp.concatenate([first_part, second_part], 1).astype(jnp...]
    pallas_call x0 -> x27, Pallas kernels: none -> 75.6 us  [the longest x9 32 us: step_weights(): pl.pallas_call(step_kernel, grid_spec=pltpu.PrefetchScalarGridSpec(num_sc...]
    ppermute x9 -> x23, starting transfers between devices: 11.2 us -> 49.6 us  [passed_along(): lax.ppermute(shard, axis, [(i, (i + by) % count) for i in range(count)])]
    dot_general x10 -> x0, matrix products: 29.3 us -> none  [the longest x1 7.33 us: body(): jnp.dot(left, block_rows[:, :proj_cols], preferred_element_type=jnp.float32)]
    add x4 -> x1, other arithmetic: 23 us -> 0.01 us  [body(): squares = squares + got]
    unnamed x34 -> x92, local copies, waits for them, and re-layouts: 33.9 us -> 14.7 us
  transfers between devices with their start and end apart: 13 -> 32, of which waited for: 7 -> 13; matrix products, arithmetic and copies ran while one was open for 8% -> 4% of each run, Pallas kernels for 0% -> 22%
where the time goes in v1:
time: 329 us
  waiting for transfers between devices  157 us (48%)
  Pallas kernels  75.6 us (23%)
  starting transfers between devices  63.6 us (19%)
  other arithmetic  15.6 us (5%)
  local copies, waits for them, and re-layouts  14.9 us (5%)
    ppermute x23, waiting for transfers between devices, passed_along(): lax.ppermute(shard, axis, [(i, (i + by) % count) for i in range(count)])  147 us
    ppermute x23, starting transfers between devices, passed_along(): lax.ppermute(shard, axis, [(i, (i + by) % count) for i in range(count)])  49.6 us
    pallas_call x9, Pallas kernels, step_weights(): pl.pallas_call(step_kernel, grid_spec=pltpu.PrefetchScalarGridSpec(num_sc...  32 us
    pallas_call x9, Pallas kernels, mix(): pl.pallas_call(mix_kernel, grid_spec=pltpu.PrefetchScalarGridSpec(num_sca...  19.3 us
    unnamed x92, local copies, waits for them, and re-layouts  14.7 us
    pallas_call x6, Pallas kernels, per_sequence(): pl.pallas_call(kernel, grid=(seqs,), in_specs=specs[:2] + [table, table,...  13.7 us
    pallas_call x3, Pallas kernels, project(): pl.pallas_call(project_kernel, grid_spec=pltpu.PrefetchScalarGridSpec(num...  10.6 us
    ppermute x4, starting transfers between devices, spread(): return (lax.ppermute(shard, axes, near), lax.ppermute(shard, axes, far))  8.08 us
  transfers between devices with their start and end apart: 32, of which 13 were waited for; matrix products, arithmetic and copies ran while one was open for 4% of the time, Pallas kernels for 22%

profile of v1, /device:TPU:0, one launch (start us, length us, event | category | flops | bytes accessed | tf_op | source)
XLA Modules:
  0.0 328.6 jit_solution(4737834283684452354)
XLA Ops:
  0.6 3.0 collective-permute-start.3
  12.1 3.0 collective-permute-start.1
  15.2 2.7 collective-permute-start.6
  17.8 2.5 convert.11
  21.7 1.9 pad_maximum_fusion.refs_2_
  26.7 3.5 %collective-permute-done.1 = f32[512]{0:T(512)S(1)} collective-permute-done((f32[512]{0:T(512)S(1)}, f32[512]{0:T(512)S(1)}, u32[]{:S(2)}, u32[]{:S(2)}) %collective-permute-start.1) | collective-permute-done | bytes 2080 | tf_op jit(solution)/shard_map/ppermute | solution.py:319
  31.1 2.7 collective-permute-start.8
  35.5 1.9 copy-done.3
  37.4 3.8 %project.3 = (f32[512,384]{1,0:T(8,128)S(1)}, f32[512,384]{1,0:T(8,128)S(1)}, bf16[512,384]{1,0:T(8,128)(2,1)S(1)}) custom-call(s32[1]{0:T(128)} %bitcast.par_ref, bf16[2,512,1024]{2,1,0:T(8,128)(2,1)S(1)} %pad_maximum_fusion.1.refs_0_, bf16[2,512,1024]{2,1,0:T(8,128)(2,1)} %collective-permute-done.7.refs_1_, bf16[2048,768]{1,0:T(8,128)(2,1)S(1)} %copy-done.3), custom_call_target="tpu_custom_call" | custom-call | flops 1610612736 | bytes 6160384 | tf_op jit(solution)/shard_map/project/pallas_call | solution.py:116
  44.0 3.8 %project.4 = (f32[512,384]{1,0:T(8,128)S(1)}, f32[512,384]{1,0:T(8,128)S(1)}, bf16[512,384]{1,0:T(8,128)(2,1)S(1)}) custom-call(s32[1]{0:T(128)} %bitcast.par_ref, bf16[2,512,1024]{2,1,0:T(8,128)(2,1)S(1)} %pad_maximum_fusion.1.refs_0_, bf16[2,512,1024]{2,1,0:T(8,128)(2,1)} %collective-permute-done.7.refs_1_, bf16[2048,768]{1,0:T(8,128)(2,1)S(1)} %copy-done.3), custom_call_target="tpu_custom_call" | custom-call | flops 1610612736 | bytes 6160384 | tf_op jit(solution)/shard_map/project/pallas_call | solution.py:116
  50.7 6.5 %collective-permute-done.8 = bf16[512,1024]{1,0:T(8,128)(2,1)} collective-permute-done((bf16[512,1024]{1,0:T(8,128)(2,1)}, bf16[512,1024]{1,0:T(8,128)(2,1)}, u32[]{:S(2)}, u32[]{:S(2)}) %collective-permute-start.8) | collective-permute-done | bytes 1048608 | tf_op jit(solution)/shard_map/ppermute | solution.py:73
  60.0 4.7 %collective-permute-start.11 = (bf16[512,768]{1,0:T(8,128)(2,1)S(1)}, bf16[512,768]{1,0:T(8,128)(2,1)S(1)}, u32[]{:S(2)}, u32[]{:S(2)}) collective-permute-start(bf16[512,768]{1,0:T(8,128)(2,1)S(1)} %copy-done.44), channel_id=1, source_target_pairs={{0,4},{4,0},{1,5},{5,1},{2,6},{6,2},{3,7},{7,3},{8,12},{12,8},{9,1... | collective-permute-start | bytes 2359304 | tf_op jit(solution)/shard_map/ppermute | solution.py:43
  64.7 17.4 %collective-permute-done.11.oth = bf16[512,768]{1,0:T(8,128)(2,1)S(1)} collective-permute-done((bf16[512,768]{1,0:T(8,128)(2,1)S(1)}, bf16[512,768]{1,0:T(8,128)(2,1)S(1)}, u32[]{:S(2)}, u32[]{:S(2)}) %collective-permute-start.11) | collective-permute-done | bytes 786464 | tf_op jit(solution)/shard_map/ppermute | solution.py:43
  88.4 1.8 collective-permute-start.13
  90.2 2.1 collective-permute-start.14
  92.3 2.1 step_weights.10
  94.4 2.9 project.5
  97.5 3.2 collective-permute-done.12.oth
  104.8 2.7 collective-permute-start.31
  107.5 1.8 rest_heads.2
  109.3 1.8 rest_heads.3
  111.2 3.6 %step_weights.11 = (f32[2,1024,128]{2,1,0:T(8,128)S(1)}, bf16[2,1024,128]{2,1,0:T(8,128)(2,1)}) custom-call(s32[1]{0:T(128)} %bitcast.par_ref, bf16[2,512,1024]{2,1,0:T(8,128)(2,1)S(1)} %pad_maximum_fusion.2.refs_0_, bf16[2,512,1024]{2,1,0:T(8,128)(2,1)S(1)} %collective-permute-done.10.refs_1_, bf16[512,128]{1,0:T(8,128)(2,1)S(1)} %get-tuple-element.142.refs_2_, ...), custom_call_target="tpu_custom_call" | custom-call | flops 536870912 | bytes 6815744 | tf_op jit(solution)/shard_map/step_weights/pallas_call | solution.py:251
  115.8 3.8 %collective-permute-start.29 = (bf16[2,1024,128]{2,1,0:T(8,128)(2,1)}, bf16[2,1024,128]{2,1,0:T(8,128)(2,1)S(1)}, u32[]{:S(2)}, u32[]{:S(2)}) collective-permute-start(bf16[2,1024,128]{2,1,0:T(8,128)(2,1)} %get-tuple-element.172), channel_id=1, source_target_pairs={{0,24},{8,0},{16,8},{24,16},{1,25},{9,1},{17,9},{25,17},{2,26},{10... | collective-permute-start | bytes 1572872 | tf_op jit(solution)/shard_map/ppermute | solution.py:43
  119.6 3.5 %step_weights.12 = (f32[2,1024,128]{2,1,0:T(8,128)S(1)}, bf16[2,1024,128]{2,1,0:T(8,128)(2,1)}) custom-call(s32[1]{0:T(128)} %bitcast.par_ref, bf16[2,512,1024]{2,1,0:T(8,128)(2,1)S(1)} %pad_maximum_fusion.2.refs_0_, bf16[2,512,1024]{2,1,0:T(8,128)(2,1)S(1)} %collective-permute-done.10.refs_1_, bf16[512,128]{1,0:T(8,128)(2,1)S(1)} %get-tuple-element.148.refs_2_, ...), custom_call_target="tpu_custom_call" | custom-call | flops 536870912 | bytes 6815744 | tf_op jit(solution)/shard_map/step_weights/pallas_call | solution.py:251
  124.1 3.5 %step_weights.13 = (f32[2,1024,128]{2,1,0:T(8,128)S(1)}, bf16[2,1024,128]{2,1,0:T(8,128)(2,1)}) custom-call(s32[1]{0:T(128)} %bitcast.par_ref, bf16[2,512,1024]{2,1,0:T(8,128)(2,1)S(1)} %pad_maximum_fusion.2.refs_0_, bf16[2,512,1024]{2,1,0:T(8,128)(2,1)S(1)} %collective-permute-done.10.refs_1_, bf16[512,128]{1,0:T(8,128)(2,1)S(1)} %get-tuple-element.150.refs_2_, ...), custom_call_target="tpu_custom_call" | custom-call | flops 536870912 | bytes 6815744 | tf_op jit(solution)/shard_map/step_weights/pallas_call | solution.py:251
  129.2 4.0 %attention_back.2 = bf16[512,768]{1,0:T(8,128)(2,1)S(1)} custom-call(f32[512,512]{1,0:T(8,128)S(1)} %get-tuple-element.133.own, bf16[512,1024]{1,0:T(8,128)(2,1)S(1)} %collective-permute-done.15.oth, f32[256,128]{1,0:T(8,128)S(1)} %get-tuple-element.121.cos, f32[256,128]{1,0:T(8,128)S(1)} %get-tuple-element.122.sin, f32[2,256,256]{2,1,0:T(8,128)S(1)} %copy-done.7, ...), custom_call_target="tpu_custom_call" | custom-call | flops 939524096 | bytes 1572864 | tf_op jit(solution)/shard_map/attention_back/pallas_call | solution.py:203
  133.3 4.0 %attention_back.3 = bf16[512,768]{1,0:T(8,128)(2,1)S(1)} custom-call(f32[512,512]{1,0:T(8,128)S(1)} %get-tuple-element.156.own, bf16[512,1024]{1,0:T(8,128)(2,1)S(1)} %collective-permute-done.15.oth, f32[256,128]{1,0:T(8,128)S(1)} %get-tuple-element.121.cos, f32[256,128]{1,0:T(8,128)S(1)} %get-tuple-element.122.sin, ...), custom_call_target="tpu_custom_call" | custom-call | flops 939524096 | bytes 1572864 | tf_op jit(solution)/shard_map/attention_back/pallas_call | solution.py:203
  137.3 4.7 %step_weights.14 = (f32[2,1024,128]{2,1,0:T(8,128)S(1)}, bf16[2,1024,128]{2,1,0:T(8,128)(2,1)}) custom-call(s32[1]{0:T(128)} %bitcast.par_ref, bf16[2,512,1024]{2,1,0:T(8,128)(2,1)S(1)} %pad_maximum_fusion.1.refs_0_, bf16[2,512,1024]{2,1,0:T(8,128)(2,1)} %collective-permute-done.7.refs_1_, bf16[512,128]{1,0:T(8,128)(2,1)S(1)} %get-tuple-element.155.refs_2_, ...), custom_call_target="tpu_custom_call" | custom-call | flops 536870912 | bytes 6815744 | tf_op jit(solution)/shard_map/step_weights/pallas_call | solution.py:251
  142.7 2.2 collective-permute-start.27
  145.6 3.8 %collective-permute-start.25 = (bf16[2,1024,128]{2,1,0:T(8,128)(2,1)}, bf16[2,1024,128]{2,1,0:T(8,128)(2,1)S(1)}, u32[]{:S(2)}, u32[]{:S(2)}) collective-permute-start(bf16[2,1024,128]{2,1,0:T(8,128)(2,1)} %get-tuple-element.170), channel_id=1, source_target_pairs={{0,24},{8,0},{16,8},{24,16},{1,25},{9,1},{17,9},{25,17},{2,26},{10... | collective-permute-start | bytes 1572872 | tf_op jit(solution)/shard_map/ppermute | solution.py:43
  150.3 4.9 %collective-permute-done.26.low_ref = bf16[2,1024,128]{2,1,0:T(8,128)(2,1)S(1)} collective-permute-done((bf16[2,1024,128]{2,1,0:T(8,128)(2,1)}, bf16[2,1024,128]{2,1,0:T(8,128)(2,1)S(1)}, u32[]{:S(2)}, u32[]{:S(2)}) %collective-permute-start.26) | collective-permute-done | bytes 524320 | tf_op jit(solution)/shard_map/ppermute | solution.py:43
  155.2 10.6 %collective-permute-start.23 = (bf16[2,1024,128]{2,1,0:T(8,128)(2,1)}, bf16[2,1024,128]{2,1,0:T(8,128)(2,1)S(1)}, u32[]{:S(2)}, u32[]{:S(2)}) collective-permute-start(bf16[2,1024,128]{2,1,0:T(8,128)(2,1)} %get-tuple-element.169), channel_id=1, source_target_pairs={{0,24},{8,0},{16,8},{24,16},{1,25},{9,1},{17,9},{25,17},{2,26},{10... | collective-permute-start | bytes 1572872 | tf_op jit(solution)/shard_map/ppermute | solution.py:43
  165.8 4.8 %step_weights.15 = (f32[2,1024,128]{2,1,0:T(8,128)S(1)}, bf16[2,1024,128]{2,1,0:T(8,128)(2,1)}) custom-call(s32[1]{0:T(128)} %bitcast.par_ref, bf16[2,512,1024]{2,1,0:T(8,128)(2,1)S(1)} %pad_maximum_fusion.1.refs_0_, bf16[2,512,1024]{2,1,0:T(8,128)(2,1)} %collective-permute-done.7.refs_1_, bf16[512,128]{1,0:T(8,128)(2,1)S(1)} %get-tuple-element.160.refs_2_, ...), custom_call_target="tpu_custom_call" | custom-call | flops 536870912 | bytes 6815744 | tf_op jit(solution)/shard_map/step_weights/pallas_call | solution.py:251
  170.7 4.1 %step_weights.16 = (f32[2,1024,256]{2,1,0:T(8,128)S(1)}, bf16[2,1024,256]{2,1,0:T(8,128)(2,1)S(1)}) custom-call(s32[1]{0:T(128)} %bitcast.par_ref, bf16[2,512,1024]{2,1,0:T(8,128)(2,1)S(1)} %pad_maximum_fusion.1.refs_0_, bf16[2,512,1024]{2,1,0:T(8,128)(2,1)} %collective-permute-done.7.refs_1_, bf16[512,256]{1,0:T(8,128)(2,1)S(1)} %get-tuple-element.162.refs_2_, ...), custom_call_target="tpu_custom_call" | custom-call | flops 1073741824 | bytes 9437184 | tf_op jit(solution)/shard_map/step_weights/pallas_call | solution.py:251
  174.9 2.8 collective-permute-done.24.low_ref
  177.7 10.5 %collective-permute-start.19 = (bf16[2,1024,256]{2,1,0:T(8,128)(2,1)S(1)}, bf16[2,1024,256]{2,1,0:T(8,128)(2,1)S(1)}, u32[]{:S(2)}, u32[]{:S(2)}) collective-permute-start(bf16[2,1024,256]{2,1,0:T(8,128)(2,1)S(1)} %get-tuple-element.167), channel_id=1, source_target_pairs={{0,24},{8,0},{16,8},{24,16},{1,25},{9,1},{17,9},{25,17},{2,26},{10... | collective-permute-start | bytes 3145736 | tf_op jit(solution)/shard_map/ppermute | solution.py:43
  189.5 4.2 %step_weights.17 = (f32[2,1024,256]{2,1,0:T(8,128)S(1)}, bf16[2,1024,256]{2,1,0:T(8,128)(2,1)S(1)}) custom-call(s32[1]{0:T(128)} %bitcast.par_ref, bf16[2,512,1024]{2,1,0:T(8,128)(2,1)S(1)} %pad_maximum_fusion.1.refs_0_, bf16[2,512,1024]{2,1,0:T(8,128)(2,1)} %collective-permute-done.7.refs_1_, bf16[512,256]{1,0:T(8,128)(2,1)S(1)} %get-tuple-element.164.refs_2_, ...), custom_call_target="tpu_custom_call" | custom-call | flops 1073741824 | bytes 9437184 | tf_op jit(solution)/shard_map/step_weights/pallas_call | solution.py:251
  194.6 5.5 %collective-permute-done.22.low_ref = bf16[2,1024,128]{2,1,0:T(8,128)(2,1)S(1)} collective-permute-done((bf16[2,1024,128]{2,1,0:T(8,128)(2,1)}, bf16[2,1024,128]{2,1,0:T(8,128)(2,1)S(1)}, u32[]{:S(2)}, u32[]{:S(2)}) %collective-permute-start.22) | collective-permute-done | bytes 524320 | tf_op jit(solution)/shard_map/ppermute | solution.py:43
  200.2 11.2 %collective-permute-done.23.high_ref = bf16[2,1024,128]{2,1,0:T(8,128)(2,1)S(1)} collective-permute-done((bf16[2,1024,128]{2,1,0:T(8,128)(2,1)}, bf16[2,1024,128]{2,1,0:T(8,128)(2,1)S(1)}, u32[]{:S(2)}, u32[]{:S(2)}) %collective-permute-start.23) | collective-permute-done | bytes 524320 | tf_op jit(solution)/shard_map/ppermute | solution.py:43
  211.5 56.3 %collective-permute-done.20.low_ref = bf16[2,1024,128]{2,1,0:T(8,128)(2,1)S(1)} collective-permute-done((bf16[2,1024,128]{2,1,0:T(8,128)(2,1)}, bf16[2,1024,128]{2,1,0:T(8,128)(2,1)S(1)}, u32[]{:S(2)}, u32[]{:S(2)}) %collective-permute-start.20) | collective-permute-done | bytes 524320 | tf_op jit(solution)/shard_map/ppermute | solution.py:43
  270.8 2.3 mix.11.outs_0_
  273.1 2.3 mix.12.outs_0_
  275.3 2.2 mix.13
  277.5 2.2 mix.14
  279.7 41.4 %collective-permute-done.21.high_ref = bf16[2,1024,128]{2,1,0:T(8,128)(2,1)S(1)} collective-permute-done((bf16[2,1024,128]{2,1,0:T(8,128)(2,1)}, bf16[2,1024,128]{2,1,0:T(8,128)(2,1)S(1)}, u32[]{:S(2)}, u32[]{:S(2)}) %collective-permute-start.21) | collective-permute-done | bytes 524320 | tf_op jit(solution)/shard_map/ppermute | solution.py:43
  321.2 2.2 mix.15
  323.4 2.6 mix.16.outs_0_
  326.0 2.6 mix.17
  (170 shorter events, 45.1 us)
Async XLA Ops:
  0.6 29.6 %collective-permute-start.3 = (bf16[512,1024]{1,0:T(8,128)(2,1)}, bf16[512,1024]{1,0:T(8,128)(2,1)S(1)}, u32[]{:S(2)}, u32[]{:S(2)}) collective-permute-start(bf16[512,1024]{1,0:T(8,128)(2,1)} %bitcast.52), channel_id=1, source_target_pairs={{0,2},{1,3},{2,6},{3,7},{4,0},{5,1},{6,4},{7,5},{8,10},{9,11},{10,... | collective-permute-start | bytes 3145736 | tf_op jit(solution)/shard_map/ppermute | solution.py:73
  3.6 26.6 %collective-permute-start.4 = (bf16[512,1024]{1,0:T(8,128)(2,1)}, bf16[512,1024]{1,0:T(8,128)(2,1)S(1)}, u32[]{:S(2)}, u32[]{:S(2)}) collective-permute-start(bf16[512,1024]{1,0:T(8,128)(2,1)} %bitcast.53), channel_id=1, source_target_pairs={{2,4},{3,5},{4,2},{5,3},{10,12},{11,13},{12,10},{13,11},{18,20},{1... | collective-permute-start | bytes 3145736 | tf_op jit(solution)/shard_map/ppermute | solution.py:73
  5.9 6.3 %collective-permute-start = (f32[512]{0:T(512)S(1)}, f32[512]{0:T(512)S(1)}, u32[]{:S(2)}, u32[]{:S(2)}) collective-permute-start(f32[512]{0:T(512)S(1)} %bitcast.57), channel_id=1, source_target_pairs={{0,1},{1,0},{2,3},{3,2},{4,5},{5,4},{6,7},{7,6},{8,9},{9,8},{10,11... | collective-permute-start | bytes 6152 | tf_op jit(solution)/shard_map/ppermute | solution.py:77
  5.9 5.5 %collective-permute-start.2 = (f32[1]{0:T(128)}, f32[1]{0:T(128)}, u32[]{:S(2)}, u32[]{:S(2)}) collective-permute-start(f32[1]{0:T(128)} %param.15), channel_id=1, source_target_pairs={{0,8},{8,16},{16,24},{24,0},{1,9},{9,17},{17,25},{25,1},{2,10},{10... | collective-permute-start | bytes 20 | tf_op jit(solution)/shard_map/ppermute | solution.py:43
  12.1 18.1 %collective-permute-start.1 = (f32[512]{0:T(512)S(1)}, f32[512]{0:T(512)S(1)}, u32[]{:S(2)}, u32[]{:S(2)}) collective-permute-start(f32[512]{0:T(512)S(1)} %add.21), channel_id=1, source_target_pairs={{0,2},{1,3},{2,0},{3,1},{4,6},{5,7},{6,4},{7,5},{8,10},{9,11},{10,... | collective-permute-start | bytes 6152 | tf_op jit(solution)/shard_map/ppermute | solution.py:319
  15.2 15.1 %collective-permute-start.6 = (f32[512]{0:T(512)S(1)}, f32[512]{0:T(512)S(1)}, u32[]{:S(2)}, u32[]{:S(2)}) collective-permute-start(f32[512]{0:T(512)S(1)} %add.21), channel_id=1, source_target_pairs={{0,6},{1,7},{2,4},{3,5},{4,2},{5,3},{6,0},{7,1},{8,14},{9,15},{10,... | collective-permute-start | bytes 6152 | tf_op jit(solution)/shard_map/ppermute | solution.py:337
  21.6 8.6 %collective-permute-start.5 = (f32[1024]{0:T(1024)S(1)}, f32[1024]{0:T(1024)S(1)}, u32[]{:S(2)}, u32[]{:S(2)}) collective-permute-start(f32[1024]{0:T(1024)S(1)} %pad_maximum_fusion.8), channel_id=1, source_target_pairs={{0,4},{4,0},{1,5},{5,1},{2,6},{6,2},{3,7},{7,3},{8,12},{12,8},{9,1... | collective-permute-start | bytes 12296 | tf_op jit(solution)/shard_map/ppermute | solution.py:43
  31.1 4.5 %collective-permute-start.7 = (bf16[2,512,1024]{2,1,0:T(8,128)(2,1)S(1)}, bf16[2,512,1024]{2,1,0:T(8,128)(2,1)}, u32[]{:S(2)}, u32[]{:S(2)}) collective-permute-start(bf16[2,512,1024]{2,1,0:T(8,128)(2,1)S(1)} %pad_maximum_fusion.1.refs_0_), channel_id=1, source_target_pairs={{0,1},{1,0},{2,3},{3,2},{4,5},{5,4},{6,7},{7,6},{8,9},{9,8},{10,11... | collective-permute-start | bytes 6291464 | tf_op jit(solution)/shard_map/ppermute | solution.py:77
  31.1 26.0 %collective-permute-start.8 = (bf16[512,1024]{1,0:T(8,128)(2,1)}, bf16[512,1024]{1,0:T(8,128)(2,1)}, u32[]{:S(2)}, u32[]{:S(2)}) collective-permute-start(bf16[512,1024]{1,0:T(8,128)(2,1)} %bitcast.9), channel_id=1, source_target_pairs={{0,2},{1,3},{2,6},{3,7},{4,0},{5,1},{6,4},{7,5},{8,10},{9,11},{10,... | collective-permute-start | bytes 3145736 | tf_op jit(solution)/shard_map/ppermute | solution.py:73
  33.8 23.3 %collective-permute-start.9 = (bf16[512,1024]{1,0:T(8,128)(2,1)}, bf16[512,1024]{1,0:T(8,128)(2,1)}, u32[]{:S(2)}, u32[]{:S(2)}) collective-permute-start(bf16[512,1024]{1,0:T(8,128)(2,1)} %bitcast.9), channel_id=1, source_target_pairs={{2,4},{3,5},{4,2},{5,3},{10,12},{11,13},{12,10},{13,11},{18,20},{1... | collective-permute-start | bytes 3145736 | tf_op jit(solution)/shard_map/ppermute | solution.py:73
  58.9 23.2 %copy-start.43 = (bf16[512,768]{1,0:T(8,128)(2,1)S(1)}, bf16[512,768]{1,0:T(8,128)(2,1)}, u32[]{:S(2)}) copy-start(bf16[512,768]{1,0:T(8,128)(2,1)} %pad_maximum_fusion.5) | copy-start | bytes 2359300
  58.9 24.9 %copy-start.22 = (f32[512,384]{1,0:T(8,128)S(1)}, f32[512,384]{1,0:T(8,128)}, u32[]{:S(2)}) copy-start(f32[512,384]{1,0:T(8,128)} %copy-done.21) | copy-start | bytes 2359300
  58.9 26.0 %copy-start.11 = (f32[512,384]{1,0:T(8,128)S(1)}, f32[512,384]{1,0:T(8,128)}, u32[]{:S(2)}) copy-start(f32[512,384]{1,0:T(8,128)} %copy-done.10) | copy-start | bytes 2359300
  59.1 25.8 %copy-start.7 = (f32[2,256,256]{2,1,0:T(8,128)S(1)}, f32[2,256,256]{2,1,0:T(8,128)}, u32[]{:S(2)}) copy-start(f32[2,256,256]{2,1,0:T(8,128)} %and_convert_fusion.1.mask) | copy-start | bytes 1572868
  59.2 27.0 %collective-permute-start.10 = (bf16[2,512,1024]{2,1,0:T(8,128)(2,1)S(1)}, bf16[2,512,1024]{2,1,0:T(8,128)(2,1)S(1)}, u32[]{:S(2)}, u32[]{:S(2)}) collective-permute-start(bf16[2,512,1024]{2,1,0:T(8,128)(2,1)S(1)} %pad_maximum_fusion.2.refs_0_), channel_id=1, source_target_pairs={{0,1},{1,0},{2,3},{3,2},{4,5},{5,4},{6,7},{7,6},{8,9},{9,8},{10,11... | collective-permute-start | bytes 6291464 | tf_op jit(solution)/shard_map/ppermute | solution.py:77
  60.0 22.1 %collective-permute-start.11 = (bf16[512,768]{1,0:T(8,128)(2,1)S(1)}, bf16[512,768]{1,0:T(8,128)(2,1)S(1)}, u32[]{:S(2)}, u32[]{:S(2)}) collective-permute-start(bf16[512,768]{1,0:T(8,128)(2,1)S(1)} %copy-done.44), channel_id=1, source_target_pairs={{0,4},{4,0},{1,5},{5,1},{2,6},{6,2},{3,7},{7,3},{8,12},{12,8},{9,1... | collective-permute-start | bytes 2359304 | tf_op jit(solution)/shard_map/ppermute | solution.py:43
  82.1 18.6 %collective-permute-start.12 = (bf16[512,768]{1,0:T(8,128)(2,1)S(1)}, bf16[512,768]{1,0:T(8,128)(2,1)S(1)}, u32[]{:S(2)}, u32[]{:S(2)}) collective-permute-start(bf16[512,768]{1,0:T(8,128)(2,1)S(1)} %copy-done.43), channel_id=1, source_target_pairs={{0,4},{4,0},{1,5},{5,1},{2,6},{6,2},{3,7},{7,3},{8,12},{12,8},{9,1... | collective-permute-start | bytes 2359304 | tf_op jit(solution)/shard_map/ppermute | solution.py:43
  88.4 12.3 %collective-permute-start.13 = (bf16[2,512,128]{2,1,0:T(8,128)(2,1)S(1)}, bf16[2,512,128]{2,1,0:T(8,128)(2,1)S(1)}, u32[]{:S(2)}, u32[]{:S(2)}) collective-permute-start(bf16[2,512,128]{2,1,0:T(8,128)(2,1)S(1)} %get-tuple-element.136), channel_id=1, source_target_pairs={{0,8},{8,16},{16,24},{24,0},{1,9},{9,17},{17,25},{25,1},{2,10},{10... | collective-permute-start | bytes 786440 | tf_op jit(solution)/shard_map/ppermute | solution.py:43
  90.2 12.1 %collective-permute-start.14 = (bf16[2,512,128]{2,1,0:T(8,128)(2,1)S(1)}, bf16[2,512,128]{2,1,0:T(8,128)(2,1)S(1)}, u32[]{:S(2)}, u32[]{:S(2)}) collective-permute-start(bf16[2,512,128]{2,1,0:T(8,128)(2,1)S(1)} %get-tuple-element.136), channel_id=1, source_target_pairs={{0,24},{8,0},{16,8},{24,16},{1,25},{9,1},{17,9},{25,17},{2,26},{10... | collective-permute-start | bytes 786440 | tf_op jit(solution)/shard_map/ppermute | solution.py:43
  97.3 10.2 %copy-start.9 = (f32[512,384]{1,0:T(8,128)S(1)}, f32[512,384]{1,0:T(8,128)}, u32[]{:S(2)}) copy-start(f32[512,384]{1,0:T(8,128)} %copy-done.8) | copy-start | bytes 2359300
  97.5 11.8 %copy-start.20 = (f32[512,384]{1,0:T(8,128)S(1)}, f32[512,384]{1,0:T(8,128)}, u32[]{:S(2)}) copy-start(f32[512,384]{1,0:T(8,128)} %copy-done.19) | copy-start | bytes 2359300
  100.7 8.6 %copy-start.33 = (bf16[2,512,128]{2,1,0:T(8,128)(2,1)}, bf16[2,512,128]{2,1,0:T(8,128)(2,1)S(1)}, u32[]{:S(2)}) copy-start(bf16[2,512,128]{2,1,0:T(8,128)(2,1)S(1)} %collective-permute-done.13.low_ref) | copy-start | bytes 786436
  103.0 24.6 %collective-permute-start.15 = (bf16[512,1024]{1,0:T(8,128)(2,1)S(1)}, bf16[512,1024]{1,0:T(8,128)(2,1)S(1)}, u32[]{:S(2)}, u32[]{:S(2)}) collective-permute-start(bf16[512,1024]{1,0:T(8,128)(2,1)S(1)} %pad_maximum_fusion.3), channel_id=1, source_target_pairs={{0,4},{4,0},{1,5},{5,1},{2,6},{6,2},{3,7},{7,3},{8,12},{12,8},{9,1... | collective-permute-start | bytes 3145736 | tf_op jit(solution)/shard_map/ppermute | solution.py:43
  103.6 38.3 %collective-permute-start.30 = (bf16[2,512,128]{2,1,0:T(8,128)(2,1)}, bf16[2,512,128]{2,1,0:T(8,128)(2,1)S(1)}, u32[]{:S(2)}, u32[]{:S(2)}) collective-permute-start(bf16[2,512,128]{2,1,0:T(8,128)(2,1)} %get-tuple-element.173), channel_id=1, source_target_pairs={{0,8},{8,16},{16,24},{24,0},{1,9},{9,17},{17,25},{25,1},{2,10},{10... | collective-permute-start | bytes 786440 | tf_op jit(solution)/shard_map/ppermute | solution.py:43
  104.8 40.1 %collective-permute-start.31 = (bf16[2,512,128]{2,1,0:T(8,128)(2,1)}, bf16[2,512,128]{2,1,0:T(8,128)(2,1)S(1)}, u32[]{:S(2)}, u32[]{:S(2)}) collective-permute-start(bf16[2,512,128]{2,1,0:T(8,128)(2,1)} %get-tuple-element.173), channel_id=1, source_target_pairs={{0,24},{8,0},{16,8},{24,16},{1,25},{9,1},{17,9},{25,17},{2,26},{10... | collective-permute-start | bytes 786440 | tf_op jit(solution)/shard_map/ppermute | solution.py:43
  115.8 29.8 %collective-permute-start.28 = (bf16[2,1024,128]{2,1,0:T(8,128)(2,1)}, bf16[2,1024,128]{2,1,0:T(8,128)(2,1)S(1)}, u32[]{:S(2)}, u32[]{:S(2)}) collective-permute-start(bf16[2,1024,128]{2,1,0:T(8,128)(2,1)} %get-tuple-element.172), channel_id=1, source_target_pairs={{0,8},{8,16},{16,24},{24,0},{1,9},{9,17},{17,25},{25,1},{2,10},{10... | collective-permute-start | bytes 1572872 | tf_op jit(solution)/shard_map/ppermute | solution.py:43
  115.8 33.7 %collective-permute-start.29 = (bf16[2,1024,128]{2,1,0:T(8,128)(2,1)}, bf16[2,1024,128]{2,1,0:T(8,128)(2,1)S(1)}, u32[]{:S(2)}, u32[]{:S(2)}) collective-permute-start(bf16[2,1024,128]{2,1,0:T(8,128)(2,1)} %get-tuple-element.172), channel_id=1, source_target_pairs={{0,24},{8,0},{16,8},{24,16},{1,25},{9,1},{17,9},{25,17},{2,26},{10... | collective-permute-start | bytes 1572872 | tf_op jit(solution)/shard_map/ppermute | solution.py:43
  127.6 27.6 %collective-permute-start.26 = (bf16[2,1024,128]{2,1,0:T(8,128)(2,1)}, bf16[2,1024,128]{2,1,0:T(8,128)(2,1)S(1)}, u32[]{:S(2)}, u32[]{:S(2)}) collective-permute-start(bf16[2,1024,128]{2,1,0:T(8,128)(2,1)} %get-tuple-element.171), channel_id=1, source_target_pairs={{0,8},{8,16},{16,24},{24,0},{1,9},{9,17},{17,25},{25,1},{2,10},{10... | collective-permute-start | bytes 1572872 | tf_op jit(solution)/shard_map/ppermute | solution.py:43
  137.3 28.5 %copy-start.6 = (f32[1,2048,128]{2,1,0:T(8,128)S(1)}, f32[1,2048,128]{2,1,0:T(8,128)}, u32[]{:S(2)}) copy-start(f32[1,2048,128]{2,1,0:T(8,128)} %param.13) | copy-start | bytes 3145732
  142.7 32.1 %collective-permute-start.27 = (bf16[2,1024,128]{2,1,0:T(8,128)(2,1)}, bf16[2,1024,128]{2,1,0:T(8,128)(2,1)S(1)}, u32[]{:S(2)}, u32[]{:S(2)}) collective-permute-start(bf16[2,1024,128]{2,1,0:T(8,128)(2,1)} %get-tuple-element.171), channel_id=1, source_target_pairs={{0,24},{8,0},{16,8},{24,16},{1,25},{9,1},{17,9},{25,17},{2,26},{10... | collective-permute-start | bytes 1572872 | tf_op jit(solution)/shard_map/ppermute | solution.py:43
  145.6 32.1 %collective-permute-start.24 = (bf16[2,1024,128]{2,1,0:T(8,128)(2,1)}, bf16[2,1024,128]{2,1,0:T(8,128)(2,1)S(1)}, u32[]{:S(2)}, u32[]{:S(2)}) collective-permute-start(bf16[2,1024,128]{2,1,0:T(8,128)(2,1)} %get-tuple-element.170), channel_id=1, source_target_pairs={{0,8},{8,16},{16,24},{24,0},{1,9},{9,17},{17,25},{25,1},{2,10},{10... | collective-permute-start | bytes 1572872 | tf_op jit(solution)/shard_map/ppermute | solution.py:43
  145.6 25.0 %copy-start.27 = (bf16[2,1024,128]{2,1,0:T(8,128)(2,1)}, bf16[2,1024,128]{2,1,0:T(8,128)(2,1)S(1)}, u32[]{:S(2)}) copy-start(bf16[2,1024,128]{2,1,0:T(8,128)(2,1)S(1)} %collective-permute-done.28.low_ref) | copy-start | bytes 1572868
  145.6 43.4 %collective-permute-start.25 = (bf16[2,1024,128]{2,1,0:T(8,128)(2,1)}, bf16[2,1024,128]{2,1,0:T(8,128)(2,1)S(1)}, u32[]{:S(2)}, u32[]{:S(2)}) collective-permute-start(bf16[2,1024,128]{2,1,0:T(8,128)(2,1)} %get-tuple-element.170), channel_id=1, source_target_pairs={{0,24},{8,0},{16,8},{24,16},{1,25},{9,1},{17,9},{25,17},{2,26},{10... | collective-permute-start | bytes 1572872 | tf_op jit(solution)/shard_map/ppermute | solution.py:43
  150.3 49.9 %collective-permute-start.22 = (bf16[2,1024,128]{2,1,0:T(8,128)(2,1)}, bf16[2,1024,128]{2,1,0:T(8,128)(2,1)S(1)}, u32[]{:S(2)}, u32[]{:S(2)}) collective-permute-start(bf16[2,1024,128]{2,1,0:T(8,128)(2,1)} %get-tuple-element.169), channel_id=1, source_target_pairs={{0,8},{8,16},{16,24},{24,0},{1,9},{9,17},{17,25},{25,1},{2,10},{10... | collective-permute-start | bytes 1572872 | tf_op jit(solution)/shard_map/ppermute | solution.py:43
  155.2 10.7 %copy-start.31 = (bf16[2,1024,128]{2,1,0:T(8,128)(2,1)}, bf16[2,1024,128]{2,1,0:T(8,128)(2,1)S(1)}, u32[]{:S(2)}) copy-start(bf16[2,1024,128]{2,1,0:T(8,128)(2,1)S(1)} %collective-permute-done.26.low_ref) | copy-start | bytes 1572868
  155.2 56.3 %collective-permute-start.23 = (bf16[2,1024,128]{2,1,0:T(8,128)(2,1)}, bf16[2,1024,128]{2,1,0:T(8,128)(2,1)S(1)}, u32[]{:S(2)}, u32[]{:S(2)}) collective-permute-start(bf16[2,1024,128]{2,1,0:T(8,128)(2,1)} %get-tuple-element.169), channel_id=1, source_target_pairs={{0,24},{8,0},{16,8},{24,16},{1,25},{9,1},{17,9},{25,17},{2,26},{10... | collective-permute-start | bytes 1572872 | tf_op jit(solution)/shard_map/ppermute | solution.py:43
  174.8 148.5 %collective-permute-start.18 = (bf16[2,1024,256]{2,1,0:T(8,128)(2,1)S(1)}, bf16[2,1024,256]{2,1,0:T(8,128)(2,1)S(1)}, u32[]{:S(2)}, u32[]{:S(2)}) collective-permute-start(bf16[2,1024,256]{2,1,0:T(8,128)(2,1)S(1)} %get-tuple-element.167), channel_id=1, source_target_pairs={{0,8},{8,16},{16,24},{24,0},{1,9},{9,17},{17,25},{25,1},{2,10},{10... | collective-permute-start | bytes 3145736 | tf_op jit(solution)/shard_map/ppermute | solution.py:43
  177.7 145.7 %collective-permute-start.19 = (bf16[2,1024,256]{2,1,0:T(8,128)(2,1)S(1)}, bf16[2,1024,256]{2,1,0:T(8,128)(2,1)S(1)}, u32[]{:S(2)}, u32[]{:S(2)}) collective-permute-start(bf16[2,1024,256]{2,1,0:T(8,128)(2,1)S(1)} %get-tuple-element.167), channel_id=1, source_target_pairs={{0,24},{8,0},{16,8},{24,16},{1,25},{9,1},{17,9},{25,17},{2,26},{10... | collective-permute-start | bytes 3145736 | tf_op jit(solution)/shard_map/ppermute | solution.py:43
  189.0 78.8 %collective-permute-start.20 = (bf16[2,1024,128]{2,1,0:T(8,128)(2,1)}, bf16[2,1024,128]{2,1,0:T(8,128)(2,1)S(1)}, u32[]{:S(2)}, u32[]{:S(2)}) collective-permute-start(bf16[2,1024,128]{2,1,0:T(8,128)(2,1)} %get-tuple-element.168), channel_id=1, source_target_pairs={{0,8},{8,16},{16,24},{24,0},{1,9},{9,17},{17,25},{25,1},{2,10},{10... | collective-permute-start | bytes 1572872 | tf_op jit(solution)/shard_map/ppermute | solution.py:43
  189.5 78.3 %copy-start.26 = (f32[2,512,128]{2,1,0:T(8,128)S(1)}, f32[2,512,128]{2,1,0:T(8,128)}, u32[]{:S(2)}) copy-start(f32[2,512,128]{2,1,0:T(8,128)} %copy-done.25) | copy-start | bytes 1572868
  189.5 78.3 %copy-start.34 = (bf16[2,512,128]{2,1,0:T(8,128)(2,1)S(1)}, bf16[2,512,128]{2,1,0:T(8,128)(2,1)}, u32[]{:S(2)}) copy-start(bf16[2,512,128]{2,1,0:T(8,128)(2,1)} %copy-done.33) | copy-start | bytes 786436
  189.5 78.3 %copy-start.36 = (bf16[2,512,128]{2,1,0:T(8,128)(2,1)S(1)}, bf16[2,512,128]{2,1,0:T(8,128)(2,1)}, u32[]{:S(2)}) copy-start(bf16[2,512,128]{2,1,0:T(8,128)(2,1)} %copy-done.35) | copy-start | bytes 786436
  200.2 69.1 %copy-start.24 = (f32[2,512,128]{2,1,0:T(8,128)S(1)}, f32[2,512,128]{2,1,0:T(8,128)}, u32[]{:S(2)}) copy-start(f32[2,512,128]{2,1,0:T(8,128)} %copy-done.23) | copy-start | bytes 1572868
  200.2 69.1 %copy-start.38 = (bf16[2,512,128]{2,1,0:T(8,128)(2,1)S(1)}, bf16[2,512,128]{2,1,0:T(8,128)(2,1)}, u32[]{:S(2)}) copy-start(bf16[2,512,128]{2,1,0:T(8,128)(2,1)} %copy-done.37) | copy-start | bytes 786436
  200.2 69.1 %copy-start.40 = (bf16[2,512,128]{2,1,0:T(8,128)(2,1)S(1)}, bf16[2,512,128]{2,1,0:T(8,128)(2,1)}, u32[]{:S(2)}) copy-start(bf16[2,512,128]{2,1,0:T(8,128)(2,1)} %copy-done.39) | copy-start | bytes 786436
  200.2 125.8 %collective-permute-start.16 = (bf16[2,1024,256]{2,1,0:T(8,128)(2,1)}, bf16[2,1024,256]{2,1,0:T(8,128)(2,1)S(1)}, u32[]{:S(2)}, u32[]{:S(2)}) collective-permute-start(bf16[2,1024,256]{2,1,0:T(8,128)(2,1)} %copy-done.41), channel_id=1, source_target_pairs={{0,8},{8,16},{16,24},{24,0},{1,9},{9,17},{17,25},{25,1},{2,10},{10... | collective-permute-start | bytes 3145736 | tf_op jit(solution)/shard_map/ppermute | solution.py:43
  211.4 114.6 %collective-permute-start.17 = (bf16[2,1024,256]{2,1,0:T(8,128)(2,1)}, bf16[2,1024,256]{2,1,0:T(8,128)(2,1)S(1)}, u32[]{:S(2)}, u32[]{:S(2)}) collective-permute-start(bf16[2,1024,256]{2,1,0:T(8,128)(2,1)} %copy-done.41), channel_id=1, source_target_pairs={{0,24},{8,0},{16,8},{24,16},{1,25},{9,1},{17,9},{25,17},{2,26},{10... | collective-permute-start | bytes 3145736 | tf_op jit(solution)/shard_map/ppermute | solution.py:43
  267.8 53.4 %collective-permute-start.21 = (bf16[2,1024,128]{2,1,0:T(8,128)(2,1)}, bf16[2,1024,128]{2,1,0:T(8,128)(2,1)S(1)}, u32[]{:S(2)}, u32[]{:S(2)}) collective-permute-start(bf16[2,1024,128]{2,1,0:T(8,128)(2,1)} %get-tuple-element.168), channel_id=1, source_target_pairs={{0,24},{8,0},{16,8},{24,16},{1,25},{9,1},{17,9},{25,17},{2,26},{10... | collective-permute-start | bytes 1572872 | tf_op jit(solution)/shard_map/ppermute | solution.py:43
  (29 other events, 60.4 us)

commit v2 on v1

--- a/solution.py
+++ b/solution.py
@@ -12,6 +12,8 @@
 F32 = jnp.float32
 BF16 = jnp.bfloat16
 BLOCK = 256
+CORE_PARTS = 4
+VMEM_LIMIT = 24 * 1024 * 1024
 
 rope_theta = 500000.0
 learn_rate = 0.001
@@ -34,7 +36,7 @@
 
 def params(count):
     return pltpu.CompilerParams(
-        dimension_semantics=("arbitrary",) * count, vmem_limit_bytes=40 * 1024 * 1024
+        dimension_semantics=("arbitrary",) * count, vmem_limit_bytes=VMEM_LIMIT
     )
 
 
@@ -93,9 +95,11 @@
         mine, theirs = pieces[2 * part : 2 * part + 2]
         at = pl.ds(part * tokens, tokens)
         other = mm(mine[1], w_mine) + mm(theirs[1], w_theirs)
-        sent_ref[at, :] = other.astype(BF16)
+        sent_ref[0, at, :] = other.astype(BF16)
         oth_ref[at, :] = other
-        own_ref[at, :] = mm(mine[0], w_mine) + mm(theirs[0], w_theirs)
+        own = mm(mine[0], w_mine) + mm(theirs[0], w_theirs)
+        sent_ref[1, at, :] = own.astype(BF16)
+        own_ref[at, :] = own
 
 
 def project(par, pieces, weight, at, cols):
@@ -106,12 +110,14 @@
         piece = pl.BlockSpec((2, tokens // steps, rows), lambda i, p: (0, i, 0))
         whole = pl.BlockSpec((2 * rows, cols), lambda i, p: (0, at))
         out = pl.BlockSpec((tokens // steps, cols), lambda i, p: (i, 0))
+        sent = pl.BlockSpec((2, tokens // steps, cols), lambda i, p: (0, i, 0))
     else:
         unit = 2 * HD
         steps = cols // unit
         piece = pl.BlockSpec((2, tokens, rows), lambda i, p: (0, 0, 0))
         whole = pl.BlockSpec((2 * rows, unit), lambda i, p: (0, at * steps + i))
         out = pl.BlockSpec((parts * tokens, unit), lambda i, p: (0, i))
+        sent = pl.BlockSpec((2, parts * tokens, unit), lambda i, p: (0, 0, i))
     tokens = tokens * parts
     return pl.pallas_call(
         project_kernel,
@@ -119,9 +125,10 @@
             num_scalar_prefetch=1,
             grid=(steps,),
             in_specs=[piece] * len(pieces) + [whole],
-            out_specs=[out] * 3,
+            out_specs=[out, out, sent],
         ),
-        out_shape=[jax.ShapeDtypeStruct((tokens, cols), kind) for kind in (F32, F32, BF16)],
+        out_shape=[jax.ShapeDtypeStruct((tokens, cols), F32)] * 2
+        + [jax.ShapeDtypeStruct((2, tokens, cols), BF16)],
         compiler_params=params(1),
         cost_estimate=cost(8 * tokens * rows * cols, 8 * tokens * rows + 10 * tokens * cols),
         name="project",
@@ -193,20 +200,22 @@
     length = tables[0].shape[0]
     seqs = mask.shape[0]
 
-    def by_rows(cols, at=0):
-        return pl.BlockSpec((length, cols), lambda s: (s, at))
-
-    arrays = [a if isinstance(a, tuple) else (a, a.shape[1], 0) for a in arrays]
-    specs = [by_rows(cols, at) for _, cols, at in arrays]
+    def by_rows(array):
+        if isinstance(array, tuple):
+            array, at = array
+            return pl.BlockSpec((None, length, array.shape[2]), lambda s: (at, s, 0))
+        return pl.BlockSpec((length, array.shape[1]), lambda s: (s, 0))
+
+    specs = [by_rows(a) for a in arrays]
+    values = [a[0] if isinstance(a, tuple) else a for a in arrays]
     table = pl.BlockSpec((length, HD), lambda s: (0, 0))
-    values = [a for a, _, _ in arrays]
     return pl.pallas_call(
         kernel,
         grid=(seqs,),
         in_specs=specs[:2]
         + [table, table, pl.BlockSpec((1, length, length), lambda s: (s, 0, 0))]
         + specs[2:],
-        out_specs=[by_rows(cols) for cols in outs],
+        out_specs=[pl.BlockSpec((length, cols), lambda s: (s, 0)) for cols in outs],
         out_shape=[jax.ShapeDtypeStruct((seqs * length, cols), BF16) for cols in outs],
         compiler_params=params(1),
         cost_estimate=cost(
@@ -280,7 +289,7 @@
 
 def mix(par, coef, chunk, rows, cols, width, to_col, begin, buffer=None):
     count = chunk[0].shape[1]
-    block = min(2 * BLOCK, count)
+    block = min(4 * BLOCK, count)
     total, first, to = rows // block, begin * BLOCK // block, to_col // cols
     source = pl.BlockSpec((1, block, cols), lambda i, j, p: (i, j, 0))
     place = pl.BlockSpec(
@@ -324,13 +333,9 @@
     cotan = cotangent[0].reshape(tokens, shard_cols)
     h_near, h_far = spread(shard, fsdp_count, tensor_count)
 
-    coef = jnp.concatenate([passed_along(edge_weight, "gossip", 1), edge_weight])
-
     wide = shard.astype(F32)
     squares = jnp.sum(wide * wide, -1)
-    got = flip(squares)
-    wq, wk, wv = after((q_w[0], k_w[0], v_w[0]), squares)
-    squares = squares + got
+    squares = squares + flip(squares)
     got_x = far_flip(squares)
     docs = documents[0].astype(F32)
     got_y = other(jnp.concatenate([squares, docs.reshape(tokens)]))
@@ -343,19 +348,18 @@
             for t in range(tensor_count)
         ],
     )
-    w_proj = jnp.concatenate(after((wk, wv, wq), squares), 1).astype(BF16)
+    w_proj = jnp.concatenate(after((k_w[0], v_w[0], q_w[0]), squares), 1).astype(BF16)
     w_out = after(o_w[0], squares).astype(BF16)
     tables = rope_tables(length, HD)
     positions = jnp.arange(length)
     causal = (positions[:, None] >= positions[None, :])[None]
 
     def mask_of(docs):
-        docs = after(docs, squares)
         return (causal & (docs[:, :, None] == docs[:, None, :])).astype(F32)
 
-    mask = mask_of(docs)
-    got_x, coef, w_proj, w_out, mask, *tables = lax.optimization_barrier(
-        (got_x, coef, w_proj, w_out, mask, *tables)
+    mask = mask_of(after(docs, squares))
+    got_x, w_proj, w_out, mask, *tables = lax.optimization_barrier(
+        (got_x, w_proj, w_out, mask, *tables)
     )
     inv_own = lax.rsqrt((squares + got_x) / model_width + norm_eps)
     inv_oth = lax.rsqrt((got_y[:tokens] + got_xy) / model_width + norm_eps)
@@ -373,21 +377,22 @@
     h_pieces = pieces_of(shard, h_near, h_far, inv_own, inv_oth)
     first_cols, rest_cols = 3 * HD, q_cols - HD
     first_own, first_oth, first_sent = project(par, h_pieces, w_proj, 0, first_cols)
-    first_sent = jnp.concatenate([first_sent, first_own.astype(BF16)], 1)
     first_got = other(first_sent)
     rest_own, rest_oth, rest_sent = project(par, after(h_pieces, first_sent), w_proj, 1, rest_cols)
-    rest_sent = jnp.concatenate([rest_sent, rest_own.astype(BF16)], 1)
     mask_oth = mask_of(after(got_y[tokens:], rest_sent).reshape(docs.shape))
-    c_near, c_far = after((c_near, c_far), rest_sent, mask_oth)
-    c_pieces = pieces_of(cotan, c_near, c_far)
-    first_got = after(first_got, c_pieces[0])
+    edge = after(edge_weight, first_sent)
+    coef = jnp.concatenate([passed_along(edge, "gossip", 1), edge_weight])
+    c_near, c_far = after((c_near, c_far), rest_sent, mask_oth, coef)
+    c_pieces = []
+    for i in range(CORE_PARTS):
+        at = slice(i * tokens // CORE_PARTS, (i + 1) * tokens // CORE_PARTS)
+        c_pieces += pieces_of(cotan[at], c_near[at], c_far[at])
+    first_got = after(first_got, *c_pieces[::2])
     first = functools.partial(
         per_sequence, first_kernel, tables=tables, outs=(HD,) * 4, name="first_head", work=4
     )
-    q0, key, value, ctx0 = first((first_own, (first_got, first_cols, 0)), mask=mask)
-    q0_oth, key_oth, value_oth, ctx0_oth = first(
-        (first_oth, (first_got, first_cols, 1)), mask=mask_oth
-    )
+    q0, key, value, ctx0 = first((first_own, (first_got, 0)), mask=mask)
+    q0_oth, key_oth, value_oth, ctx0_oth = first((first_oth, (first_got, 1)), mask=mask_oth)
     rest_got = other(after(rest_sent, first_got))
 
     def shared(pair, *gates):
@@ -400,7 +405,6 @@
     z1 = shared(o_step(ctx0, ctx0_oth, o_w[0], 0, HD, (0, blocks // 2)))
     z2 = shared(o_step(after(ctx0, z1[0]), ctx0_oth, o_w[0], 0, HD, (blocks // 2, blocks)))
     d_own, d_oth, d_sent = project(par, after(c_pieces, z2[0]), w_out, 0, q_cols)
-    d_sent = jnp.concatenate([d_sent, d_own.astype(BF16)], 1)
     rest_got = after(rest_got, d_sent, *z1[1:])
     d_got = other(after(d_sent, rest_got))
     rest = functools.partial(
@@ -411,9 +415,9 @@
         name="rest_heads",
         work=4 * (heads - 1),
     )
-    q_rest, ctx_rest = rest((rest_own, (rest_got, rest_cols, 0), key, value), mask=mask)
+    q_rest, ctx_rest = rest((rest_own, (rest_got, 0), key, value), mask=mask)
     q_rest_oth, ctx_rest_oth = rest(
-        (rest_oth, (rest_got, rest_cols, 1), key_oth, value_oth), mask=mask_oth
+        (rest_oth, (rest_got, 1), key_oth, value_oth), mask=mask_oth
     )
     chunks = [z1, z2]
     for i in range(heads - 1):
@@ -429,17 +433,15 @@
         name="attention_back",
         work=14 * heads,
     )
-    d_proj = back((d_own, (d_got, q_cols, 0), q0, q_rest, key, value), mask=mask)[0]
+    d_proj = back((d_own, (d_got, 0), q0, q_rest, key, value), mask=mask)[0]
     d_proj_oth = back(
-        (d_oth, (d_got, q_cols, 1), q0_oth, q_rest_oth, key_oth, value_oth), mask=mask_oth
+        (d_oth, (d_got, 1), q0_oth, q_rest_oth, key_oth, value_oth), mask=mask_oth
     )[0]
     h_step = functools.partial(step_weights, par, h_pieces)
-    half = q_cols // 2
     for weight, first_col, begin, cols in (
         (k_w[0], 0, 0, HD),
         (v_w[0], 0, HD, HD),
-        (q_w[0], 0, 2 * HD, half),
-        (q_w[0], half, 2 * HD + half, half),
+        *((q_w[0], i * HD, (i + 2) * HD, HD) for i in range(heads)),
     ):
         at = slice(begin, begin + cols)
         d_own = after(d_proj[:, at], chunks[-1][0])
@@ -450,7 +452,7 @@
     for chunk, (name, cols, width, first_col) in zip(
         chunks,
         [("o", HD, q_cols, max(i, 0) * HD) for i in range(-1, heads)]
-        + [("k", HD, HD, 0), ("v", HD, HD, 0), ("q", half, q_cols, 0), ("q", half, q_cols, half)],
+        + [("k", HD, HD, 0), ("v", HD, HD, 0), *(("q", HD, q_cols, i * HD) for i in range(heads))],
     ):
         chunk = (chunk[0], *after(chunk[1:], last))
         begin = blocks // 2 if chunk[0].shape[1] < shard_cols and name in outs else 0

time: 329 us -> 318 us (0.967)
  starting transfers between devices: 63.6 us -> 53.4 us
  local copies, waits for them, and re-layouts: 14.9 us -> 7.52 us
  Pallas kernels: 75.6 us -> 80.3 us
  waiting for transfers between devices: 157 us -> 161 us
    ppermute x23 -> x27, starting transfers between devices: 49.6 us -> 38.4 us  [passed_along(): lax.ppermute(shard, axis, [(i, (i + by) % count) for i in range(count)])]
    unnamed x92 -> x42, local copies, waits for them, and re-layouts: 14.7 us -> 7.09 us
    ppermute x4, waiting for transfers between devices: 6.46 us -> 0.01 us  [spread(): return (lax.ppermute(shard, axes, near), lax.ppermute(shard, axes, far))]
    ppermute x1, waiting for transfers between devices: 3.51 us -> 9.16 us  [body(): lax.ppermute(block, 'tensor', [(t, (t + share) % tensor_count) for t in r...]
    ppermute x23 -> x27, waiting for transfers between devices: 147 us -> 151 us  [passed_along(): lax.ppermute(shard, axis, [(i, (i + by) % count) for i in range(count)])]
    pallas_call x9 -> x11, Pallas kernels: 32 us -> 35.9 us  [step_weights(): pl.pallas_call(step_kernel, grid_spec=pltpu.PrefetchScalarGridSpec(num_sc...]
    pallas_call x9 -> x11, Pallas kernels: 19.3 us -> 17.7 us  [mix(): pl.pallas_call(mix_kernel, grid_spec=pltpu.PrefetchScalarGridSpec(num_sca...]
  transfers between devices with their start and end apart: 32 -> 39, of which waited for: 13 -> 21; matrix products, arithmetic and copies ran while one was open for 4% -> 4% of each run, Pallas kernels for 22% -> 25%
where the time goes in v2:
time: 318 us
  waiting for transfers between devices  161 us (51%)
  Pallas kernels  80.3 us (25%)
  starting transfers between devices  53.4 us (17%)
  other arithmetic  14 us (4%)
  local copies, waits for them, and re-layouts  7.52 us (2%)
    ppermute x27, waiting for transfers between devices, passed_along(): lax.ppermute(shard, axis, [(i, (i + by) % count) for i in range(count)])  151 us
    ppermute x27, starting transfers between devices, passed_along(): lax.ppermute(shard, axis, [(i, (i + by) % count) for i in range(count)])  38.4 us
    pallas_call x11, Pallas kernels, step_weights(): pl.pallas_call(step_kernel, grid_spec=pltpu.PrefetchScalarGridSpec(num_sc...  35.9 us
    pallas_call x11, Pallas kernels, mix(): pl.pallas_call(mix_kernel, grid_spec=pltpu.PrefetchScalarGridSpec(num_sca...  17.7 us
    pallas_call x6, Pallas kernels, per_sequence(): pl.pallas_call(kernel, grid=(seqs,), in_specs=specs[:2] + [table, table,...  15.2 us
    pallas_call x3, Pallas kernels, project(): pl.pallas_call(project_kernel, grid_spec=pltpu.PrefetchScalarGridSpec(num...  11.5 us
    ppermute x1, waiting for transfers between devices, body(): lax.ppermute(block, 'tensor', [(t, (t + share) % tensor_count) for t in r...  9.16 us
    ppermute x4, starting transfers between devices, spread(): return (lax.ppermute(shard, axes, near), lax.ppermute(shard, axes, far))  8.04 us
  transfers between devices with their start and end apart: 39, of which 21 were waited for; matrix products, arithmetic and copies ran while one was open for 4% of the time, Pallas kernels for 25%

profile of v2, /device:TPU:0, one launch (start us, length us, event | category | flops | bytes accessed | tf_op | source)
XLA Modules:
  0.0 317.7 jit_solution(16074787665287054475)
XLA Ops:
  0.6 3.0 collective-permute-start
  7.4 2.8 collective-permute-start.2
  10.2 2.9 collective-permute-start.5
  13.1 2.6 convert.11
  21.1 9.2 %collective-permute-done.2 = f32[512]{0:T(512)S(1)} collective-permute-done((f32[512]{0:T(512)S(1)}, f32[512]{0:T(512)S(1)}, u32[]{:S(2)}, u32[]{:S(2)}) %collective-permute-start.2) | collective-permute-done | bytes 2080 | tf_op jit(solution)/shard_map/ppermute | solution.py:328
  31.1 2.7 collective-permute-start.8
  38.0 4.6 %project.3 = (f32[512,384]{1,0:T(8,128)S(1)}, f32[512,384]{1,0:T(8,128)S(1)}, bf16[2,512,384]{2,1,0:T(8,128)(2,1)}) custom-call(s32[1]{0:T(128)} %bitcast.par_ref, bf16[2,512,1024]{2,1,0:T(8,128)(2,1)S(1)} %pad_maximum_fusion.1.refs_0_, bf16[2,512,1024]{2,1,0:T(8,128)(2,1)} %collective-permute-done.6.refs_1_, bf16[2048,768]{1,0:T(8,128)(2,1)S(1)} %copy-done.3), custom_call_target="tpu_custom_call" | custom-call | flops 1610612736 | bytes 6160384 | tf_op jit(solution)/shard_map/project/pallas_call | solution.py:122
  44.4 2.3 collective-permute-start.14
  46.7 3.9 %project.4 = (f32[512,384]{1,0:T(8,128)S(1)}, f32[512,384]{1,0:T(8,128)S(1)}, bf16[2,512,384]{2,1,0:T(8,128)(2,1)S(1)}) custom-call(s32[1]{0:T(128)} %bitcast.par_ref, bf16[2,512,1024]{2,1,0:T(8,128)(2,1)S(1)} %pad_maximum_fusion.1.refs_0_, bf16[2,512,1024]{2,1,0:T(8,128)(2,1)} %collective-permute-done.6.refs_1_, bf16[2048,768]{1,0:T(8,128)(2,1)S(1)} %copy-done.3), custom_call_target="tpu_custom_call" | custom-call | flops 1610612736 | bytes 6160384 | tf_op jit(solution)/shard_map/project/pallas_call | solution.py:122
  55.0 3.7 %collective-permute-done.7 = f32[1]{0:T(128)} collective-permute-done((f32[1]{0:T(128)}, f32[1]{0:T(128)}, u32[]{:S(2)}, u32[]{:S(2)}) %collective-permute-start.7) | collective-permute-done | bytes 36 | tf_op jit(solution)/shard_map/ppermute | solution.py:45
  59.5 2.0 fusion.2
  62.9 13.1 %collective-permute-done.14.oth = bf16[2,512,384]{2,1,0:T(8,128)(2,1)} collective-permute-done((bf16[2,512,384]{2,1,0:T(8,128)(2,1)}, bf16[2,512,384]{2,1,0:T(8,128)(2,1)}, u32[]{:S(2)}, u32[]{:S(2)}) %collective-permute-start.14) | collective-permute-done | bytes 786464 | tf_op jit(solution)/shard_map/ppermute | solution.py:45
  75.9 2.5 collective-permute-start.15
  85.8 2.1 collective-permute-start.17
  89.5 3.0 project.5
  92.5 2.6 collective-permute-done.16.low_ref
  95.0 4.0 %collective-permute-done.17.high_ref = bf16[2,512,128]{2,1,0:T(8,128)(2,1)S(1)} collective-permute-done((bf16[2,512,128]{2,1,0:T(8,128)(2,1)S(1)}, bf16[2,512,128]{2,1,0:T(8,128)(2,1)S(1)}, u32[]{:S(2)}, u32[]{:S(2)}) %collective-permute-start.17) | collective-permute-done | bytes 262176 | tf_op jit(solution)/shard_map/ppermute | solution.py:45
  100.5 2.7 collective-permute-start.38
  106.8 2.9 step_weights.13
  109.8 3.8 %collective-permute-start.36 = (bf16[2,1024,128]{2,1,0:T(8,128)(2,1)S(1)}, bf16[2,1024,128]{2,1,0:T(8,128)(2,1)S(1)}, u32[]{:S(2)}, u32[]{:S(2)}) collective-permute-start(bf16[2,1024,128]{2,1,0:T(8,128)(2,1)S(1)} %get-tuple-element.192), channel_id=1, source_target_pairs={{0,24},{8,0},{16,8},{24,16},{1,25},{9,1},{17,9},{25,17},{2,26},{10... | collective-permute-start | bytes 1572872 | tf_op jit(solution)/shard_map/ppermute | solution.py:45
  113.6 2.9 step_weights.14
  116.5 3.0 step_weights.15
  119.5 4.0 %collective-permute-done.18.oth = bf16[2,512,512]{2,1,0:T(8,128)(2,1)S(1)} collective-permute-done((bf16[2,512,512]{2,1,0:T(8,128)(2,1)S(1)}, bf16[2,512,512]{2,1,0:T(8,128)(2,1)S(1)}, u32[]{:S(2)}, u32[]{:S(2)}) %collective-permute-start.18) | collective-permute-done | bytes 1048608 | tf_op jit(solution)/shard_map/ppermute | solution.py:45
  125.3 3.9 %attention_back.2 = bf16[512,768]{1,0:T(8,128)(2,1)S(1)} custom-call(f32[512,512]{1,0:T(8,128)S(1)} %get-tuple-element.146.own, bf16[2,512,512]{2,1,0:T(8,128)(2,1)S(1)} %collective-permute-done.18.oth, f32[256,128]{1,0:T(8,128)S(1)} %get-tuple-element.128.cos, f32[256,128]{1,0:T(8,128)S(1)} %get-tuple-element.129.sin, f32[2,256,256]{2,1,0:T(8,128)S(1)} %copy-done.7, ...), custom_call_target="tpu_custom_call" | custom-call | flops 939524096 | bytes 1572864 | tf_op jit(solution)/shard_map/attention_back/pallas_call | solution.py:212
  129.3 3.9 %attention_back.3 = bf16[512,768]{1,0:T(8,128)(2,1)S(1)} custom-call(f32[512,512]{1,0:T(8,128)S(1)} %get-tuple-element.170.own, bf16[2,512,512]{2,1,0:T(8,128)(2,1)S(1)} %collective-permute-done.18.oth, f32[256,128]{1,0:T(8,128)S(1)} %get-tuple-element.128.cos, f32[256,128]{1,0:T(8,128)S(1)} %get-tuple-element.129.sin, ...), custom_call_target="tpu_custom_call" | custom-call | flops 939524096 | bytes 1572864 | tf_op jit(solution)/shard_map/attention_back/pallas_call | solution.py:212
  133.5 2.1 collective-permute-start.34
  135.6 3.8 %collective-permute-start.32 = (bf16[2,1024,128]{2,1,0:T(8,128)(2,1)S(1)}, bf16[2,1024,128]{2,1,0:T(8,128)(2,1)S(1)}, u32[]{:S(2)}, u32[]{:S(2)}) collective-permute-start(bf16[2,1024,128]{2,1,0:T(8,128)(2,1)S(1)} %get-tuple-element.190), channel_id=1, source_target_pairs={{0,24},{8,0},{16,8},{24,16},{1,25},{9,1},{17,9},{25,17},{2,26},{10... | collective-permute-start | bytes 1572872 | tf_op jit(solution)/shard_map/ppermute | solution.py:45
  139.4 4.0 %step_weights.16 = (f32[2,1024,128]{2,1,0:T(8,128)S(1)}, bf16[2,1024,128]{2,1,0:T(8,128)(2,1)S(1)}) custom-call(s32[1]{0:T(128)} %bitcast.par_ref, bf16[2,512,1024]{2,1,0:T(8,128)(2,1)S(1)} %pad_maximum_fusion.1.refs_0_, bf16[2,512,1024]{2,1,0:T(8,128)(2,1)} %collective-permute-done.6.refs_1_, bf16[512,128]{1,0:T(8,128)(2,1)S(1)} %get-tuple-element.169.refs_2_, ...), custom_call_target="tpu_custom_call" | custom-call | flops 536870912 | bytes 6815744 | tf_op jit(solution)/shard_map/step_weights/pallas_call | solution.py:260
  143.5 5.8 %collective-permute-done.33.low_ref = bf16[2,1024,128]{2,1,0:T(8,128)(2,1)S(1)} collective-permute-done((bf16[2,1024,128]{2,1,0:T(8,128)(2,1)S(1)}, bf16[2,1024,128]{2,1,0:T(8,128)(2,1)S(1)}, u32[]{:S(2)}, u32[]{:S(2)}) %collective-permute-start.33) | collective-permute-done | bytes 524320 | tf_op jit(solution)/shard_map/ppermute | solution.py:45
  149.3 2.0 collective-permute-start.30
  151.3 4.1 %step_weights.17 = (f32[2,1024,128]{2,1,0:T(8,128)S(1)}, bf16[2,1024,128]{2,1,0:T(8,128)(2,1)S(1)}) custom-call(s32[1]{0:T(128)} %bitcast.par_ref, bf16[2,512,1024]{2,1,0:T(8,128)(2,1)S(1)} %pad_maximum_fusion.1.refs_0_, bf16[2,512,1024]{2,1,0:T(8,128)(2,1)} %collective-permute-done.6.refs_1_, bf16[512,128]{1,0:T(8,128)(2,1)S(1)} %get-tuple-element.174.refs_2_, ...), custom_call_target="tpu_custom_call" | custom-call | flops 536870912 | bytes 6815744 | tf_op jit(solution)/shard_map/step_weights/pallas_call | solution.py:260
  155.4 4.0 %step_weights.18 = (f32[2,1024,128]{2,1,0:T(8,128)S(1)}, bf16[2,1024,128]{2,1,0:T(8,128)(2,1)S(1)}) custom-call(s32[1]{0:T(128)} %bitcast.par_ref, bf16[2,512,1024]{2,1,0:T(8,128)(2,1)S(1)} %pad_maximum_fusion.1.refs_0_, bf16[2,512,1024]{2,1,0:T(8,128)(2,1)} %collective-permute-done.6.refs_1_, bf16[512,128]{1,0:T(8,128)(2,1)S(1)} %get-tuple-element.176.refs_2_, ...), custom_call_target="tpu_custom_call" | custom-call | flops 536870912 | bytes 6815744 | tf_op jit(solution)/shard_map/step_weights/pallas_call | solution.py:260
  161.1 10.7 %collective-permute-done.31.low_ref = bf16[2,1024,128]{2,1,0:T(8,128)(2,1)S(1)} collective-permute-done((bf16[2,1024,128]{2,1,0:T(8,128)(2,1)S(1)}, bf16[2,1024,128]{2,1,0:T(8,128)(2,1)S(1)}, u32[]{:S(2)}, u32[]{:S(2)}) %collective-permute-start.31) | collective-permute-done | bytes 524320 | tf_op jit(solution)/shard_map/ppermute | solution.py:45
  173.5 9.6 %collective-permute-done.32.high_ref = bf16[2,1024,128]{2,1,0:T(8,128)(2,1)S(1)} collective-permute-done((bf16[2,1024,128]{2,1,0:T(8,128)(2,1)S(1)}, bf16[2,1024,128]{2,1,0:T(8,128)(2,1)S(1)}, u32[]{:S(2)}, u32[]{:S(2)}) %collective-permute-start.32) | collective-permute-done | bytes 524320 | tf_op jit(solution)/shard_map/ppermute | solution.py:45
  183.6 4.0 %step_weights.19 = (f32[2,1024,128]{2,1,0:T(8,128)S(1)}, bf16[2,1024,128]{2,1,0:T(8,128)(2,1)S(1)}) custom-call(s32[1]{0:T(128)} %bitcast.par_ref, bf16[2,512,1024]{2,1,0:T(8,128)(2,1)S(1)} %pad_maximum_fusion.1.refs_0_, bf16[2,512,1024]{2,1,0:T(8,128)(2,1)} %collective-permute-done.6.refs_1_, bf16[512,128]{1,0:T(8,128)(2,1)S(1)} %get-tuple-element.178.refs_2_, ...), custom_call_target="tpu_custom_call" | custom-call | flops 536870912 | bytes 6815744 | tf_op jit(solution)/shard_map/step_weights/pallas_call | solution.py:260
  187.6 6.7 %collective-permute-done.29.low_ref = bf16[2,1024,128]{2,1,0:T(8,128)(2,1)S(1)} collective-permute-done((bf16[2,1024,128]{2,1,0:T(8,128)(2,1)S(1)}, bf16[2,1024,128]{2,1,0:T(8,128)(2,1)S(1)}, u32[]{:S(2)}, u32[]{:S(2)}) %collective-permute-start.29) | collective-permute-done | bytes 524320 | tf_op jit(solution)/shard_map/ppermute | solution.py:45
  196.0 9.5 %collective-permute-done.30.high_ref = bf16[2,1024,128]{2,1,0:T(8,128)(2,1)S(1)} collective-permute-done((bf16[2,1024,128]{2,1,0:T(8,128)(2,1)S(1)}, bf16[2,1024,128]{2,1,0:T(8,128)(2,1)S(1)}, u32[]{:S(2)}, u32[]{:S(2)}) %collective-permute-start.30) | collective-permute-done | bytes 524320 | tf_op jit(solution)/shard_map/ppermute | solution.py:45
  206.0 4.0 %step_weights.20 = (f32[2,1024,128]{2,1,0:T(8,128)S(1)}, bf16[2,1024,128]{2,1,0:T(8,128)(2,1)S(1)}) custom-call(s32[1]{0:T(128)} %bitcast.par_ref, bf16[2,512,1024]{2,1,0:T(8,128)(2,1)S(1)} %pad_maximum_fusion.1.refs_0_, bf16[2,512,1024]{2,1,0:T(8,128)(2,1)} %collective-permute-done.6.refs_1_, bf16[512,128]{1,0:T(8,128)(2,1)S(1)} %get-tuple-element.180.refs_2_, ...), custom_call_target="tpu_custom_call" | custom-call | flops 536870912 | bytes 6815744 | tf_op jit(solution)/shard_map/step_weights/pallas_call | solution.py:260
  210.0 6.8 %collective-permute-done.27.low_ref = bf16[2,1024,128]{2,1,0:T(8,128)(2,1)S(1)} collective-permute-done((bf16[2,1024,128]{2,1,0:T(8,128)(2,1)S(1)}, bf16[2,1024,128]{2,1,0:T(8,128)(2,1)S(1)}, u32[]{:S(2)}, u32[]{:S(2)}) %collective-permute-start.27) | collective-permute-done | bytes 524320 | tf_op jit(solution)/shard_map/ppermute | solution.py:45
  218.4 9.5 %collective-permute-done.28.high_ref = bf16[2,1024,128]{2,1,0:T(8,128)(2,1)S(1)} collective-permute-done((bf16[2,1024,128]{2,1,0:T(8,128)(2,1)S(1)}, bf16[2,1024,128]{2,1,0:T(8,128)(2,1)S(1)}, u32[]{:S(2)}, u32[]{:S(2)}) %collective-permute-start.28) | collective-permute-done | bytes 524320 | tf_op jit(solution)/shard_map/ppermute | solution.py:45
  228.4 10.9 %collective-permute-done.25.low_ref = bf16[2,1024,128]{2,1,0:T(8,128)(2,1)S(1)} collective-permute-done((bf16[2,1024,128]{2,1,0:T(8,128)(2,1)S(1)}, bf16[2,1024,128]{2,1,0:T(8,128)(2,1)S(1)}, u32[]{:S(2)}, u32[]{:S(2)}) %collective-permute-start.25) | collective-permute-done | bytes 524320 | tf_op jit(solution)/shard_map/ppermute | solution.py:45
  240.9 4.0 %step_weights.21 = (f32[2,1024,128]{2,1,0:T(8,128)S(1)}, bf16[2,1024,128]{2,1,0:T(8,128)(2,1)S(1)}) custom-call(s32[1]{0:T(128)} %bitcast.par_ref, bf16[2,512,1024]{2,1,0:T(8,128)(2,1)S(1)} %pad_maximum_fusion.1.refs_0_, bf16[2,512,1024]{2,1,0:T(8,128)(2,1)} %collective-permute-done.6.refs_1_, bf16[512,128]{1,0:T(8,128)(2,1)S(1)} %get-tuple-element.182.refs_2_, ...), custom_call_target="tpu_custom_call" | custom-call | flops 536870912 | bytes 6815744 | tf_op jit(solution)/shard_map/step_weights/pallas_call | solution.py:260
  244.9 5.5 %collective-permute-done.26.high_ref = bf16[2,1024,128]{2,1,0:T(8,128)(2,1)S(1)} collective-permute-done((bf16[2,1024,128]{2,1,0:T(8,128)(2,1)S(1)}, bf16[2,1024,128]{2,1,0:T(8,128)(2,1)S(1)}, u32[]{:S(2)}, u32[]{:S(2)}) %collective-permute-start.26) | collective-permute-done | bytes 524320 | tf_op jit(solution)/shard_map/ppermute | solution.py:45
  250.9 11.0 %collective-permute-done.23.low_ref = bf16[2,1024,128]{2,1,0:T(8,128)(2,1)S(1)} collective-permute-done((bf16[2,1024,128]{2,1,0:T(8,128)(2,1)S(1)}, bf16[2,1024,128]{2,1,0:T(8,128)(2,1)S(1)}, u32[]{:S(2)}, u32[]{:S(2)}) %collective-permute-start.23) | collective-permute-done | bytes 524320 | tf_op jit(solution)/shard_map/ppermute | solution.py:45
  277.7 6.7 %collective-permute-done.21.low_ref = bf16[2,1024,128]{2,1,0:T(8,128)(2,1)S(1)} collective-permute-done((bf16[2,1024,128]{2,1,0:T(8,128)(2,1)S(1)}, bf16[2,1024,128]{2,1,0:T(8,128)(2,1)S(1)}, u32[]{:S(2)}, u32[]{:S(2)}) %collective-permute-start.21) | collective-permute-done | bytes 524320 | tf_op jit(solution)/shard_map/ppermute | solution.py:45
  284.4 10.9 %collective-permute-done.22.high_ref = bf16[2,1024,128]{2,1,0:T(8,128)(2,1)S(1)} collective-permute-done((bf16[2,1024,128]{2,1,0:T(8,128)(2,1)S(1)}, bf16[2,1024,128]{2,1,0:T(8,128)(2,1)S(1)}, u32[]{:S(2)}, u32[]{:S(2)}) %collective-permute-start.22) | collective-permute-done | bytes 524320 | tf_op jit(solution)/shard_map/ppermute | solution.py:45
  296.9 10.0 %collective-permute-done.19.low_ref = bf16[2,1024,128]{2,1,0:T(8,128)(2,1)S(1)} collective-permute-done((bf16[2,1024,128]{2,1,0:T(8,128)(2,1)S(1)}, bf16[2,1024,128]{2,1,0:T(8,128)(2,1)S(1)}, u32[]{:S(2)}, u32[]{:S(2)}) %collective-permute-start.19) | collective-permute-done | bytes 524320 | tf_op jit(solution)/shard_map/ppermute | solution.py:45
  306.9 9.1 %collective-permute-done.20.high_ref = bf16[2,1024,128]{2,1,0:T(8,128)(2,1)S(1)} collective-permute-done((bf16[2,1024,128]{2,1,0:T(8,128)(2,1)S(1)}, bf16[2,1024,128]{2,1,0:T(8,128)(2,1)S(1)}, u32[]{:S(2)}, u32[]{:S(2)}) %collective-permute-start.20) | collective-permute-done | bytes 524320 | tf_op jit(solution)/shard_map/ppermute | solution.py:45
  (133 shorter events, 66.9 us)
Async XLA Ops:
  0.6 29.6 %collective-permute-start = (bf16[512,1024]{1,0:T(8,128)(2,1)}, bf16[512,1024]{1,0:T(8,128)(2,1)S(1)}, u32[]{:S(2)}, u32[]{:S(2)}) collective-permute-start(bf16[512,1024]{1,0:T(8,128)(2,1)} %bitcast.67), channel_id=1, source_target_pairs={{0,2},{1,3},{2,6},{3,7},{4,0},{5,1},{6,4},{7,5},{8,10},{9,11},{10,... | collective-permute-start | bytes 3145736 | tf_op jit(solution)/shard_map/ppermute | solution.py:75
  3.6 26.6 %collective-permute-start.3 = (bf16[512,1024]{1,0:T(8,128)(2,1)}, bf16[512,1024]{1,0:T(8,128)(2,1)S(1)}, u32[]{:S(2)}, u32[]{:S(2)}) collective-permute-start(bf16[512,1024]{1,0:T(8,128)(2,1)} %bitcast.68), channel_id=1, source_target_pairs={{2,4},{3,5},{4,2},{5,3},{10,12},{11,13},{12,10},{13,11},{18,20},{1... | collective-permute-start | bytes 3145736 | tf_op jit(solution)/shard_map/ppermute | solution.py:75
  5.9 1.5 collective-permute-start.1
  7.4 22.8 %collective-permute-start.2 = (f32[512]{0:T(512)S(1)}, f32[512]{0:T(512)S(1)}, u32[]{:S(2)}, u32[]{:S(2)}) collective-permute-start(f32[512]{0:T(512)S(1)} %add.21), channel_id=1, source_target_pairs={{0,2},{1,3},{2,0},{3,1},{4,6},{5,7},{6,4},{7,5},{8,10},{9,11},{10,... | collective-permute-start | bytes 6152 | tf_op jit(solution)/shard_map/ppermute | solution.py:328
  10.2 20.1 %collective-permute-start.5 = (f32[512]{0:T(512)S(1)}, f32[512]{0:T(512)S(1)}, u32[]{:S(2)}, u32[]{:S(2)}) collective-permute-start(f32[512]{0:T(512)S(1)} %add.21), channel_id=1, source_target_pairs={{0,6},{1,7},{2,4},{3,5},{4,2},{5,3},{6,0},{7,1},{8,14},{9,15},{10,... | collective-permute-start | bytes 6152 | tf_op jit(solution)/shard_map/ppermute | solution.py:342
  16.0 14.3 %collective-permute-start.4 = (f32[1024]{0:T(1024)S(1)}, f32[1024]{0:T(1024)S(1)}, u32[]{:S(2)}, u32[]{:S(2)}) collective-permute-start(f32[1024]{0:T(1024)S(1)} %pad_maximum_fusion.8), channel_id=1, source_target_pairs={{0,4},{4,0},{1,5},{5,1},{2,6},{6,2},{3,7},{7,3},{8,12},{12,8},{9,1... | collective-permute-start | bytes 12296 | tf_op jit(solution)/shard_map/ppermute | solution.py:45
  19.5 10.8 %copy-start.19 = (bf16[1,2,256,1024]{3,2,1,0:T(8,128)(2,1)S(1)}, bf16[1,2,256,1024]{3,2,1,0:T(8,128)(2,1)}, u32[]{:S(2)}) copy-start(bf16[1,2,256,1024]{3,2,1,0:T(8,128)(2,1)} %param.8) | copy-start | bytes 3145732
  31.1 5.1 %collective-permute-start.6 = (bf16[2,512,1024]{2,1,0:T(8,128)(2,1)S(1)}, bf16[2,512,1024]{2,1,0:T(8,128)(2,1)}, u32[]{:S(2)}, u32[]{:S(2)}) collective-permute-start(bf16[2,512,1024]{2,1,0:T(8,128)(2,1)S(1)} %pad_maximum_fusion.1.refs_0_), channel_id=1, source_target_pairs={{0,1},{1,0},{2,3},{3,2},{4,5},{5,4},{6,7},{7,6},{8,9},{9,8},{10,11... | collective-permute-start | bytes 6291464 | tf_op jit(solution)/shard_map/ppermute | solution.py:79
  31.1 28.3 %collective-permute-start.8 = (bf16[512,1024]{1,0:T(8,128)(2,1)}, bf16[512,1024]{1,0:T(8,128)(2,1)}, u32[]{:S(2)}, u32[]{:S(2)}) collective-permute-start(bf16[512,1024]{1,0:T(8,128)(2,1)} %bitcast.9), channel_id=1, source_target_pairs={{0,2},{1,3},{2,6},{3,7},{4,0},{5,1},{6,4},{7,5},{8,10},{9,11},{10,... | collective-permute-start | bytes 3145736 | tf_op jit(solution)/shard_map/ppermute | solution.py:75
  33.8 25.6 %collective-permute-start.9 = (bf16[512,1024]{1,0:T(8,128)(2,1)}, bf16[512,1024]{1,0:T(8,128)(2,1)}, u32[]{:S(2)}, u32[]{:S(2)}) collective-permute-start(bf16[512,1024]{1,0:T(8,128)(2,1)} %bitcast.9), channel_id=1, source_target_pairs={{2,4},{3,5},{4,2},{5,3},{10,12},{11,13},{12,10},{13,11},{18,20},{1... | collective-permute-start | bytes 3145736 | tf_op jit(solution)/shard_map/ppermute | solution.py:75
  44.4 31.6 %collective-permute-start.14 = (bf16[2,512,384]{2,1,0:T(8,128)(2,1)}, bf16[2,512,384]{2,1,0:T(8,128)(2,1)}, u32[]{:S(2)}, u32[]{:S(2)}) collective-permute-start(bf16[2,512,384]{2,1,0:T(8,128)(2,1)} %get-tuple-element.117), channel_id=1, source_target_pairs={{0,4},{4,0},{1,5},{5,1},{2,6},{6,2},{3,7},{7,3},{8,12},{12,8},{9,1... | collective-permute-start | bytes 2359304 | tf_op jit(solution)/shard_map/ppermute | solution.py:45
  53.3 5.4 %collective-permute-start.7 = (f32[1]{0:T(128)}, f32[1]{0:T(128)}, u32[]{:S(2)}, u32[]{:S(2)}) collective-permute-start(f32[1]{0:T(128)} %param.15), channel_id=1, source_target_pairs={{0,8},{8,16},{16,24},{24,0},{1,9},{9,17},{17,25},{25,1},{2,10},{10... | collective-permute-start | bytes 20 | tf_op jit(solution)/shard_map/ppermute | solution.py:45
  61.5 14.4 %copy-start.18 = (bf16[2,512,384]{2,1,0:T(8,128)(2,1)S(1)}, bf16[2,512,384]{2,1,0:T(8,128)(2,1)}, u32[]{:S(2)}) copy-start(bf16[2,512,384]{2,1,0:T(8,128)(2,1)} %copy-done.17) | copy-start | bytes 2359300
  61.5 16.9 %copy-start.16 = (f32[512,384]{1,0:T(8,128)S(1)}, f32[512,384]{1,0:T(8,128)}, u32[]{:S(2)}) copy-start(f32[512,384]{1,0:T(8,128)} %copy-done.15) | copy-start | bytes 2359300
  61.5 18.9 %copy-start.7 = (f32[2,256,256]{2,1,0:T(8,128)S(1)}, f32[2,256,256]{2,1,0:T(8,128)}, u32[]{:S(2)}) copy-start(f32[2,256,256]{2,1,0:T(8,128)} %and_convert_fusion.1.mask) | copy-start | bytes 1572868
  61.5 18.9 %copy-start.14 = (f32[512,384]{1,0:T(8,128)S(1)}, f32[512,384]{1,0:T(8,128)}, u32[]{:S(2)}) copy-start(f32[512,384]{1,0:T(8,128)} %copy-done.13) | copy-start | bytes 2359300
  61.7 20.7 %copy-start.1 = (f32[1,2048,512]{2,1,0:T(8,128)S(1)}, f32[1,2048,512]{2,1,0:T(8,128)}, u32[]{:S(2)}) copy-start(f32[1,2048,512]{2,1,0:T(8,128)} %param.14) | copy-start | bytes 12582916
  61.8 20.6 %collective-permute-start.13 = (bf16[2,128,1024]{2,1,0:T(8,128)(2,1)S(1)}, bf16[2,128,1024]{2,1,0:T(8,128)(2,1)S(1)}, u32[]{:S(2)}, u32[]{:S(2)}) collective-permute-start(bf16[2,128,1024]{2,1,0:T(8,128)(2,1)S(1)} %pad_maximum_fusion.5.refs_6_), channel_id=1, source_target_pairs={{0,1},{1,0},{2,3},{3,2},{4,5},{5,4},{6,7},{7,6},{8,9},{9,8},{10,11... | collective-permute-start | bytes 1572872 | tf_op jit(solution)/shard_map/ppermute | solution.py:79
  61.9 20.5 %collective-permute-start.12 = (bf16[2,128,1024]{2,1,0:T(8,128)(2,1)S(1)}, bf16[2,128,1024]{2,1,0:T(8,128)(2,1)S(1)}, u32[]{:S(2)}, u32[]{:S(2)}) collective-permute-start(bf16[2,128,1024]{2,1,0:T(8,128)(2,1)S(1)} %pad_maximum_fusion.4.refs_4_), channel_id=1, source_target_pairs={{0,1},{1,0},{2,3},{3,2},{4,5},{5,4},{6,7},{7,6},{8,9},{9,8},{10,11... | collective-permute-start | bytes 1572872 | tf_op jit(solution)/shard_map/ppermute | solution.py:79
  62.4 20.0 %collective-permute-start.11 = (bf16[2,128,1024]{2,1,0:T(8,128)(2,1)S(1)}, bf16[2,128,1024]{2,1,0:T(8,128)(2,1)S(1)}, u32[]{:S(2)}, u32[]{:S(2)}) collective-permute-start(bf16[2,128,1024]{2,1,0:T(8,128)(2,1)S(1)} %pad_maximum_fusion.3.refs_2_), channel_id=1, source_target_pairs={{0,1},{1,0},{2,3},{3,2},{4,5},{5,4},{6,7},{7,6},{8,9},{9,8},{10,11... | collective-permute-start | bytes 1572872 | tf_op jit(solution)/shard_map/ppermute | solution.py:79
  62.4 20.0 %collective-permute-start.10 = (bf16[2,128,1024]{2,1,0:T(8,128)(2,1)S(1)}, bf16[2,128,1024]{2,1,0:T(8,128)(2,1)S(1)}, u32[]{:S(2)}, u32[]{:S(2)}) collective-permute-start(bf16[2,128,1024]{2,1,0:T(8,128)(2,1)S(1)} %pad_maximum_fusion.2.refs_0_), channel_id=1, source_target_pairs={{0,1},{1,0},{2,3},{3,2},{4,5},{5,4},{6,7},{7,6},{8,9},{9,8},{10,11... | collective-permute-start | bytes 1572872 | tf_op jit(solution)/shard_map/ppermute | solution.py:79
  75.9 23.1 %collective-permute-start.15 = (bf16[2,512,384]{2,1,0:T(8,128)(2,1)S(1)}, bf16[2,512,384]{2,1,0:T(8,128)(2,1)S(1)}, u32[]{:S(2)}, u32[]{:S(2)}) collective-permute-start(bf16[2,512,384]{2,1,0:T(8,128)(2,1)S(1)} %copy-done.18), channel_id=1, source_target_pairs={{0,4},{4,0},{1,5},{5,1},{2,6},{6,2},{3,7},{7,3},{8,12},{12,8},{9,1... | collective-permute-start | bytes 2359304 | tf_op jit(solution)/shard_map/ppermute | solution.py:45
  83.9 11.1 %collective-permute-start.16 = (bf16[2,512,128]{2,1,0:T(8,128)(2,1)S(1)}, bf16[2,512,128]{2,1,0:T(8,128)(2,1)S(1)}, u32[]{:S(2)}, u32[]{:S(2)}) collective-permute-start(bf16[2,512,128]{2,1,0:T(8,128)(2,1)S(1)} %get-tuple-element.149), channel_id=1, source_target_pairs={{0,8},{8,16},{16,24},{24,0},{1,9},{9,17},{17,25},{25,1},{2,10},{10... | collective-permute-start | bytes 786440 | tf_op jit(solution)/shard_map/ppermute | solution.py:45
  85.8 13.3 %collective-permute-start.17 = (bf16[2,512,128]{2,1,0:T(8,128)(2,1)S(1)}, bf16[2,512,128]{2,1,0:T(8,128)(2,1)S(1)}, u32[]{:S(2)}, u32[]{:S(2)}) collective-permute-start(bf16[2,512,128]{2,1,0:T(8,128)(2,1)S(1)} %get-tuple-element.149), channel_id=1, source_target_pairs={{0,24},{8,0},{16,8},{24,16},{1,25},{9,1},{17,9},{25,17},{2,26},{10... | collective-permute-start | bytes 786440 | tf_op jit(solution)/shard_map/ppermute | solution.py:45
  89.5 13.7 %copy-start.12 = (f32[512,384]{1,0:T(8,128)S(1)}, f32[512,384]{1,0:T(8,128)}, u32[]{:S(2)}) copy-start(f32[512,384]{1,0:T(8,128)} %copy-done.11) | copy-start | bytes 2359300
  92.4 12.5 %copy-start.10 = (f32[512,384]{1,0:T(8,128)S(1)}, f32[512,384]{1,0:T(8,128)}, u32[]{:S(2)}) copy-start(f32[512,384]{1,0:T(8,128)} %copy-done.9) | copy-start | bytes 2359300
  99.1 24.4 %collective-permute-start.18 = (bf16[2,512,512]{2,1,0:T(8,128)(2,1)S(1)}, bf16[2,512,512]{2,1,0:T(8,128)(2,1)S(1)}, u32[]{:S(2)}, u32[]{:S(2)}) collective-permute-start(bf16[2,512,512]{2,1,0:T(8,128)(2,1)S(1)} %get-tuple-element.151), channel_id=1, source_target_pairs={{0,4},{4,0},{1,5},{5,1},{2,6},{6,2},{3,7},{7,3},{8,12},{12,8},{9,1... | collective-permute-start | bytes 3145736 | tf_op jit(solution)/shard_map/ppermute | solution.py:45
  99.4 34.1 %collective-permute-start.37 = (bf16[2,512,128]{2,1,0:T(8,128)(2,1)S(1)}, bf16[2,512,128]{2,1,0:T(8,128)(2,1)S(1)}, u32[]{:S(2)}, u32[]{:S(2)}) collective-permute-start(bf16[2,512,128]{2,1,0:T(8,128)(2,1)S(1)} %get-tuple-element.193), channel_id=1, source_target_pairs={{0,8},{8,16},{16,24},{24,0},{1,9},{9,17},{17,25},{25,1},{2,10},{10... | collective-permute-start | bytes 786440 | tf_op jit(solution)/shard_map/ppermute | solution.py:45
  100.5 35.1 %collective-permute-start.38 = (bf16[2,512,128]{2,1,0:T(8,128)(2,1)S(1)}, bf16[2,512,128]{2,1,0:T(8,128)(2,1)S(1)}, u32[]{:S(2)}, u32[]{:S(2)}) collective-permute-start(bf16[2,512,128]{2,1,0:T(8,128)(2,1)S(1)} %get-tuple-element.193), channel_id=1, source_target_pairs={{0,24},{8,0},{16,8},{24,16},{1,25},{9,1},{17,9},{25,17},{2,26},{10... | collective-permute-start | bytes 786440 | tf_op jit(solution)/shard_map/ppermute | solution.py:45
  109.8 25.8 %collective-permute-start.35 = (bf16[2,1024,128]{2,1,0:T(8,128)(2,1)S(1)}, bf16[2,1024,128]{2,1,0:T(8,128)(2,1)S(1)}, u32[]{:S(2)}, u32[]{:S(2)}) collective-permute-start(bf16[2,1024,128]{2,1,0:T(8,128)(2,1)S(1)} %get-tuple-element.192), channel_id=1, source_target_pairs={{0,8},{8,16},{16,24},{24,0},{1,9},{9,17},{17,25},{25,1},{2,10},{10... | collective-permute-start | bytes 1572872 | tf_op jit(solution)/shard_map/ppermute | solution.py:45
  109.8 33.6 %collective-permute-start.36 = (bf16[2,1024,128]{2,1,0:T(8,128)(2,1)S(1)}, bf16[2,1024,128]{2,1,0:T(8,128)(2,1)S(1)}, u32[]{:S(2)}, u32[]{:S(2)}) collective-permute-start(bf16[2,1024,128]{2,1,0:T(8,128)(2,1)S(1)} %get-tuple-element.192), channel_id=1, source_target_pairs={{0,24},{8,0},{16,8},{24,16},{1,25},{9,1},{17,9},{25,17},{2,26},{10... | collective-permute-start | bytes 1572872 | tf_op jit(solution)/shard_map/ppermute | solution.py:45
  123.5 25.8 %collective-permute-start.33 = (bf16[2,1024,128]{2,1,0:T(8,128)(2,1)S(1)}, bf16[2,1024,128]{2,1,0:T(8,128)(2,1)S(1)}, u32[]{:S(2)}, u32[]{:S(2)}) collective-permute-start(bf16[2,1024,128]{2,1,0:T(8,128)(2,1)S(1)} %get-tuple-element.191), channel_id=1, source_target_pairs={{0,8},{8,16},{16,24},{24,0},{1,9},{9,17},{17,25},{25,1},{2,10},{10... | collective-permute-start | bytes 1572872 | tf_op jit(solution)/shard_map/ppermute | solution.py:45
  133.5 27.2 %collective-permute-start.34 = (bf16[2,1024,128]{2,1,0:T(8,128)(2,1)S(1)}, bf16[2,1024,128]{2,1,0:T(8,128)(2,1)S(1)}, u32[]{:S(2)}, u32[]{:S(2)}) collective-permute-start(bf16[2,1024,128]{2,1,0:T(8,128)(2,1)S(1)} %get-tuple-element.191), channel_id=1, source_target_pairs={{0,24},{8,0},{16,8},{24,16},{1,25},{9,1},{17,9},{25,17},{2,26},{10... | collective-permute-start | bytes 1572872 | tf_op jit(solution)/shard_map/ppermute | solution.py:45
  135.6 36.2 %collective-permute-start.31 = (bf16[2,1024,128]{2,1,0:T(8,128)(2,1)S(1)}, bf16[2,1024,128]{2,1,0:T(8,128)(2,1)S(1)}, u32[]{:S(2)}, u32[]{:S(2)}) collective-permute-start(bf16[2,1024,128]{2,1,0:T(8,128)(2,1)S(1)} %get-tuple-element.190), channel_id=1, source_target_pairs={{0,8},{8,16},{16,24},{24,0},{1,9},{9,17},{17,25},{25,1},{2,10},{10... | collective-permute-start | bytes 1572872 | tf_op jit(solution)/shard_map/ppermute | solution.py:45
  135.6 47.5 %collective-permute-start.32 = (bf16[2,1024,128]{2,1,0:T(8,128)(2,1)S(1)}, bf16[2,1024,128]{2,1,0:T(8,128)(2,1)S(1)}, u32[]{:S(2)}, u32[]{:S(2)}) collective-permute-start(bf16[2,1024,128]{2,1,0:T(8,128)(2,1)S(1)} %get-tuple-element.190), channel_id=1, source_target_pairs={{0,24},{8,0},{16,8},{24,16},{1,25},{9,1},{17,9},{25,17},{2,26},{10... | collective-permute-start | bytes 1572872 | tf_op jit(solution)/shard_map/ppermute | solution.py:45
  139.4 11.9 %copy-start.6 = (f32[1,2048,128]{2,1,0:T(8,128)S(1)}, f32[1,2048,128]{2,1,0:T(8,128)}, u32[]{:S(2)}) copy-start(f32[1,2048,128]{2,1,0:T(8,128)} %param.13) | copy-start | bytes 3145732
  143.4 50.9 %collective-permute-start.29 = (bf16[2,1024,128]{2,1,0:T(8,128)(2,1)S(1)}, bf16[2,1024,128]{2,1,0:T(8,128)(2,1)S(1)}, u32[]{:S(2)}, u32[]{:S(2)}) collective-permute-start(bf16[2,1024,128]{2,1,0:T(8,128)(2,1)S(1)} %get-tuple-element.189), channel_id=1, source_target_pairs={{0,8},{8,16},{16,24},{24,0},{1,9},{9,17},{17,25},{25,1},{2,10},{10... | collective-permute-start | bytes 1572872 | tf_op jit(solution)/shard_map/ppermute | solution.py:45
  149.3 56.2 %collective-permute-start.30 = (bf16[2,1024,128]{2,1,0:T(8,128)(2,1)S(1)}, bf16[2,1024,128]{2,1,0:T(8,128)(2,1)S(1)}, u32[]{:S(2)}, u32[]{:S(2)}) collective-permute-start(bf16[2,1024,128]{2,1,0:T(8,128)(2,1)S(1)} %get-tuple-element.189), channel_id=1, source_target_pairs={{0,24},{8,0},{16,8},{24,16},{1,25},{9,1},{17,9},{25,17},{2,26},{10... | collective-permute-start | bytes 1572872 | tf_op jit(solution)/shard_map/ppermute | solution.py:45
  160.6 56.2 %collective-permute-start.27 = (bf16[2,1024,128]{2,1,0:T(8,128)(2,1)S(1)}, bf16[2,1024,128]{2,1,0:T(8,128)(2,1)S(1)}, u32[]{:S(2)}, u32[]{:S(2)}) collective-permute-start(bf16[2,1024,128]{2,1,0:T(8,128)(2,1)S(1)} %get-tuple-element.188), channel_id=1, source_target_pairs={{0,8},{8,16},{16,24},{24,0},{1,9},{9,17},{17,25},{25,1},{2,10},{10... | collective-permute-start | bytes 1572872 | tf_op jit(solution)/shard_map/ppermute | solution.py:45
  171.8 56.2 %collective-permute-start.28 = (bf16[2,1024,128]{2,1,0:T(8,128)(2,1)S(1)}, bf16[2,1024,128]{2,1,0:T(8,128)(2,1)S(1)}, u32[]{:S(2)}, u32[]{:S(2)}) collective-permute-start(bf16[2,1024,128]{2,1,0:T(8,128)(2,1)S(1)} %get-tuple-element.188), channel_id=1, source_target_pairs={{0,24},{8,0},{16,8},{24,16},{1,25},{9,1},{17,9},{25,17},{2,26},{10... | collective-permute-start | bytes 1572872 | tf_op jit(solution)/shard_map/ppermute | solution.py:45
  183.1 56.3 %collective-permute-start.25 = (bf16[2,1024,128]{2,1,0:T(8,128)(2,1)S(1)}, bf16[2,1024,128]{2,1,0:T(8,128)(2,1)S(1)}, u32[]{:S(2)}, u32[]{:S(2)}) collective-permute-start(bf16[2,1024,128]{2,1,0:T(8,128)(2,1)S(1)} %get-tuple-element.187), channel_id=1, source_target_pairs={{0,8},{8,16},{16,24},{24,0},{1,9},{9,17},{17,25},{25,1},{2,10},{10... | collective-permute-start | bytes 1572872 | tf_op jit(solution)/shard_map/ppermute | solution.py:45
  194.3 56.1 %collective-permute-start.26 = (bf16[2,1024,128]{2,1,0:T(8,128)(2,1)S(1)}, bf16[2,1024,128]{2,1,0:T(8,128)(2,1)S(1)}, u32[]{:S(2)}, u32[]{:S(2)}) collective-permute-start(bf16[2,1024,128]{2,1,0:T(8,128)(2,1)S(1)} %get-tuple-element.187), channel_id=1, source_target_pairs={{0,24},{8,0},{16,8},{24,16},{1,25},{9,1},{17,9},{25,17},{2,26},{10... | collective-permute-start | bytes 1572872 | tf_op jit(solution)/shard_map/ppermute | solution.py:45
  205.5 56.3 %collective-permute-start.23 = (bf16[2,1024,128]{2,1,0:T(8,128)(2,1)S(1)}, bf16[2,1024,128]{2,1,0:T(8,128)(2,1)S(1)}, u32[]{:S(2)}, u32[]{:S(2)}) collective-permute-start(bf16[2,1024,128]{2,1,0:T(8,128)(2,1)S(1)} %get-tuple-element.186), channel_id=1, source_target_pairs={{0,8},{8,16},{16,24},{24,0},{1,9},{9,17},{17,25},{25,1},{2,10},{10... | collective-permute-start | bytes 1572872 | tf_op jit(solution)/shard_map/ppermute | solution.py:45
  216.8 59.2 %collective-permute-start.24 = (bf16[2,1024,128]{2,1,0:T(8,128)(2,1)S(1)}, bf16[2,1024,128]{2,1,0:T(8,128)(2,1)S(1)}, u32[]{:S(2)}, u32[]{:S(2)}) collective-permute-start(bf16[2,1024,128]{2,1,0:T(8,128)(2,1)S(1)} %get-tuple-element.186), channel_id=1, source_target_pairs={{0,24},{8,0},{16,8},{24,16},{1,25},{9,1},{17,9},{25,17},{2,26},{10... | collective-permute-start | bytes 1572872 | tf_op jit(solution)/shard_map/ppermute | solution.py:45
  228.0 56.4 %collective-permute-start.21 = (bf16[2,1024,128]{2,1,0:T(8,128)(2,1)S(1)}, bf16[2,1024,128]{2,1,0:T(8,128)(2,1)S(1)}, u32[]{:S(2)}, u32[]{:S(2)}) collective-permute-start(bf16[2,1024,128]{2,1,0:T(8,128)(2,1)S(1)} %get-tuple-element.185), channel_id=1, source_target_pairs={{0,8},{8,16},{16,24},{24,0},{1,9},{9,17},{17,25},{25,1},{2,10},{10... | collective-permute-start | bytes 1572872 | tf_op jit(solution)/shard_map/ppermute | solution.py:45
  239.4 55.9 %collective-permute-start.22 = (bf16[2,1024,128]{2,1,0:T(8,128)(2,1)S(1)}, bf16[2,1024,128]{2,1,0:T(8,128)(2,1)S(1)}, u32[]{:S(2)}, u32[]{:S(2)}) collective-permute-start(bf16[2,1024,128]{2,1,0:T(8,128)(2,1)S(1)} %get-tuple-element.185), channel_id=1, source_target_pairs={{0,24},{8,0},{16,8},{24,16},{1,25},{9,1},{17,9},{25,17},{2,26},{10... | collective-permute-start | bytes 1572872 | tf_op jit(solution)/shard_map/ppermute | solution.py:45
  250.4 56.5 %collective-permute-start.19 = (bf16[2,1024,128]{2,1,0:T(8,128)(2,1)S(1)}, bf16[2,1024,128]{2,1,0:T(8,128)(2,1)S(1)}, u32[]{:S(2)}, u32[]{:S(2)}) collective-permute-start(bf16[2,1024,128]{2,1,0:T(8,128)(2,1)S(1)} %get-tuple-element.184), channel_id=1, source_target_pairs={{0,8},{8,16},{16,24},{24,0},{1,9},{9,17},{17,25},{25,1},{2,10},{10... | collective-permute-start | bytes 1572872 | tf_op jit(solution)/shard_map/ppermute | solution.py:45
  261.9 54.1 %collective-permute-start.20 = (bf16[2,1024,128]{2,1,0:T(8,128)(2,1)S(1)}, bf16[2,1024,128]{2,1,0:T(8,128)(2,1)S(1)}, u32[]{:S(2)}, u32[]{:S(2)}) collective-permute-start(bf16[2,1024,128]{2,1,0:T(8,128)(2,1)S(1)} %get-tuple-element.184), channel_id=1, source_target_pairs={{0,24},{8,0},{16,8},{24,16},{1,25},{9,1},{17,9},{25,17},{2,26},{10... | collective-permute-start | bytes 1572872 | tf_op jit(solution)/shard_map/ppermute | solution.py:45
  (11 other events, 21.0 us)

commit v3 on v2

--- a/solution.py
+++ b/solution.py
@@ -88,7 +88,7 @@
 
 
 def project_kernel(par_ref, *refs):
-    *pieces, w_ref, own_ref, oth_ref, sent_ref = refs
+    *pieces, w_ref, sum_ref, sent_ref = refs
     _, tokens, rows = pieces[0].shape
     w_mine, w_theirs = parity_halves(par_ref, w_ref, rows)
     for part in range(len(pieces) // 2):
@@ -96,10 +96,10 @@
         at = pl.ds(part * tokens, tokens)
         other = mm(mine[1], w_mine) + mm(theirs[1], w_theirs)
         sent_ref[0, at, :] = other.astype(BF16)
-        oth_ref[at, :] = other
+        sum_ref[1, at, :] = other
         own = mm(mine[0], w_mine) + mm(theirs[0], w_theirs)
         sent_ref[1, at, :] = own.astype(BF16)
-        own_ref[at, :] = own
+        sum_ref[0, at, :] = own
 
 
 def project(par, pieces, weight, at, cols):
@@ -109,15 +109,13 @@
         steps, unit = 2, cols
         piece = pl.BlockSpec((2, tokens // steps, rows), lambda i, p: (0, i, 0))
         whole = pl.BlockSpec((2 * rows, cols), lambda i, p: (0, at))
-        out = pl.BlockSpec((tokens // steps, cols), lambda i, p: (i, 0))
-        sent = pl.BlockSpec((2, tokens // steps, cols), lambda i, p: (0, i, 0))
+        out = pl.BlockSpec((2, tokens // steps, cols), lambda i, p: (0, i, 0))
     else:
         unit = 2 * HD
         steps = cols // unit
         piece = pl.BlockSpec((2, tokens, rows), lambda i, p: (0, 0, 0))
         whole = pl.BlockSpec((2 * rows, unit), lambda i, p: (0, at * steps + i))
-        out = pl.BlockSpec((parts * tokens, unit), lambda i, p: (0, i))
-        sent = pl.BlockSpec((2, parts * tokens, unit), lambda i, p: (0, 0, i))
+        out = pl.BlockSpec((2, parts * tokens, unit), lambda i, p: (0, 0, i))
     tokens = tokens * parts
     return pl.pallas_call(
         project_kernel,
@@ -125,10 +123,9 @@
             num_scalar_prefetch=1,
             grid=(steps,),
             in_specs=[piece] * len(pieces) + [whole],
-            out_specs=[out, out, sent],
+            out_specs=[out, out],
         ),
-        out_shape=[jax.ShapeDtypeStruct((tokens, cols), F32)] * 2
-        + [jax.ShapeDtypeStruct((2, tokens, cols), BF16)],
+        out_shape=[jax.ShapeDtypeStruct((2, tokens, cols), kind) for kind in (F32, BF16)],
         compiler_params=params(1),
         cost_estimate=cost(8 * tokens * rows * cols, 8 * tokens * rows + 10 * tokens * cols),
         name="project",
@@ -198,62 +195,58 @@
 
 def per_sequence(kernel, arrays, *, tables, mask, outs, name, work):
     length = tables[0].shape[0]
-    seqs = mask.shape[0]
-
-    def by_rows(array):
-        if isinstance(array, tuple):
-            array, at = array
-            return pl.BlockSpec((None, length, array.shape[2]), lambda s: (at, s, 0))
-        return pl.BlockSpec((length, array.shape[1]), lambda s: (s, 0))
-
-    specs = [by_rows(a) for a in arrays]
-    values = [a[0] if isinstance(a, tuple) else a for a in arrays]
-    table = pl.BlockSpec((length, HD), lambda s: (0, 0))
+    groups, seqs = mask.shape[:2]
+
+    def by_rows(cols):
+        return pl.BlockSpec((None, length, cols), lambda g, s: (g, s, 0))
+
+    specs = [by_rows(a.shape[2]) for a in arrays]
+    table = pl.BlockSpec((length, HD), lambda g, s: (0, 0))
+    square = pl.BlockSpec((None, 1, length, length), lambda g, s: (g, s, 0, 0))
     return pl.pallas_call(
         kernel,
-        grid=(seqs,),
-        in_specs=specs[:2]
-        + [table, table, pl.BlockSpec((1, length, length), lambda s: (s, 0, 0))]
-        + specs[2:],
-        out_specs=[pl.BlockSpec((length, cols), lambda s: (s, 0)) for cols in outs],
-        out_shape=[jax.ShapeDtypeStruct((seqs * length, cols), BF16) for cols in outs],
-        compiler_params=params(1),
+        grid=(groups, seqs),
+        in_specs=specs[:2] + [table, table, square] + specs[2:],
+        out_specs=[by_rows(cols) for cols in outs],
+        out_shape=[jax.ShapeDtypeStruct((groups, seqs * length, cols), BF16) for cols in outs],
+        compiler_params=params(2),
         cost_estimate=cost(
-            seqs * work * length * length * HD,
-            4 * seqs * length * sum(outs),
-            seqs * length * length,
+            groups * seqs * work * length * length * HD,
+            4 * groups * seqs * length * sum(outs),
+            groups * seqs * length * length,
         ),
         name=name,
-    )(*values[:2], *tables, mask, *values[2:])
+    )(*arrays[:2], *tables, mask, *arrays[2:])
 
 
 def step_kernel(par_ref, *refs):
-    *pieces, dy_own, dy_oth, w_mine, w_theirs, u_ref, sent_ref = refs
+    *pieces, dy, w_mine, w_theirs, u_ref, sent_ref = refs
     cols = u_ref.shape[2]
     tokens = pieces[0].shape[1]
     at = pl.ds(pl.multiple_of(pl.program_id(1) * cols, cols), cols)
     for place, weight in ((0, w_mine), (1, w_theirs)):
         grad = 0.0
-        for group, dy in ((0, dy_own), (1, dy_oth)):
+        for group in range(2):
             term = 0.0
             for part in range(len(pieces) // 2):
                 rows = pl.ds(part * tokens, tokens)
-                term += mm(pieces[2 * part + place][group], dy[rows, at], TN)
+                term += mm(pieces[2 * part + place][group], dy[group, rows, at], TN)
             grad += term.astype(BF16).astype(F32)
         updated = weight[...] - learn_rate * grad
         u_ref[place] = updated
         sent_ref[place] = updated.astype(BF16)
 
 
-def step_weights(par, pieces, d_own, d_oth, weight, first_col, unit, blocks=None):
+def step_weights(par, pieces, d_both, d_col, cols, weight, first_col, unit, blocks=None):
     _, part_tokens, rows = pieces[0].shape
-    tokens, cols = d_own.shape
+    tokens = d_both.shape[1]
+    d_at = d_col // cols
     total = rows // BLOCK
     begin, end = blocks or (0, total)
     count = end - begin
     at = first_col // unit
     piece = pl.BlockSpec((2, part_tokens, BLOCK), lambda j, k, p: (0, 0, begin + j))
-    whole = pl.BlockSpec((tokens, cols), lambda j, k, p: (0, 0))
+    whole = pl.BlockSpec((2, tokens, cols), lambda j, k, p: (0, 0, d_at))
     out = pl.BlockSpec((2, BLOCK, unit), lambda j, k, p: (0, j, k))
     mine = lambda j, k, p: (p[0] * total + begin + j, at + k)
     theirs = lambda j, k, p: ((1 - p[0]) * total + begin + j, at + k)
@@ -263,7 +256,7 @@
             num_scalar_prefetch=1,
             grid=(count, cols // unit),
             in_specs=[piece] * len(pieces)
-            + [whole, whole]
+            + [whole]
             + [pl.BlockSpec((BLOCK, unit), mine), pl.BlockSpec((BLOCK, unit), theirs)],
             out_specs=[out, out],
         ),
@@ -274,7 +267,7 @@
         compiler_params=params(2),
         cost_estimate=cost(8 * tokens * count * BLOCK * cols, count * BLOCK * (8 * tokens + 20 * cols)),
         name="step_weights",
-    )(par, *pieces, d_own, d_oth, weight, weight)
+    )(par, *pieces, d_both, weight, weight)
 
 
 def mix_kernel(par_ref, coef, u_ref, low_ref, high_ref, *outs):
@@ -357,10 +350,7 @@
     def mask_of(docs):
         return (causal & (docs[:, :, None] == docs[:, None, :])).astype(F32)
 
-    mask = mask_of(after(docs, squares))
-    got_x, w_proj, w_out, mask, *tables = lax.optimization_barrier(
-        (got_x, w_proj, w_out, mask, *tables)
-    )
+    got_x, w_proj, w_out, *tables = lax.optimization_barrier((got_x, w_proj, w_out, *tables))
     inv_own = lax.rsqrt((squares + got_x) / model_width + norm_eps)
     inv_oth = lax.rsqrt((got_y[:tokens] + got_xy) / model_width + norm_eps)
 
@@ -376,23 +366,24 @@
     c_near, c_far = spread(after(cotan, h_near, h_far), fsdp_count, tensor_count)
     h_pieces = pieces_of(shard, h_near, h_far, inv_own, inv_oth)
     first_cols, rest_cols = 3 * HD, q_cols - HD
-    first_own, first_oth, first_sent = project(par, h_pieces, w_proj, 0, first_cols)
+    first_sum, first_sent = project(par, h_pieces, w_proj, 0, first_cols)
     first_got = other(first_sent)
-    rest_own, rest_oth, rest_sent = project(par, after(h_pieces, first_sent), w_proj, 1, rest_cols)
-    mask_oth = mask_of(after(got_y[tokens:], rest_sent).reshape(docs.shape))
+    rest_sum, rest_sent = project(par, after(h_pieces, first_sent), w_proj, 1, rest_cols)
+    mask = jnp.stack(
+        [mask_of(after(both, rest_sent)) for both in (docs, got_y[tokens:].reshape(docs.shape))]
+    )
     edge = after(edge_weight, first_sent)
     coef = jnp.concatenate([passed_along(edge, "gossip", 1), edge_weight])
-    c_near, c_far = after((c_near, c_far), rest_sent, mask_oth, coef)
+    c_near, c_far = after((c_near, c_far), rest_sent, mask, coef)
     c_pieces = []
     for i in range(CORE_PARTS):
         at = slice(i * tokens // CORE_PARTS, (i + 1) * tokens // CORE_PARTS)
         c_pieces += pieces_of(cotan[at], c_near[at], c_far[at])
     first_got = after(first_got, *c_pieces[::2])
-    first = functools.partial(
-        per_sequence, first_kernel, tables=tables, outs=(HD,) * 4, name="first_head", work=4
-    )
-    q0, key, value, ctx0 = first((first_own, (first_got, 0)), mask=mask)
-    q0_oth, key_oth, value_oth, ctx0_oth = first((first_oth, (first_got, 1)), mask=mask_oth)
+    attend = functools.partial(per_sequence, tables=tables, mask=mask)
+    q0, key, value, ctx0 = attend(
+        first_kernel, (first_sum, first_got), outs=(HD,) * 4, name="first_head", work=4
+    )
     rest_got = other(after(rest_sent, first_got))
 
     def shared(pair, *gates):
@@ -402,50 +393,36 @@
 
     o_step = functools.partial(step_weights, par, c_pieces)
     blocks = shard_cols // BLOCK
-    z1 = shared(o_step(ctx0, ctx0_oth, o_w[0], 0, HD, (0, blocks // 2)))
-    z2 = shared(o_step(after(ctx0, z1[0]), ctx0_oth, o_w[0], 0, HD, (blocks // 2, blocks)))
-    d_own, d_oth, d_sent = project(par, after(c_pieces, z2[0]), w_out, 0, q_cols)
+    z1 = shared(o_step(ctx0, 0, HD, o_w[0], 0, HD, (0, blocks // 2)))
+    z2 = shared(o_step(after(ctx0, z1[0]), 0, HD, o_w[0], 0, HD, (blocks // 2, blocks)))
+    d_sum, d_sent = project(par, after(c_pieces, z2[0]), w_out, 0, q_cols)
     rest_got = after(rest_got, d_sent, *z1[1:])
     d_got = other(after(d_sent, rest_got))
-    rest = functools.partial(
-        per_sequence,
+    q_rest, ctx_rest = attend(
         functools.partial(rest_kernel, heads - 1),
-        tables=tables,
+        (rest_sum, rest_got, key, value),
         outs=(rest_cols,) * 2,
         name="rest_heads",
         work=4 * (heads - 1),
     )
-    q_rest, ctx_rest = rest((rest_own, (rest_got, 0), key, value), mask=mask)
-    q_rest_oth, ctx_rest_oth = rest(
-        (rest_oth, (rest_got, 1), key_oth, value_oth), mask=mask_oth
-    )
     chunks = [z1, z2]
     for i in range(heads - 1):
-        at = slice(i * HD, (i + 1) * HD)
-        d_ctx = after(ctx_rest[:, at], chunks[-1][0])
-        chunks.append(shared(o_step(d_ctx, ctx_rest_oth[:, at], o_w[0], (i + 1) * HD, HD)))
+        d_ctx = after(ctx_rest, chunks[-1][0], *(z2[1:] if i == 1 else ()))
+        chunks.append(shared(o_step(d_ctx, i * HD, HD, o_w[0], (i + 1) * HD, HD)))
     d_got = after(d_got, chunks[-1][0])
-    back = functools.partial(
-        per_sequence,
+    d_proj = attend(
         functools.partial(back_kernel, heads),
-        tables=tables,
+        (d_sum, d_got, q0, q_rest, key, value),
         outs=(q_cols + 2 * HD,),
         name="attention_back",
         work=14 * heads,
-    )
-    d_proj = back((d_own, (d_got, 0), q0, q_rest, key, value), mask=mask)[0]
-    d_proj_oth = back(
-        (d_oth, (d_got, 1), q0_oth, q_rest_oth, key_oth, value_oth), mask=mask_oth
     )[0]
     h_step = functools.partial(step_weights, par, h_pieces)
-    for weight, first_col, begin, cols in (
-        (k_w[0], 0, 0, HD),
-        (v_w[0], 0, HD, HD),
-        *((q_w[0], i * HD, (i + 2) * HD, HD) for i in range(heads)),
+    for i, (weight, first_col) in enumerate(
+        ((k_w[0], 0), (v_w[0], 0), *((q_w[0], i * HD) for i in range(heads)))
     ):
-        at = slice(begin, begin + cols)
-        d_own = after(d_proj[:, at], chunks[-1][0])
-        chunks.append(shared(h_step(d_own, d_proj_oth[:, at], weight, first_col, cols)))
+        d_both = after(d_proj, chunks[-1][0])
+        chunks.append(shared(h_step(d_both, i * HD, HD, weight, first_col, HD)))
 
     outs = {}
     last = coef

time: 318 us -> 317 us (level)
  starting transfers between devices: 53.4 us -> 106 us
  waiting for transfers between devices: 161 us -> 113 us
  local copies, waits for them, and re-layouts: 7.52 us -> 3.45 us
    ppermute x27, starting transfers between devices: 38.4 us -> 91.3 us  [passed_along(): lax.ppermute(shard, axis, [(i, (i + by) % count) for i in range(count)])]
    ppermute x27, waiting for transfers between devices: 151 us -> 101 us  [passed_along(): lax.ppermute(shard, axis, [(i, (i + by) % count) for i in range(count)])]
    unnamed x42 -> x20, local copies, waits for them, and re-layouts: 7.09 us -> 3.43 us
    pallas_call x6 -> x3, Pallas kernels: 15.2 us -> 13.4 us  [per_sequence(): pl.pallas_call(kernel, grid=(groups, seqs), in_specs=specs[:2] + [table,...]
  transfers between devices with their start and end apart: 39 -> 39, of which waited for: 21 -> 18; matrix products, arithmetic and copies ran while one was open for 4% -> 4% of each run, Pallas kernels for 25% -> 24%
where the time goes in v3:
time: 317 us; the launch traced here: 316 us
  waiting for transfers between devices  113 us (36%)
  starting transfers between devices  106 us (33%)
  Pallas kernels  78.3 us (25%)
  other arithmetic  13 us (4%)
  local copies, waits for them, and re-layouts  3.45 us (1%)
    ppermute x27, waiting for transfers between devices, passed_along(): lax.ppermute(shard, axis, [(i, (i + by) % count) for i in range(count)])  101 us
    ppermute x27, starting transfers between devices, passed_along(): lax.ppermute(shard, axis, [(i, (i + by) % count) for i in range(count)])  91.3 us
    pallas_call x11, Pallas kernels, step_weights(): pl.pallas_call(step_kernel, grid_spec=pltpu.PrefetchScalarGridSpec(num_sc...  36.2 us
    pallas_call x11, Pallas kernels, mix(): pl.pallas_call(mix_kernel, grid_spec=pltpu.PrefetchScalarGridSpec(num_sca...  17.7 us
    pallas_call x3, Pallas kernels, per_sequence(): pl.pallas_call(kernel, grid=(groups, seqs), in_specs=specs[:2] + [table,...  13.4 us
    pallas_call x3, Pallas kernels, project(): pl.pallas_call(project_kernel, grid_spec=pltpu.PrefetchScalarGridSpec(num...  11 us
    ppermute x1, waiting for transfers between devices, body(): lax.ppermute(block, 'tensor', [(t, (t + share) % tensor_count) for t in r...  9.38 us
    ppermute x4, starting transfers between devices, spread(): return (lax.ppermute(shard, axes, near), lax.ppermute(shard, axes, far))  8.04 us
  transfers between devices with their start and end apart: 39, of which 18 were waited for; matrix products, arithmetic and copies ran while one was open for 4% of the time, Pallas kernels for 24%

profile of v3, /device:TPU:0, one launch (start us, length us, event | category | flops | bytes accessed | tf_op | source)
XLA Modules:
  0.0 315.9 jit_solution(5256769414997167237)
XLA Ops:
  0.6 3.0 collective-permute-start
  7.3 2.8 collective-permute-start.2
  10.1 2.9 collective-permute-start.5
  13.1 2.6 convert.12
  20.8 9.4 %collective-permute-done.2 = f32[512]{0:T(512)S(1)} collective-permute-done((f32[512]{0:T(512)S(1)}, f32[512]{0:T(512)S(1)}, u32[]{:S(2)}, u32[]{:S(2)}) %collective-permute-start.2) | collective-permute-done | bytes 2080 | tf_op jit(solution)/shard_map/ppermute | solution.py:321
  31.1 2.7 collective-permute-start.8
  38.1 4.0 %project.3 = (f32[2,512,384]{2,1,0:T(8,128)S(1)}, bf16[2,512,384]{2,1,0:T(8,128)(2,1)S(1)}) custom-call(s32[1]{0:T(128)} %bitcast.par_ref, bf16[2,512,1024]{2,1,0:T(8,128)(2,1)S(1)} %pad_maximum_fusion.1.refs_0_, bf16[2,512,1024]{2,1,0:T(8,128)(2,1)} %collective-permute-done.6.refs_1_, bf16[2048,768]{1,0:T(8,128)(2,1)S(1)} %copy-done.3), custom_call_target="tpu_custom_call" | custom-call | flops 1610612736 | bytes 6160384 | tf_op jit(solution)/shard_map/project/pallas_call | solution.py:120
  42.1 2.4 collective-permute-start.14
  44.4 4.0 %project.4 = (f32[2,512,384]{2,1,0:T(8,128)S(1)}, bf16[2,512,384]{2,1,0:T(8,128)(2,1)S(1)}) custom-call(s32[1]{0:T(128)} %bitcast.par_ref, bf16[2,512,1024]{2,1,0:T(8,128)(2,1)S(1)} %pad_maximum_fusion.1.refs_0_, bf16[2,512,1024]{2,1,0:T(8,128)(2,1)} %collective-permute-done.6.refs_1_, bf16[2048,768]{1,0:T(8,128)(2,1)S(1)} %copy-done.3), custom_call_target="tpu_custom_call" | custom-call | flops 1610612736 | bytes 6160384 | tf_op jit(solution)/shard_map/project/pallas_call | solution.py:120
  50.4 3.7 %collective-permute-done.7 = f32[1]{0:T(128)} collective-permute-done((f32[1]{0:T(128)}, f32[1]{0:T(128)}, u32[]{:S(2)}, u32[]{:S(2)}) %collective-permute-start.7) | collective-permute-done | bytes 36 | tf_op jit(solution)/shard_map/ppermute | solution.py:45
  54.7 2.7 collective-permute-done.8
  60.8 15.0 %collective-permute-done.14.oth = bf16[2,512,384]{2,1,0:T(8,128)(2,1)S(1)} collective-permute-done((bf16[2,512,384]{2,1,0:T(8,128)(2,1)S(1)}, bf16[2,512,384]{2,1,0:T(8,128)(2,1)S(1)}, u32[]{:S(2)}, u32[]{:S(2)}) %collective-permute-start.14) | collective-permute-done | bytes 786464 | tf_op jit(solution)/shard_map/ppermute | solution.py:45
  75.8 2.5 collective-permute-start.15
  78.3 2.1 first_head.1
  83.8 2.1 collective-permute-start.17
  87.5 3.0 project.5
  90.5 2.6 collective-permute-done.16.low_ref
  93.0 4.0 %collective-permute-done.17.high_ref = bf16[2,512,128]{2,1,0:T(8,128)(2,1)S(1)} collective-permute-done((bf16[2,512,128]{2,1,0:T(8,128)(2,1)S(1)}, bf16[2,512,128]{2,1,0:T(8,128)(2,1)S(1)}, u32[]{:S(2)}, u32[]{:S(2)}) %collective-permute-start.17) | collective-permute-done | bytes 262176 | tf_op jit(solution)/shard_map/ppermute | solution.py:45
  99.5 2.1 collective-permute-start.20
  101.6 3.4 %rest_heads.1 = (bf16[2,512,384]{2,1,0:T(8,128)(2,1)S(1)}, bf16[2,512,384]{2,1,0:T(8,128)(2,1)S(1)}) custom-call(f32[2,512,384]{2,1,0:T(8,128)S(1)} %get-tuple-element.139.own, bf16[2,512,384]{2,1,0:T(8,128)(2,1)S(1)} %collective-permute-done.15.oth, f32[256,128]{1,0:T(8,128)S(1)} %get-tuple-element.118.cos, f32[256,128]{1,0:T(8,128)S(1)} %get-tuple-element.119.sin, ...), custom_call_target="tpu_custom_call" | custom-call | flops 402653184 | bytes 3145728 | tf_op jit(solution)/shard_map/rest_heads/pallas_call | solution.py:206
  105.0 3.0 step_weights.13
  108.1 3.8 %collective-permute-start.38 = (bf16[2,1024,128]{2,1,0:T(8,128)(2,1)S(1)}, bf16[2,1024,128]{2,1,0:T(8,128)(2,1)S(1)}, u32[]{:S(2)}, u32[]{:S(2)}) collective-permute-start(bf16[2,1024,128]{2,1,0:T(8,128)(2,1)S(1)} %get-tuple-element.173), channel_id=1, source_target_pairs={{0,24},{8,0},{16,8},{24,16},{1,25},{9,1},{17,9},{25,17},{2,26},{10... | collective-permute-start | bytes 1572872 | tf_op jit(solution)/shard_map/ppermute | solution.py:45
  112.0 10.7 %collective-permute-done.20.high_ref = bf16[2,512,128]{2,1,0:T(8,128)(2,1)S(1)} collective-permute-done((bf16[2,512,128]{2,1,0:T(8,128)(2,1)S(1)}, bf16[2,512,128]{2,1,0:T(8,128)(2,1)S(1)}, u32[]{:S(2)}, u32[]{:S(2)}) %collective-permute-start.20) | collective-permute-done | bytes 262176 | tf_op jit(solution)/shard_map/ppermute | solution.py:45
  122.7 3.0 step_weights.14
  125.8 3.8 %collective-permute-start.36 = (bf16[2,1024,128]{2,1,0:T(8,128)(2,1)S(1)}, bf16[2,1024,128]{2,1,0:T(8,128)(2,1)S(1)}, u32[]{:S(2)}, u32[]{:S(2)}) collective-permute-start(bf16[2,1024,128]{2,1,0:T(8,128)(2,1)S(1)} %get-tuple-element.172), channel_id=1, source_target_pairs={{0,24},{8,0},{16,8},{24,16},{1,25},{9,1},{17,9},{25,17},{2,26},{10... | collective-permute-start | bytes 1572872 | tf_op jit(solution)/shard_map/ppermute | solution.py:45
  129.6 3.0 step_weights.15
  132.7 7.9 %attention_back.1.refs_2_ = bf16[2,512,768]{2,1,0:T(8,128)(2,1)S(1)} custom-call(f32[2,512,512]{2,1,0:T(8,128)S(1)} %get-tuple-element.133.own, bf16[2,512,512]{2,1,0:T(8,128)(2,1)S(1)} %collective-permute-done.18.oth, f32[256,128]{1,0:T(8,128)S(1)} %get-tuple-element.118.cos, f32[256,128]{1,0:T(8,128)S(1)} %get-tuple-element.119.sin, ...), custom_call_target="tpu_custom_call" | custom-call | flops 1879048192 | bytes 3145728 | tf_op jit(solution)/shard_map/attention_back/pallas_call | solution.py:206
  140.5 3.8 %collective-permute-start.34 = (bf16[2,1024,128]{2,1,0:T(8,128)(2,1)S(1)}, bf16[2,1024,128]{2,1,0:T(8,128)(2,1)S(1)}, u32[]{:S(2)}, u32[]{:S(2)}) collective-permute-start(bf16[2,1024,128]{2,1,0:T(8,128)(2,1)S(1)} %get-tuple-element.171), channel_id=1, source_target_pairs={{0,24},{8,0},{16,8},{24,16},{1,25},{9,1},{17,9},{25,17},{2,26},{10... | collective-permute-start | bytes 1572872 | tf_op jit(solution)/shard_map/ppermute | solution.py:45
  144.4 3.9 %step_weights.16 = (f32[2,1024,128]{2,1,0:T(8,128)S(1)}, bf16[2,1024,128]{2,1,0:T(8,128)(2,1)S(1)}) custom-call(s32[1]{0:T(128)} %bitcast.par_ref, bf16[2,512,1024]{2,1,0:T(8,128)(2,1)S(1)} %pad_maximum_fusion.1.refs_0_, bf16[2,512,1024]{2,1,0:T(8,128)(2,1)} %collective-permute-done.6.refs_1_, bf16[2,512,768]{2,1,0:T(8,128)(2,1)S(1)} %attention_back.1.refs_2_, ...), custom_call_target="tpu_custom_call" | custom-call | flops 536870912 | bytes 6815744 | tf_op jit(solution)/shard_map/step_weights/pallas_call | solution.py:253
  148.4 10.3 %collective-permute-start.32 = (bf16[2,1024,128]{2,1,0:T(8,128)(2,1)S(1)}, bf16[2,1024,128]{2,1,0:T(8,128)(2,1)S(1)}, u32[]{:S(2)}, u32[]{:S(2)}) collective-permute-start(bf16[2,1024,128]{2,1,0:T(8,128)(2,1)S(1)} %get-tuple-element.170), channel_id=1, source_target_pairs={{0,24},{8,0},{16,8},{24,16},{1,25},{9,1},{17,9},{25,17},{2,26},{10... | collective-permute-start | bytes 1572872 | tf_op jit(solution)/shard_map/ppermute | solution.py:45
  158.7 4.1 %step_weights.17 = (f32[2,1024,128]{2,1,0:T(8,128)S(1)}, bf16[2,1024,128]{2,1,0:T(8,128)(2,1)S(1)}) custom-call(s32[1]{0:T(128)} %bitcast.par_ref, bf16[2,512,1024]{2,1,0:T(8,128)(2,1)S(1)} %pad_maximum_fusion.1.refs_0_, bf16[2,512,1024]{2,1,0:T(8,128)(2,1)} %collective-permute-done.6.refs_1_, bf16[2,512,768]{2,1,0:T(8,128)(2,1)S(1)} %attention_back.1.refs_2_, ...), custom_call_target="tpu_custom_call" | custom-call | flops 536870912 | bytes 6815744 | tf_op jit(solution)/shard_map/step_weights/pallas_call | solution.py:253
  162.8 4.0 %step_weights.18 = (f32[2,1024,128]{2,1,0:T(8,128)S(1)}, bf16[2,1024,128]{2,1,0:T(8,128)(2,1)S(1)}) custom-call(s32[1]{0:T(128)} %bitcast.par_ref, bf16[2,512,1024]{2,1,0:T(8,128)(2,1)S(1)} %pad_maximum_fusion.1.refs_0_, bf16[2,512,1024]{2,1,0:T(8,128)(2,1)} %collective-permute-done.6.refs_1_, bf16[2,512,768]{2,1,0:T(8,128)(2,1)S(1)} %attention_back.1.refs_2_, ...), custom_call_target="tpu_custom_call" | custom-call | flops 536870912 | bytes 6815744 | tf_op jit(solution)/shard_map/step_weights/pallas_call | solution.py:253
  166.9 3.4 %collective-permute-done.33.low_ref = bf16[2,1024,128]{2,1,0:T(8,128)(2,1)S(1)} collective-permute-done((bf16[2,1024,128]{2,1,0:T(8,128)(2,1)S(1)}, bf16[2,1024,128]{2,1,0:T(8,128)(2,1)S(1)}, u32[]{:S(2)}, u32[]{:S(2)}) %collective-permute-start.33) | collective-permute-done | bytes 524320 | tf_op jit(solution)/shard_map/ppermute | solution.py:45
  170.3 10.8 %collective-permute-start.30 = (bf16[2,1024,128]{2,1,0:T(8,128)(2,1)S(1)}, bf16[2,1024,128]{2,1,0:T(8,128)(2,1)S(1)}, u32[]{:S(2)}, u32[]{:S(2)}) collective-permute-start(bf16[2,1024,128]{2,1,0:T(8,128)(2,1)S(1)} %get-tuple-element.169), channel_id=1, source_target_pairs={{0,24},{8,0},{16,8},{24,16},{1,25},{9,1},{17,9},{25,17},{2,26},{10... | collective-permute-start | bytes 1572872 | tf_op jit(solution)/shard_map/ppermute | solution.py:45
  181.9 4.0 %step_weights.19 = (f32[2,1024,128]{2,1,0:T(8,128)S(1)}, bf16[2,1024,128]{2,1,0:T(8,128)(2,1)S(1)}) custom-call(s32[1]{0:T(128)} %bitcast.par_ref, bf16[2,512,1024]{2,1,0:T(8,128)(2,1)S(1)} %pad_maximum_fusion.1.refs_0_, bf16[2,512,1024]{2,1,0:T(8,128)(2,1)} %collective-permute-done.6.refs_1_, bf16[2,512,768]{2,1,0:T(8,128)(2,1)S(1)} %attention_back.1.refs_2_, ...), custom_call_target="tpu_custom_call" | custom-call | flops 536870912 | bytes 6815744 | tf_op jit(solution)/shard_map/step_weights/pallas_call | solution.py:253
  185.9 6.9 %collective-permute-done.31.low_ref = bf16[2,1024,128]{2,1,0:T(8,128)(2,1)S(1)} collective-permute-done((bf16[2,1024,128]{2,1,0:T(8,128)(2,1)S(1)}, bf16[2,1024,128]{2,1,0:T(8,128)(2,1)S(1)}, u32[]{:S(2)}, u32[]{:S(2)}) %collective-permute-start.31) | collective-permute-done | bytes 524320 | tf_op jit(solution)/shard_map/ppermute | solution.py:45
  192.8 10.7 %collective-permute-start.28 = (bf16[2,1024,128]{2,1,0:T(8,128)(2,1)S(1)}, bf16[2,1024,128]{2,1,0:T(8,128)(2,1)S(1)}, u32[]{:S(2)}, u32[]{:S(2)}) collective-permute-start(bf16[2,1024,128]{2,1,0:T(8,128)(2,1)S(1)} %get-tuple-element.168), channel_id=1, source_target_pairs={{0,24},{8,0},{16,8},{24,16},{1,25},{9,1},{17,9},{25,17},{2,26},{10... | collective-permute-start | bytes 1572872 | tf_op jit(solution)/shard_map/ppermute | solution.py:45
  204.3 4.0 %step_weights.20 = (f32[2,1024,128]{2,1,0:T(8,128)S(1)}, bf16[2,1024,128]{2,1,0:T(8,128)(2,1)S(1)}) custom-call(s32[1]{0:T(128)} %bitcast.par_ref, bf16[2,512,1024]{2,1,0:T(8,128)(2,1)S(1)} %pad_maximum_fusion.1.refs_0_, bf16[2,512,1024]{2,1,0:T(8,128)(2,1)} %collective-permute-done.6.refs_1_, bf16[2,512,768]{2,1,0:T(8,128)(2,1)S(1)} %attention_back.1.refs_2_, ...), custom_call_target="tpu_custom_call" | custom-call | flops 536870912 | bytes 6815744 | tf_op jit(solution)/shard_map/step_weights/pallas_call | solution.py:253
  208.3 6.9 %collective-permute-done.29.low_ref = bf16[2,1024,128]{2,1,0:T(8,128)(2,1)S(1)} collective-permute-done((bf16[2,1024,128]{2,1,0:T(8,128)(2,1)S(1)}, bf16[2,1024,128]{2,1,0:T(8,128)(2,1)S(1)}, u32[]{:S(2)}, u32[]{:S(2)}) %collective-permute-start.29) | collective-permute-done | bytes 524320 | tf_op jit(solution)/shard_map/ppermute | solution.py:45
  215.3 10.6 %collective-permute-start.26 = (bf16[2,1024,128]{2,1,0:T(8,128)(2,1)S(1)}, bf16[2,1024,128]{2,1,0:T(8,128)(2,1)S(1)}, u32[]{:S(2)}, u32[]{:S(2)}) collective-permute-start(bf16[2,1024,128]{2,1,0:T(8,128)(2,1)S(1)} %get-tuple-element.167), channel_id=1, source_target_pairs={{0,24},{8,0},{16,8},{24,16},{1,25},{9,1},{17,9},{25,17},{2,26},{10... | collective-permute-start | bytes 1572872 | tf_op jit(solution)/shard_map/ppermute | solution.py:45
  226.8 11.1 %collective-permute-done.27.low_ref = bf16[2,1024,128]{2,1,0:T(8,128)(2,1)S(1)} collective-permute-done((bf16[2,1024,128]{2,1,0:T(8,128)(2,1)S(1)}, bf16[2,1024,128]{2,1,0:T(8,128)(2,1)S(1)}, u32[]{:S(2)}, u32[]{:S(2)}) %collective-permute-start.27) | collective-permute-done | bytes 524320 | tf_op jit(solution)/shard_map/ppermute | solution.py:45
  237.8 10.6 %collective-permute-start.24 = (bf16[2,1024,128]{2,1,0:T(8,128)(2,1)S(1)}, bf16[2,1024,128]{2,1,0:T(8,128)(2,1)S(1)}, u32[]{:S(2)}, u32[]{:S(2)}) collective-permute-start(bf16[2,1024,128]{2,1,0:T(8,128)(2,1)S(1)} %get-tuple-element.166), channel_id=1, source_target_pairs={{0,24},{8,0},{16,8},{24,16},{1,25},{9,1},{17,9},{25,17},{2,26},{10... | collective-permute-start | bytes 1572872 | tf_op jit(solution)/shard_map/ppermute | solution.py:45
  248.4 4.0 %step_weights.21 = (f32[2,1024,128]{2,1,0:T(8,128)S(1)}, bf16[2,1024,128]{2,1,0:T(8,128)(2,1)S(1)}) custom-call(s32[1]{0:T(128)} %bitcast.par_ref, bf16[2,512,1024]{2,1,0:T(8,128)(2,1)S(1)} %pad_maximum_fusion.1.refs_0_, bf16[2,512,1024]{2,1,0:T(8,128)(2,1)} %collective-permute-done.6.refs_1_, bf16[2,512,768]{2,1,0:T(8,128)(2,1)S(1)} %attention_back.1.refs_2_, ...), custom_call_target="tpu_custom_call" | custom-call | flops 536870912 | bytes 6815744 | tf_op jit(solution)/shard_map/step_weights/pallas_call | solution.py:253
  252.5 7.9 %collective-permute-done.25.low_ref = bf16[2,1024,128]{2,1,0:T(8,128)(2,1)S(1)} collective-permute-done((bf16[2,1024,128]{2,1,0:T(8,128)(2,1)S(1)}, bf16[2,1024,128]{2,1,0:T(8,128)(2,1)S(1)}, u32[]{:S(2)}, u32[]{:S(2)}) %collective-permute-start.25) | collective-permute-done | bytes 524320 | tf_op jit(solution)/shard_map/ppermute | solution.py:45
  260.3 10.5 %collective-permute-start.22 = (bf16[2,1024,128]{2,1,0:T(8,128)(2,1)S(1)}, bf16[2,1024,128]{2,1,0:T(8,128)(2,1)S(1)}, u32[]{:S(2)}, u32[]{:S(2)}) collective-permute-start(bf16[2,1024,128]{2,1,0:T(8,128)(2,1)S(1)} %get-tuple-element.165), channel_id=1, source_target_pairs={{0,24},{8,0},{16,8},{24,16},{1,25},{9,1},{17,9},{25,17},{2,26},{10... | collective-permute-start | bytes 1572872 | tf_op jit(solution)/shard_map/ppermute | solution.py:45
  285.2 8.5 %collective-permute-done.24.high_ref = bf16[2,1024,128]{2,1,0:T(8,128)(2,1)S(1)} collective-permute-done((bf16[2,1024,128]{2,1,0:T(8,128)(2,1)S(1)}, bf16[2,1024,128]{2,1,0:T(8,128)(2,1)S(1)}, u32[]{:S(2)}, u32[]{:S(2)}) %collective-permute-start.24) | collective-permute-done | bytes 524320 | tf_op jit(solution)/shard_map/ppermute | solution.py:45
  295.3 10.0 %collective-permute-done.21.low_ref = bf16[2,1024,128]{2,1,0:T(8,128)(2,1)S(1)} collective-permute-done((bf16[2,1024,128]{2,1,0:T(8,128)(2,1)S(1)}, bf16[2,1024,128]{2,1,0:T(8,128)(2,1)S(1)}, u32[]{:S(2)}, u32[]{:S(2)}) %collective-permute-start.21) | collective-permute-done | bytes 524320 | tf_op jit(solution)/shard_map/ppermute | solution.py:45
  305.4 8.8 %collective-permute-done.22.high_ref = bf16[2,1024,128]{2,1,0:T(8,128)(2,1)S(1)} collective-permute-done((bf16[2,1024,128]{2,1,0:T(8,128)(2,1)S(1)}, bf16[2,1024,128]{2,1,0:T(8,128)(2,1)S(1)}, u32[]{:S(2)}, u32[]{:S(2)}) %collective-permute-start.22) | collective-permute-done | bytes 524320 | tf_op jit(solution)/shard_map/ppermute | solution.py:45
  (104 shorter events, 47.0 us)
Async XLA Ops:
  0.6 29.6 %collective-permute-start = (bf16[512,1024]{1,0:T(8,128)(2,1)}, bf16[512,1024]{1,0:T(8,128)(2,1)S(1)}, u32[]{:S(2)}, u32[]{:S(2)}) collective-permute-start(bf16[512,1024]{1,0:T(8,128)(2,1)} %bitcast.67), channel_id=1, source_target_pairs={{0,2},{1,3},{2,6},{3,7},{4,0},{5,1},{6,4},{7,5},{8,10},{9,11},{10,... | collective-permute-start | bytes 3145736 | tf_op jit(solution)/shard_map/ppermute | solution.py:75
  3.6 26.6 %collective-permute-start.3 = (bf16[512,1024]{1,0:T(8,128)(2,1)}, bf16[512,1024]{1,0:T(8,128)(2,1)S(1)}, u32[]{:S(2)}, u32[]{:S(2)}) collective-permute-start(bf16[512,1024]{1,0:T(8,128)(2,1)} %bitcast.68), channel_id=1, source_target_pairs={{2,4},{3,5},{4,2},{5,3},{10,12},{11,13},{12,10},{13,11},{18,20},{1... | collective-permute-start | bytes 3145736 | tf_op jit(solution)/shard_map/ppermute | solution.py:75
  5.9 1.5 collective-permute-start.1
  7.3 22.9 %collective-permute-start.2 = (f32[512]{0:T(512)S(1)}, f32[512]{0:T(512)S(1)}, u32[]{:S(2)}, u32[]{:S(2)}) collective-permute-start(f32[512]{0:T(512)S(1)} %add.21), channel_id=1, source_target_pairs={{0,2},{1,3},{2,0},{3,1},{4,6},{5,7},{6,4},{7,5},{8,10},{9,11},{10,... | collective-permute-start | bytes 6152 | tf_op jit(solution)/shard_map/ppermute | solution.py:321
  10.1 20.1 %collective-permute-start.5 = (f32[512]{0:T(512)S(1)}, f32[512]{0:T(512)S(1)}, u32[]{:S(2)}, u32[]{:S(2)}) collective-permute-start(f32[512]{0:T(512)S(1)} %add.21), channel_id=1, source_target_pairs={{0,6},{1,7},{2,4},{3,5},{4,2},{5,3},{6,0},{7,1},{8,14},{9,15},{10,... | collective-permute-start | bytes 6152 | tf_op jit(solution)/shard_map/ppermute | solution.py:335
  13.1 2.6 copy-start.4
  13.1 2.8 copy-start.5
  15.9 3.3 %copy-start = (f32[1,2048,512]{2,1,0:T(8,128)S(1)}, f32[1,2048,512]{2,1,0:T(8,128)}, u32[]{:S(2)}) copy-start(f32[1,2048,512]{2,1,0:T(8,128)} %param.14) | copy-start | bytes 12582916
  15.9 14.3 %collective-permute-start.4 = (f32[1024]{0:T(1024)S(1)}, f32[1024]{0:T(1024)S(1)}, u32[]{:S(2)}, u32[]{:S(2)}) collective-permute-start(f32[1024]{0:T(1024)S(1)} %pad_maximum_fusion.8), channel_id=1, source_target_pairs={{0,4},{4,0},{1,5},{5,1},{2,6},{6,2},{3,7},{7,3},{8,12},{12,8},{9,1... | collective-permute-start | bytes 12296 | tf_op jit(solution)/shard_map/ppermute | solution.py:45
  19.2 11.0 %copy-start.8 = (bf16[1,2,256,1024]{3,2,1,0:T(8,128)(2,1)S(1)}, bf16[1,2,256,1024]{3,2,1,0:T(8,128)(2,1)}, u32[]{:S(2)}) copy-start(bf16[1,2,256,1024]{3,2,1,0:T(8,128)(2,1)} %param.8) | copy-start | bytes 3145732
  31.1 5.1 %collective-permute-start.6 = (bf16[2,512,1024]{2,1,0:T(8,128)(2,1)S(1)}, bf16[2,512,1024]{2,1,0:T(8,128)(2,1)}, u32[]{:S(2)}, u32[]{:S(2)}) collective-permute-start(bf16[2,512,1024]{2,1,0:T(8,128)(2,1)S(1)} %pad_maximum_fusion.1.refs_0_), channel_id=1, source_target_pairs={{0,1},{1,0},{2,3},{3,2},{4,5},{5,4},{6,7},{7,6},{8,9},{9,8},{10,11... | collective-permute-start | bytes 6291464 | tf_op jit(solution)/shard_map/ppermute | solution.py:79
  31.1 26.3 %collective-permute-start.8 = (bf16[512,1024]{1,0:T(8,128)(2,1)}, bf16[512,1024]{1,0:T(8,128)(2,1)}, u32[]{:S(2)}, u32[]{:S(2)}) collective-permute-start(bf16[512,1024]{1,0:T(8,128)(2,1)} %bitcast.8), channel_id=1, source_target_pairs={{0,2},{1,3},{2,6},{3,7},{4,0},{5,1},{6,4},{7,5},{8,10},{9,11},{10,... | collective-permute-start | bytes 3145736 | tf_op jit(solution)/shard_map/ppermute | solution.py:75
  33.8 23.6 %collective-permute-start.9 = (bf16[512,1024]{1,0:T(8,128)(2,1)}, bf16[512,1024]{1,0:T(8,128)(2,1)}, u32[]{:S(2)}, u32[]{:S(2)}) collective-permute-start(bf16[512,1024]{1,0:T(8,128)(2,1)} %bitcast.8), channel_id=1, source_target_pairs={{2,4},{3,5},{4,2},{5,3},{10,12},{11,13},{12,10},{13,11},{18,20},{1... | collective-permute-start | bytes 3145736 | tf_op jit(solution)/shard_map/ppermute | solution.py:75
  36.2 1.9 copy-start.3
  42.1 33.7 %collective-permute-start.14 = (bf16[2,512,384]{2,1,0:T(8,128)(2,1)S(1)}, bf16[2,512,384]{2,1,0:T(8,128)(2,1)S(1)}, u32[]{:S(2)}, u32[]{:S(2)}) collective-permute-start(bf16[2,512,384]{2,1,0:T(8,128)(2,1)S(1)} %get-tuple-element.106), channel_id=1, source_target_pairs={{0,4},{4,0},{1,5},{5,1},{2,6},{6,2},{3,7},{7,3},{8,12},{12,8},{9,1... | collective-permute-start | bytes 2359304 | tf_op jit(solution)/shard_map/ppermute | solution.py:45
  48.5 5.6 %collective-permute-start.7 = (f32[1]{0:T(128)}, f32[1]{0:T(128)}, u32[]{:S(2)}, u32[]{:S(2)}) collective-permute-start(f32[1]{0:T(128)} %param.15), channel_id=1, source_target_pairs={{0,8},{8,16},{16,24},{24,0},{1,9},{9,17},{17,25},{25,1},{2,10},{10... | collective-permute-start | bytes 20 | tf_op jit(solution)/shard_map/ppermute | solution.py:45
  59.6 20.8 %copy-start.1 = (f32[1,2048,512]{2,1,0:T(8,128)S(1)}, f32[1,2048,512]{2,1,0:T(8,128)}, u32[]{:S(2)}) copy-start(f32[1,2048,512]{2,1,0:T(8,128)} %param.14) | copy-start | bytes 12582916
  59.7 20.7 %collective-permute-start.13 = (bf16[2,128,1024]{2,1,0:T(8,128)(2,1)S(1)}, bf16[2,128,1024]{2,1,0:T(8,128)(2,1)S(1)}, u32[]{:S(2)}, u32[]{:S(2)}) collective-permute-start(bf16[2,128,1024]{2,1,0:T(8,128)(2,1)S(1)} %pad_maximum_fusion.5.refs_6_), channel_id=1, source_target_pairs={{0,1},{1,0},{2,3},{3,2},{4,5},{5,4},{6,7},{7,6},{8,9},{9,8},{10,11... | collective-permute-start | bytes 1572872 | tf_op jit(solution)/shard_map/ppermute | solution.py:79
  59.8 20.6 %collective-permute-start.12 = (bf16[2,128,1024]{2,1,0:T(8,128)(2,1)S(1)}, bf16[2,128,1024]{2,1,0:T(8,128)(2,1)S(1)}, u32[]{:S(2)}, u32[]{:S(2)}) collective-permute-start(bf16[2,128,1024]{2,1,0:T(8,128)(2,1)S(1)} %pad_maximum_fusion.4.refs_4_), channel_id=1, source_target_pairs={{0,1},{1,0},{2,3},{3,2},{4,5},{5,4},{6,7},{7,6},{8,9},{9,8},{10,11... | collective-permute-start | bytes 1572872 | tf_op jit(solution)/shard_map/ppermute | solution.py:79
  60.3 20.1 %collective-permute-start.11 = (bf16[2,128,1024]{2,1,0:T(8,128)(2,1)S(1)}, bf16[2,128,1024]{2,1,0:T(8,128)(2,1)S(1)}, u32[]{:S(2)}, u32[]{:S(2)}) collective-permute-start(bf16[2,128,1024]{2,1,0:T(8,128)(2,1)S(1)} %pad_maximum_fusion.3.refs_2_), channel_id=1, source_target_pairs={{0,1},{1,0},{2,3},{3,2},{4,5},{5,4},{6,7},{7,6},{8,9},{9,8},{10,11... | collective-permute-start | bytes 1572872 | tf_op jit(solution)/shard_map/ppermute | solution.py:79
  60.4 20.1 %collective-permute-start.10 = (bf16[2,128,1024]{2,1,0:T(8,128)(2,1)S(1)}, bf16[2,128,1024]{2,1,0:T(8,128)(2,1)S(1)}, u32[]{:S(2)}, u32[]{:S(2)}) collective-permute-start(bf16[2,128,1024]{2,1,0:T(8,128)(2,1)S(1)} %pad_maximum_fusion.2.refs_0_), channel_id=1, source_target_pairs={{0,1},{1,0},{2,3},{3,2},{4,5},{5,4},{6,7},{7,6},{8,9},{9,8},{10,11... | collective-permute-start | bytes 1572872 | tf_op jit(solution)/shard_map/ppermute | solution.py:79
  75.8 21.3 %collective-permute-start.15 = (bf16[2,512,384]{2,1,0:T(8,128)(2,1)S(1)}, bf16[2,512,384]{2,1,0:T(8,128)(2,1)S(1)}, u32[]{:S(2)}, u32[]{:S(2)}) collective-permute-start(bf16[2,512,384]{2,1,0:T(8,128)(2,1)S(1)} %get-tuple-element.135), channel_id=1, source_target_pairs={{0,4},{4,0},{1,5},{5,1},{2,6},{6,2},{3,7},{7,3},{8,12},{12,8},{9,1... | collective-permute-start | bytes 2359304 | tf_op jit(solution)/shard_map/ppermute | solution.py:45
  82.0 11.1 %collective-permute-start.16 = (bf16[2,512,128]{2,1,0:T(8,128)(2,1)S(1)}, bf16[2,512,128]{2,1,0:T(8,128)(2,1)S(1)}, u32[]{:S(2)}, u32[]{:S(2)}) collective-permute-start(bf16[2,512,128]{2,1,0:T(8,128)(2,1)S(1)} %get-tuple-element.136), channel_id=1, source_target_pairs={{0,8},{8,16},{16,24},{24,0},{1,9},{9,17},{17,25},{25,1},{2,10},{10... | collective-permute-start | bytes 786440 | tf_op jit(solution)/shard_map/ppermute | solution.py:45
  83.8 13.3 %collective-permute-start.17 = (bf16[2,512,128]{2,1,0:T(8,128)(2,1)S(1)}, bf16[2,512,128]{2,1,0:T(8,128)(2,1)S(1)}, u32[]{:S(2)}, u32[]{:S(2)}) collective-permute-start(bf16[2,512,128]{2,1,0:T(8,128)(2,1)S(1)} %get-tuple-element.136), channel_id=1, source_target_pairs={{0,24},{8,0},{16,8},{24,16},{1,25},{9,1},{17,9},{25,17},{2,26},{10... | collective-permute-start | bytes 786440 | tf_op jit(solution)/shard_map/ppermute | solution.py:45
  85.9 1.6 copy-start.7
  97.1 35.5 %collective-permute-start.18 = (bf16[2,512,512]{2,1,0:T(8,128)(2,1)S(1)}, bf16[2,512,512]{2,1,0:T(8,128)(2,1)S(1)}, u32[]{:S(2)}, u32[]{:S(2)}) collective-permute-start(bf16[2,512,512]{2,1,0:T(8,128)(2,1)S(1)} %get-tuple-element.138), channel_id=1, source_target_pairs={{0,4},{4,0},{1,5},{5,1},{2,6},{6,2},{3,7},{7,3},{8,12},{12,8},{9,1... | collective-permute-start | bytes 3145736 | tf_op jit(solution)/shard_map/ppermute | solution.py:45
  97.8 14.2 %collective-permute-start.19 = (bf16[2,512,128]{2,1,0:T(8,128)(2,1)S(1)}, bf16[2,512,128]{2,1,0:T(8,128)(2,1)S(1)}, u32[]{:S(2)}, u32[]{:S(2)}) collective-permute-start(bf16[2,512,128]{2,1,0:T(8,128)(2,1)S(1)} %get-tuple-element.145), channel_id=1, source_target_pairs={{0,8},{8,16},{16,24},{24,0},{1,9},{9,17},{17,25},{25,1},{2,10},{10... | collective-permute-start | bytes 786440 | tf_op jit(solution)/shard_map/ppermute | solution.py:45
  99.5 23.2 %collective-permute-start.20 = (bf16[2,512,128]{2,1,0:T(8,128)(2,1)S(1)}, bf16[2,512,128]{2,1,0:T(8,128)(2,1)S(1)}, u32[]{:S(2)}, u32[]{:S(2)}) collective-permute-start(bf16[2,512,128]{2,1,0:T(8,128)(2,1)S(1)} %get-tuple-element.145), channel_id=1, source_target_pairs={{0,24},{8,0},{16,8},{24,16},{1,25},{9,1},{17,9},{25,17},{2,26},{10... | collective-permute-start | bytes 786440 | tf_op jit(solution)/shard_map/ppermute | solution.py:45
  108.1 32.5 %collective-permute-start.37 = (bf16[2,1024,128]{2,1,0:T(8,128)(2,1)S(1)}, bf16[2,1024,128]{2,1,0:T(8,128)(2,1)S(1)}, u32[]{:S(2)}, u32[]{:S(2)}) collective-permute-start(bf16[2,1024,128]{2,1,0:T(8,128)(2,1)S(1)} %get-tuple-element.173), channel_id=1, source_target_pairs={{0,8},{8,16},{16,24},{24,0},{1,9},{9,17},{17,25},{25,1},{2,10},{10... | collective-permute-start | bytes 1572872 | tf_op jit(solution)/shard_map/ppermute | solution.py:45
  108.1 40.2 %collective-permute-start.38 = (bf16[2,1024,128]{2,1,0:T(8,128)(2,1)S(1)}, bf16[2,1024,128]{2,1,0:T(8,128)(2,1)S(1)}, u32[]{:S(2)}, u32[]{:S(2)}) collective-permute-start(bf16[2,1024,128]{2,1,0:T(8,128)(2,1)S(1)} %get-tuple-element.173), channel_id=1, source_target_pairs={{0,24},{8,0},{16,8},{24,16},{1,25},{9,1},{17,9},{25,17},{2,26},{10... | collective-permute-start | bytes 1572872 | tf_op jit(solution)/shard_map/ppermute | solution.py:45
  125.7 22.7 %collective-permute-start.35 = (bf16[2,1024,128]{2,1,0:T(8,128)(2,1)S(1)}, bf16[2,1024,128]{2,1,0:T(8,128)(2,1)S(1)}, u32[]{:S(2)}, u32[]{:S(2)}) collective-permute-start(bf16[2,1024,128]{2,1,0:T(8,128)(2,1)S(1)} %get-tuple-element.172), channel_id=1, source_target_pairs={{0,8},{8,16},{16,24},{24,0},{1,9},{9,17},{17,25},{25,1},{2,10},{10... | collective-permute-start | bytes 1572872 | tf_op jit(solution)/shard_map/ppermute | solution.py:45
  125.8 41.1 %collective-permute-start.36 = (bf16[2,1024,128]{2,1,0:T(8,128)(2,1)S(1)}, bf16[2,1024,128]{2,1,0:T(8,128)(2,1)S(1)}, u32[]{:S(2)}, u32[]{:S(2)}) collective-permute-start(bf16[2,1024,128]{2,1,0:T(8,128)(2,1)S(1)} %get-tuple-element.172), channel_id=1, source_target_pairs={{0,24},{8,0},{16,8},{24,16},{1,25},{9,1},{17,9},{25,17},{2,26},{10... | collective-permute-start | bytes 1572872 | tf_op jit(solution)/shard_map/ppermute | solution.py:45
  132.6 37.7 %collective-permute-start.33 = (bf16[2,1024,128]{2,1,0:T(8,128)(2,1)S(1)}, bf16[2,1024,128]{2,1,0:T(8,128)(2,1)S(1)}, u32[]{:S(2)}, u32[]{:S(2)}) collective-permute-start(bf16[2,1024,128]{2,1,0:T(8,128)(2,1)S(1)} %get-tuple-element.171), channel_id=1, source_target_pairs={{0,8},{8,16},{16,24},{24,0},{1,9},{9,17},{17,25},{25,1},{2,10},{10... | collective-permute-start | bytes 1572872 | tf_op jit(solution)/shard_map/ppermute | solution.py:45
  140.5 18.1 %copy-start.6 = (f32[1,2048,128]{2,1,0:T(8,128)S(1)}, f32[1,2048,128]{2,1,0:T(8,128)}, u32[]{:S(2)}) copy-start(f32[1,2048,128]{2,1,0:T(8,128)} %param.13) | copy-start | bytes 3145732
  140.5 41.0 %collective-permute-start.34 = (bf16[2,1024,128]{2,1,0:T(8,128)(2,1)S(1)}, bf16[2,1024,128]{2,1,0:T(8,128)(2,1)S(1)}, u32[]{:S(2)}, u32[]{:S(2)}) collective-permute-start(bf16[2,1024,128]{2,1,0:T(8,128)(2,1)S(1)} %get-tuple-element.171), channel_id=1, source_target_pairs={{0,24},{8,0},{16,8},{24,16},{1,25},{9,1},{17,9},{25,17},{2,26},{10... | collective-permute-start | bytes 1572872 | tf_op jit(solution)/shard_map/ppermute | solution.py:45
  148.3 44.5 %collective-permute-start.31 = (bf16[2,1024,128]{2,1,0:T(8,128)(2,1)S(1)}, bf16[2,1024,128]{2,1,0:T(8,128)(2,1)S(1)}, u32[]{:S(2)}, u32[]{:S(2)}) collective-permute-start(bf16[2,1024,128]{2,1,0:T(8,128)(2,1)S(1)} %get-tuple-element.170), channel_id=1, source_target_pairs={{0,8},{8,16},{16,24},{24,0},{1,9},{9,17},{17,25},{25,1},{2,10},{10... | collective-permute-start | bytes 1572872 | tf_op jit(solution)/shard_map/ppermute | solution.py:45
  148.4 55.6 %collective-permute-start.32 = (bf16[2,1024,128]{2,1,0:T(8,128)(2,1)S(1)}, bf16[2,1024,128]{2,1,0:T(8,128)(2,1)S(1)}, u32[]{:S(2)}, u32[]{:S(2)}) collective-permute-start(bf16[2,1024,128]{2,1,0:T(8,128)(2,1)S(1)} %get-tuple-element.170), channel_id=1, source_target_pairs={{0,24},{8,0},{16,8},{24,16},{1,25},{9,1},{17,9},{25,17},{2,26},{10... | collective-permute-start | bytes 1572872 | tf_op jit(solution)/shard_map/ppermute | solution.py:45
  158.7 4.1 %copy-start.2 = (f32[1,2048,512]{2,1,0:T(8,128)S(1)}, f32[1,2048,512]{2,1,0:T(8,128)}, u32[]{:S(2)}) copy-start(f32[1,2048,512]{2,1,0:T(8,128)} %param.11) | copy-start | bytes 12582916
  166.8 48.5 %collective-permute-start.29 = (bf16[2,1024,128]{2,1,0:T(8,128)(2,1)S(1)}, bf16[2,1024,128]{2,1,0:T(8,128)(2,1)S(1)}, u32[]{:S(2)}, u32[]{:S(2)}) collective-permute-start(bf16[2,1024,128]{2,1,0:T(8,128)(2,1)S(1)} %get-tuple-element.169), channel_id=1, source_target_pairs={{0,8},{8,16},{16,24},{24,0},{1,9},{9,17},{17,25},{25,1},{2,10},{10... | collective-permute-start | bytes 1572872 | tf_op jit(solution)/shard_map/ppermute | solution.py:45
  170.3 56.2 %collective-permute-start.30 = (bf16[2,1024,128]{2,1,0:T(8,128)(2,1)S(1)}, bf16[2,1024,128]{2,1,0:T(8,128)(2,1)S(1)}, u32[]{:S(2)}, u32[]{:S(2)}) collective-permute-start(bf16[2,1024,128]{2,1,0:T(8,128)(2,1)S(1)} %get-tuple-element.169), channel_id=1, source_target_pairs={{0,24},{8,0},{16,8},{24,16},{1,25},{9,1},{17,9},{25,17},{2,26},{10... | collective-permute-start | bytes 1572872 | tf_op jit(solution)/shard_map/ppermute | solution.py:45
  181.5 56.3 %collective-permute-start.27 = (bf16[2,1024,128]{2,1,0:T(8,128)(2,1)S(1)}, bf16[2,1024,128]{2,1,0:T(8,128)(2,1)S(1)}, u32[]{:S(2)}, u32[]{:S(2)}) collective-permute-start(bf16[2,1024,128]{2,1,0:T(8,128)(2,1)S(1)} %get-tuple-element.168), channel_id=1, source_target_pairs={{0,8},{8,16},{16,24},{24,0},{1,9},{9,17},{17,25},{25,1},{2,10},{10... | collective-permute-start | bytes 1572872 | tf_op jit(solution)/shard_map/ppermute | solution.py:45
  192.8 59.6 %collective-permute-start.28 = (bf16[2,1024,128]{2,1,0:T(8,128)(2,1)S(1)}, bf16[2,1024,128]{2,1,0:T(8,128)(2,1)S(1)}, u32[]{:S(2)}, u32[]{:S(2)}) collective-permute-start(bf16[2,1024,128]{2,1,0:T(8,128)(2,1)S(1)} %get-tuple-element.168), channel_id=1, source_target_pairs={{0,24},{8,0},{16,8},{24,16},{1,25},{9,1},{17,9},{25,17},{2,26},{10... | collective-permute-start | bytes 1572872 | tf_op jit(solution)/shard_map/ppermute | solution.py:45
  204.0 56.3 %collective-permute-start.25 = (bf16[2,1024,128]{2,1,0:T(8,128)(2,1)S(1)}, bf16[2,1024,128]{2,1,0:T(8,128)(2,1)S(1)}, u32[]{:S(2)}, u32[]{:S(2)}) collective-permute-start(bf16[2,1024,128]{2,1,0:T(8,128)(2,1)S(1)} %get-tuple-element.167), channel_id=1, source_target_pairs={{0,8},{8,16},{16,24},{24,0},{1,9},{9,17},{17,25},{25,1},{2,10},{10... | collective-permute-start | bytes 1572872 | tf_op jit(solution)/shard_map/ppermute | solution.py:45
  215.3 68.2 %collective-permute-start.26 = (bf16[2,1024,128]{2,1,0:T(8,128)(2,1)S(1)}, bf16[2,1024,128]{2,1,0:T(8,128)(2,1)S(1)}, u32[]{:S(2)}, u32[]{:S(2)}) collective-permute-start(bf16[2,1024,128]{2,1,0:T(8,128)(2,1)S(1)} %get-tuple-element.167), channel_id=1, source_target_pairs={{0,24},{8,0},{16,8},{24,16},{1,25},{9,1},{17,9},{25,17},{2,26},{10... | collective-permute-start | bytes 1572872 | tf_op jit(solution)/shard_map/ppermute | solution.py:45
  226.4 58.8 %collective-permute-start.23 = (bf16[2,1024,128]{2,1,0:T(8,128)(2,1)S(1)}, bf16[2,1024,128]{2,1,0:T(8,128)(2,1)S(1)}, u32[]{:S(2)}, u32[]{:S(2)}) collective-permute-start(bf16[2,1024,128]{2,1,0:T(8,128)(2,1)S(1)} %get-tuple-element.166), channel_id=1, source_target_pairs={{0,8},{8,16},{16,24},{24,0},{1,9},{9,17},{17,25},{25,1},{2,10},{10... | collective-permute-start | bytes 1572872 | tf_op jit(solution)/shard_map/ppermute | solution.py:45
  237.8 55.9 %collective-permute-start.24 = (bf16[2,1024,128]{2,1,0:T(8,128)(2,1)S(1)}, bf16[2,1024,128]{2,1,0:T(8,128)(2,1)S(1)}, u32[]{:S(2)}, u32[]{:S(2)}) collective-permute-start(bf16[2,1024,128]{2,1,0:T(8,128)(2,1)S(1)} %get-tuple-element.166), channel_id=1, source_target_pairs={{0,24},{8,0},{16,8},{24,16},{1,25},{9,1},{17,9},{25,17},{2,26},{10... | collective-permute-start | bytes 1572872 | tf_op jit(solution)/shard_map/ppermute | solution.py:45
  252.4 53.0 %collective-permute-start.21 = (bf16[2,1024,128]{2,1,0:T(8,128)(2,1)S(1)}, bf16[2,1024,128]{2,1,0:T(8,128)(2,1)S(1)}, u32[]{:S(2)}, u32[]{:S(2)}) collective-permute-start(bf16[2,1024,128]{2,1,0:T(8,128)(2,1)S(1)} %get-tuple-element.165), channel_id=1, source_target_pairs={{0,8},{8,16},{16,24},{24,0},{1,9},{9,17},{17,25},{25,1},{2,10},{10... | collective-permute-start | bytes 1572872 | tf_op jit(solution)/shard_map/ppermute | solution.py:45
  260.3 53.9 %collective-permute-start.22 = (bf16[2,1024,128]{2,1,0:T(8,128)(2,1)S(1)}, bf16[2,1024,128]{2,1,0:T(8,128)(2,1)S(1)}, u32[]{:S(2)}, u32[]{:S(2)}) collective-permute-start(bf16[2,1024,128]{2,1,0:T(8,128)(2,1)S(1)} %get-tuple-element.165), channel_id=1, source_target_pairs={{0,24},{8,0},{16,8},{24,16},{1,25},{9,1},{17,9},{25,17},{2,26},{10... | collective-permute-start | bytes 1572872 | tf_op jit(solution)/shard_map/ppermute | solution.py:45

commit v4 on v3

--- a/solution.py
+++ b/solution.py
@@ -384,7 +384,7 @@
     q0, key, value, ctx0 = attend(
         first_kernel, (first_sum, first_got), outs=(HD,) * 4, name="first_head", work=4
     )
-    rest_got = other(after(rest_sent, first_got))
+    rest_got = other(after(rest_sent, ctx0))
 
     def shared(pair, *gates):
         updated, sent = pair

time: 317 us -> 319 us (level)
  transfers between devices with their start and end apart: 39 -> 39, of which waited for: 18 -> 19; matrix products, arithmetic and copies ran while one was open for 4% -> 4% of each run, Pallas kernels for 24% -> 24%
where the time goes in v4:
time: 319 us; the launch traced here: 318 us
  waiting for transfers between devices  114 us (36%)
  starting transfers between devices  108 us (34%)
  Pallas kernels  78.3 us (25%)
  other arithmetic  13 us (4%)
  local copies, waits for them, and re-layouts  3.45 us (1%)
    ppermute x27, waiting for transfers between devices, passed_along(): lax.ppermute(shard, axis, [(i, (i + by) % count) for i in range(count)])  102 us
    ppermute x27, starting transfers between devices, passed_along(): lax.ppermute(shard, axis, [(i, (i + by) % count) for i in range(count)])  92.5 us
    pallas_call x11, Pallas kernels, step_weights(): pl.pallas_call(step_kernel, grid_spec=pltpu.PrefetchScalarGridSpec(num_sc...  36.2 us
    pallas_call x11, Pallas kernels, mix(): pl.pallas_call(mix_kernel, grid_spec=pltpu.PrefetchScalarGridSpec(num_sca...  17.7 us
    pallas_call x3, Pallas kernels, per_sequence(): pl.pallas_call(kernel, grid=(groups, seqs), in_specs=specs[:2] + [table,...  13.4 us
    pallas_call x3, Pallas kernels, project(): pl.pallas_call(project_kernel, grid_spec=pltpu.PrefetchScalarGridSpec(num...  11 us
    ppermute x1, waiting for transfers between devices, body(): lax.ppermute(block, 'tensor', [(t, (t + share) % tensor_count) for t in r...  9.38 us
    ppermute x4, starting transfers between devices, spread(): return (lax.ppermute(shard, axes, near), lax.ppermute(shard, axes, far))  8.04 us
  transfers between devices with their start and end apart: 39, of which 19 were waited for; matrix products, arithmetic and copies ran while one was open for 4% of the time, Pallas kernels for 24%

profile of v4, /device:TPU:0, one launch (start us, length us, event | category | flops | bytes accessed | tf_op | source)
XLA Modules:
  0.0 318.0 jit_solution(15706737299016645756)
XLA Ops:
  0.6 3.0 collective-permute-start
  7.3 2.8 collective-permute-start.2
  10.1 2.9 collective-permute-start.5
  13.1 2.6 convert.12
  20.8 9.4 %collective-permute-done.2 = f32[512]{0:T(512)S(1)} collective-permute-done((f32[512]{0:T(512)S(1)}, f32[512]{0:T(512)S(1)}, u32[]{:S(2)}, u32[]{:S(2)}) %collective-permute-start.2) | collective-permute-done | bytes 2080 | tf_op jit(solution)/shard_map/ppermute | solution.py:321
  31.1 2.7 collective-permute-start.8
  38.1 4.0 %project.3 = (f32[2,512,384]{2,1,0:T(8,128)S(1)}, bf16[2,512,384]{2,1,0:T(8,128)(2,1)S(1)}) custom-call(s32[1]{0:T(128)} %bitcast.par_ref, bf16[2,512,1024]{2,1,0:T(8,128)(2,1)S(1)} %pad_maximum_fusion.1.refs_0_, bf16[2,512,1024]{2,1,0:T(8,128)(2,1)} %collective-permute-done.6.refs_1_, bf16[2048,768]{1,0:T(8,128)(2,1)S(1)} %copy-done.3), custom_call_target="tpu_custom_call" | custom-call | flops 1610612736 | bytes 6160384 | tf_op jit(solution)/shard_map/project/pallas_call | solution.py:120
  42.1 2.4 collective-permute-start.14
  44.4 4.0 %project.4 = (f32[2,512,384]{2,1,0:T(8,128)S(1)}, bf16[2,512,384]{2,1,0:T(8,128)(2,1)S(1)}) custom-call(s32[1]{0:T(128)} %bitcast.par_ref, bf16[2,512,1024]{2,1,0:T(8,128)(2,1)S(1)} %pad_maximum_fusion.1.refs_0_, bf16[2,512,1024]{2,1,0:T(8,128)(2,1)} %collective-permute-done.6.refs_1_, bf16[2048,768]{1,0:T(8,128)(2,1)S(1)} %copy-done.3), custom_call_target="tpu_custom_call" | custom-call | flops 1610612736 | bytes 6160384 | tf_op jit(solution)/shard_map/project/pallas_call | solution.py:120
  50.4 3.7 %collective-permute-done.7 = f32[1]{0:T(128)} collective-permute-done((f32[1]{0:T(128)}, f32[1]{0:T(128)}, u32[]{:S(2)}, u32[]{:S(2)}) %collective-permute-start.7) | collective-permute-done | bytes 36 | tf_op jit(solution)/shard_map/ppermute | solution.py:45
  54.7 2.7 collective-permute-done.8
  60.8 15.0 %collective-permute-done.14.oth = bf16[2,512,384]{2,1,0:T(8,128)(2,1)S(1)} collective-permute-done((bf16[2,512,384]{2,1,0:T(8,128)(2,1)S(1)}, bf16[2,512,384]{2,1,0:T(8,128)(2,1)S(1)}, u32[]{:S(2)}, u32[]{:S(2)}) %collective-permute-start.14) | collective-permute-done | bytes 786464 | tf_op jit(solution)/shard_map/ppermute | solution.py:45
  75.8 2.1 first_head.1
  77.9 2.5 collective-permute-start.15
  83.8 2.1 collective-permute-start.17
  87.5 3.0 project.5
  90.5 2.6 collective-permute-done.16.low_ref
  93.1 4.0 %collective-permute-done.17.high_ref = bf16[2,512,128]{2,1,0:T(8,128)(2,1)S(1)} collective-permute-done((bf16[2,512,128]{2,1,0:T(8,128)(2,1)S(1)}, bf16[2,512,128]{2,1,0:T(8,128)(2,1)S(1)}, u32[]{:S(2)}, u32[]{:S(2)}) %collective-permute-start.17) | collective-permute-done | bytes 262176 | tf_op jit(solution)/shard_map/ppermute | solution.py:45
  101.7 2.1 collective-permute-start.20
  103.7 3.4 %rest_heads.1 = (bf16[2,512,384]{2,1,0:T(8,128)(2,1)S(1)}, bf16[2,512,384]{2,1,0:T(8,128)(2,1)S(1)}) custom-call(f32[2,512,384]{2,1,0:T(8,128)S(1)} %get-tuple-element.139.own, bf16[2,512,384]{2,1,0:T(8,128)(2,1)S(1)} %collective-permute-done.15.oth, f32[256,128]{1,0:T(8,128)S(1)} %get-tuple-element.118.cos, f32[256,128]{1,0:T(8,128)S(1)} %get-tuple-element.119.sin, ...), custom_call_target="tpu_custom_call" | custom-call | flops 402653184 | bytes 3145728 | tf_op jit(solution)/shard_map/rest_heads/pallas_call | solution.py:206
  107.2 3.1 step_weights.13
  110.3 3.8 %collective-permute-start.38 = (bf16[2,1024,128]{2,1,0:T(8,128)(2,1)S(1)}, bf16[2,1024,128]{2,1,0:T(8,128)(2,1)S(1)}, u32[]{:S(2)}, u32[]{:S(2)}) collective-permute-start(bf16[2,1024,128]{2,1,0:T(8,128)(2,1)S(1)} %get-tuple-element.173), channel_id=1, source_target_pairs={{0,24},{8,0},{16,8},{24,16},{1,25},{9,1},{17,9},{25,17},{2,26},{10... | collective-permute-start | bytes 1572872 | tf_op jit(solution)/shard_map/ppermute | solution.py:45
  114.1 10.7 %collective-permute-done.20.high_ref = bf16[2,512,128]{2,1,0:T(8,128)(2,1)S(1)} collective-permute-done((bf16[2,512,128]{2,1,0:T(8,128)(2,1)S(1)}, bf16[2,512,128]{2,1,0:T(8,128)(2,1)S(1)}, u32[]{:S(2)}, u32[]{:S(2)}) %collective-permute-start.20) | collective-permute-done | bytes 262176 | tf_op jit(solution)/shard_map/ppermute | solution.py:45
  124.8 3.0 step_weights.14
  127.9 3.8 %collective-permute-start.36 = (bf16[2,1024,128]{2,1,0:T(8,128)(2,1)S(1)}, bf16[2,1024,128]{2,1,0:T(8,128)(2,1)S(1)}, u32[]{:S(2)}, u32[]{:S(2)}) collective-permute-start(bf16[2,1024,128]{2,1,0:T(8,128)(2,1)S(1)} %get-tuple-element.172), channel_id=1, source_target_pairs={{0,24},{8,0},{16,8},{24,16},{1,25},{9,1},{17,9},{25,17},{2,26},{10... | collective-permute-start | bytes 1572872 | tf_op jit(solution)/shard_map/ppermute | solution.py:45
  131.7 3.0 step_weights.15
  134.8 7.9 %attention_back.1.refs_2_ = bf16[2,512,768]{2,1,0:T(8,128)(2,1)S(1)} custom-call(f32[2,512,512]{2,1,0:T(8,128)S(1)} %get-tuple-element.133.own, bf16[2,512,512]{2,1,0:T(8,128)(2,1)S(1)} %collective-permute-done.18.oth, f32[256,128]{1,0:T(8,128)S(1)} %get-tuple-element.118.cos, f32[256,128]{1,0:T(8,128)S(1)} %get-tuple-element.119.sin, ...), custom_call_target="tpu_custom_call" | custom-call | flops 1879048192 | bytes 3145728 | tf_op jit(solution)/shard_map/attention_back/pallas_call | solution.py:206
  142.7 3.9 %collective-permute-start.34 = (bf16[2,1024,128]{2,1,0:T(8,128)(2,1)S(1)}, bf16[2,1024,128]{2,1,0:T(8,128)(2,1)S(1)}, u32[]{:S(2)}, u32[]{:S(2)}) collective-permute-start(bf16[2,1024,128]{2,1,0:T(8,128)(2,1)S(1)} %get-tuple-element.171), channel_id=1, source_target_pairs={{0,24},{8,0},{16,8},{24,16},{1,25},{9,1},{17,9},{25,17},{2,26},{10... | collective-permute-start | bytes 1572872 | tf_op jit(solution)/shard_map/ppermute | solution.py:45
  146.6 3.9 %step_weights.16 = (f32[2,1024,128]{2,1,0:T(8,128)S(1)}, bf16[2,1024,128]{2,1,0:T(8,128)(2,1)S(1)}) custom-call(s32[1]{0:T(128)} %bitcast.par_ref, bf16[2,512,1024]{2,1,0:T(8,128)(2,1)S(1)} %pad_maximum_fusion.1.refs_0_, bf16[2,512,1024]{2,1,0:T(8,128)(2,1)} %collective-permute-done.6.refs_1_, bf16[2,512,768]{2,1,0:T(8,128)(2,1)S(1)} %attention_back.1.refs_2_, ...), custom_call_target="tpu_custom_call" | custom-call | flops 536870912 | bytes 6815744 | tf_op jit(solution)/shard_map/step_weights/pallas_call | solution.py:253
  150.6 10.3 %collective-permute-start.32 = (bf16[2,1024,128]{2,1,0:T(8,128)(2,1)S(1)}, bf16[2,1024,128]{2,1,0:T(8,128)(2,1)S(1)}, u32[]{:S(2)}, u32[]{:S(2)}) collective-permute-start(bf16[2,1024,128]{2,1,0:T(8,128)(2,1)S(1)} %get-tuple-element.170), channel_id=1, source_target_pairs={{0,24},{8,0},{16,8},{24,16},{1,25},{9,1},{17,9},{25,17},{2,26},{10... | collective-permute-start | bytes 1572872 | tf_op jit(solution)/shard_map/ppermute | solution.py:45
  160.9 4.1 %step_weights.17 = (f32[2,1024,128]{2,1,0:T(8,128)S(1)}, bf16[2,1024,128]{2,1,0:T(8,128)(2,1)S(1)}) custom-call(s32[1]{0:T(128)} %bitcast.par_ref, bf16[2,512,1024]{2,1,0:T(8,128)(2,1)S(1)} %pad_maximum_fusion.1.refs_0_, bf16[2,512,1024]{2,1,0:T(8,128)(2,1)} %collective-permute-done.6.refs_1_, bf16[2,512,768]{2,1,0:T(8,128)(2,1)S(1)} %attention_back.1.refs_2_, ...), custom_call_target="tpu_custom_call" | custom-call | flops 536870912 | bytes 6815744 | tf_op jit(solution)/shard_map/step_weights/pallas_call | solution.py:253
  164.9 4.0 %step_weights.18 = (f32[2,1024,128]{2,1,0:T(8,128)S(1)}, bf16[2,1024,128]{2,1,0:T(8,128)(2,1)S(1)}) custom-call(s32[1]{0:T(128)} %bitcast.par_ref, bf16[2,512,1024]{2,1,0:T(8,128)(2,1)S(1)} %pad_maximum_fusion.1.refs_0_, bf16[2,512,1024]{2,1,0:T(8,128)(2,1)} %collective-permute-done.6.refs_1_, bf16[2,512,768]{2,1,0:T(8,128)(2,1)S(1)} %attention_back.1.refs_2_, ...), custom_call_target="tpu_custom_call" | custom-call | flops 536870912 | bytes 6815744 | tf_op jit(solution)/shard_map/step_weights/pallas_call | solution.py:253
  169.1 3.3 %collective-permute-done.33.low_ref = bf16[2,1024,128]{2,1,0:T(8,128)(2,1)S(1)} collective-permute-done((bf16[2,1024,128]{2,1,0:T(8,128)(2,1)S(1)}, bf16[2,1024,128]{2,1,0:T(8,128)(2,1)S(1)}, u32[]{:S(2)}, u32[]{:S(2)}) %collective-permute-start.33) | collective-permute-done | bytes 524320 | tf_op jit(solution)/shard_map/ppermute | solution.py:45
  172.4 10.9 %collective-permute-start.30 = (bf16[2,1024,128]{2,1,0:T(8,128)(2,1)S(1)}, bf16[2,1024,128]{2,1,0:T(8,128)(2,1)S(1)}, u32[]{:S(2)}, u32[]{:S(2)}) collective-permute-start(bf16[2,1024,128]{2,1,0:T(8,128)(2,1)S(1)} %get-tuple-element.169), channel_id=1, source_target_pairs={{0,24},{8,0},{16,8},{24,16},{1,25},{9,1},{17,9},{25,17},{2,26},{10... | collective-permute-start | bytes 1572872 | tf_op jit(solution)/shard_map/ppermute | solution.py:45
  184.1 4.0 %step_weights.19 = (f32[2,1024,128]{2,1,0:T(8,128)S(1)}, bf16[2,1024,128]{2,1,0:T(8,128)(2,1)S(1)}) custom-call(s32[1]{0:T(128)} %bitcast.par_ref, bf16[2,512,1024]{2,1,0:T(8,128)(2,1)S(1)} %pad_maximum_fusion.1.refs_0_, bf16[2,512,1024]{2,1,0:T(8,128)(2,1)} %collective-permute-done.6.refs_1_, bf16[2,512,768]{2,1,0:T(8,128)(2,1)S(1)} %attention_back.1.refs_2_, ...), custom_call_target="tpu_custom_call" | custom-call | flops 536870912 | bytes 6815744 | tf_op jit(solution)/shard_map/step_weights/pallas_call | solution.py:253
  188.1 6.9 %collective-permute-done.31.low_ref = bf16[2,1024,128]{2,1,0:T(8,128)(2,1)S(1)} collective-permute-done((bf16[2,1024,128]{2,1,0:T(8,128)(2,1)S(1)}, bf16[2,1024,128]{2,1,0:T(8,128)(2,1)S(1)}, u32[]{:S(2)}, u32[]{:S(2)}) %collective-permute-start.31) | collective-permute-done | bytes 524320 | tf_op jit(solution)/shard_map/ppermute | solution.py:45
  194.9 10.8 %collective-permute-start.28 = (bf16[2,1024,128]{2,1,0:T(8,128)(2,1)S(1)}, bf16[2,1024,128]{2,1,0:T(8,128)(2,1)S(1)}, u32[]{:S(2)}, u32[]{:S(2)}) collective-permute-start(bf16[2,1024,128]{2,1,0:T(8,128)(2,1)S(1)} %get-tuple-element.168), channel_id=1, source_target_pairs={{0,24},{8,0},{16,8},{24,16},{1,25},{9,1},{17,9},{25,17},{2,26},{10... | collective-permute-start | bytes 1572872 | tf_op jit(solution)/shard_map/ppermute | solution.py:45
  206.5 4.0 %step_weights.20 = (f32[2,1024,128]{2,1,0:T(8,128)S(1)}, bf16[2,1024,128]{2,1,0:T(8,128)(2,1)S(1)}) custom-call(s32[1]{0:T(128)} %bitcast.par_ref, bf16[2,512,1024]{2,1,0:T(8,128)(2,1)S(1)} %pad_maximum_fusion.1.refs_0_, bf16[2,512,1024]{2,1,0:T(8,128)(2,1)} %collective-permute-done.6.refs_1_, bf16[2,512,768]{2,1,0:T(8,128)(2,1)S(1)} %attention_back.1.refs_2_, ...), custom_call_target="tpu_custom_call" | custom-call | flops 536870912 | bytes 6815744 | tf_op jit(solution)/shard_map/step_weights/pallas_call | solution.py:253
  210.5 6.9 %collective-permute-done.29.low_ref = bf16[2,1024,128]{2,1,0:T(8,128)(2,1)S(1)} collective-permute-done((bf16[2,1024,128]{2,1,0:T(8,128)(2,1)S(1)}, bf16[2,1024,128]{2,1,0:T(8,128)(2,1)S(1)}, u32[]{:S(2)}, u32[]{:S(2)}) %collective-permute-start.29) | collective-permute-done | bytes 524320 | tf_op jit(solution)/shard_map/ppermute | solution.py:45
  217.4 10.7 %collective-permute-start.26 = (bf16[2,1024,128]{2,1,0:T(8,128)(2,1)S(1)}, bf16[2,1024,128]{2,1,0:T(8,128)(2,1)S(1)}, u32[]{:S(2)}, u32[]{:S(2)}) collective-permute-start(bf16[2,1024,128]{2,1,0:T(8,128)(2,1)S(1)} %get-tuple-element.167), channel_id=1, source_target_pairs={{0,24},{8,0},{16,8},{24,16},{1,25},{9,1},{17,9},{25,17},{2,26},{10... | collective-permute-start | bytes 1572872 | tf_op jit(solution)/shard_map/ppermute | solution.py:45
  228.9 11.1 %collective-permute-done.27.low_ref = bf16[2,1024,128]{2,1,0:T(8,128)(2,1)S(1)} collective-permute-done((bf16[2,1024,128]{2,1,0:T(8,128)(2,1)S(1)}, bf16[2,1024,128]{2,1,0:T(8,128)(2,1)S(1)}, u32[]{:S(2)}, u32[]{:S(2)}) %collective-permute-start.27) | collective-permute-done | bytes 524320 | tf_op jit(solution)/shard_map/ppermute | solution.py:45
  240.0 10.6 %collective-permute-start.24 = (bf16[2,1024,128]{2,1,0:T(8,128)(2,1)S(1)}, bf16[2,1024,128]{2,1,0:T(8,128)(2,1)S(1)}, u32[]{:S(2)}, u32[]{:S(2)}) collective-permute-start(bf16[2,1024,128]{2,1,0:T(8,128)(2,1)S(1)} %get-tuple-element.166), channel_id=1, source_target_pairs={{0,24},{8,0},{16,8},{24,16},{1,25},{9,1},{17,9},{25,17},{2,26},{10... | collective-permute-start | bytes 1572872 | tf_op jit(solution)/shard_map/ppermute | solution.py:45
  250.6 4.0 %step_weights.21 = (f32[2,1024,128]{2,1,0:T(8,128)S(1)}, bf16[2,1024,128]{2,1,0:T(8,128)(2,1)S(1)}) custom-call(s32[1]{0:T(128)} %bitcast.par_ref, bf16[2,512,1024]{2,1,0:T(8,128)(2,1)S(1)} %pad_maximum_fusion.1.refs_0_, bf16[2,512,1024]{2,1,0:T(8,128)(2,1)} %collective-permute-done.6.refs_1_, bf16[2,512,768]{2,1,0:T(8,128)(2,1)S(1)} %attention_back.1.refs_2_, ...), custom_call_target="tpu_custom_call" | custom-call | flops 536870912 | bytes 6815744 | tf_op jit(solution)/shard_map/step_weights/pallas_call | solution.py:253
  254.6 7.8 %collective-permute-done.25.low_ref = bf16[2,1024,128]{2,1,0:T(8,128)(2,1)S(1)} collective-permute-done((bf16[2,1024,128]{2,1,0:T(8,128)(2,1)S(1)}, bf16[2,1024,128]{2,1,0:T(8,128)(2,1)S(1)}, u32[]{:S(2)}, u32[]{:S(2)}) %collective-permute-start.25) | collective-permute-done | bytes 524320 | tf_op jit(solution)/shard_map/ppermute | solution.py:45
  262.5 10.5 %collective-permute-start.22 = (bf16[2,1024,128]{2,1,0:T(8,128)(2,1)S(1)}, bf16[2,1024,128]{2,1,0:T(8,128)(2,1)S(1)}, u32[]{:S(2)}, u32[]{:S(2)}) collective-permute-start(bf16[2,1024,128]{2,1,0:T(8,128)(2,1)S(1)} %get-tuple-element.165), channel_id=1, source_target_pairs={{0,24},{8,0},{16,8},{24,16},{1,25},{9,1},{17,9},{25,17},{2,26},{10... | collective-permute-start | bytes 1572872 | tf_op jit(solution)/shard_map/ppermute | solution.py:45
  287.4 8.5 %collective-permute-done.24.high_ref = bf16[2,1024,128]{2,1,0:T(8,128)(2,1)S(1)} collective-permute-done((bf16[2,1024,128]{2,1,0:T(8,128)(2,1)S(1)}, bf16[2,1024,128]{2,1,0:T(8,128)(2,1)S(1)}, u32[]{:S(2)}, u32[]{:S(2)}) %collective-permute-start.24) | collective-permute-done | bytes 524320 | tf_op jit(solution)/shard_map/ppermute | solution.py:45
  297.5 10.0 %collective-permute-done.21.low_ref = bf16[2,1024,128]{2,1,0:T(8,128)(2,1)S(1)} collective-permute-done((bf16[2,1024,128]{2,1,0:T(8,128)(2,1)S(1)}, bf16[2,1024,128]{2,1,0:T(8,128)(2,1)S(1)}, u32[]{:S(2)}, u32[]{:S(2)}) %collective-permute-start.21) | collective-permute-done | bytes 524320 | tf_op jit(solution)/shard_map/ppermute | solution.py:45
  307.5 8.8 %collective-permute-done.22.high_ref = bf16[2,1024,128]{2,1,0:T(8,128)(2,1)S(1)} collective-permute-done((bf16[2,1024,128]{2,1,0:T(8,128)(2,1)S(1)}, bf16[2,1024,128]{2,1,0:T(8,128)(2,1)S(1)}, u32[]{:S(2)}, u32[]{:S(2)}) %collective-permute-start.22) | collective-permute-done | bytes 524320 | tf_op jit(solution)/shard_map/ppermute | solution.py:45
  (104 shorter events, 49.0 us)
Async XLA Ops:
  0.6 29.6 %collective-permute-start = (bf16[512,1024]{1,0:T(8,128)(2,1)}, bf16[512,1024]{1,0:T(8,128)(2,1)S(1)}, u32[]{:S(2)}, u32[]{:S(2)}) collective-permute-start(bf16[512,1024]{1,0:T(8,128)(2,1)} %bitcast.67), channel_id=1, source_target_pairs={{0,2},{1,3},{2,6},{3,7},{4,0},{5,1},{6,4},{7,5},{8,10},{9,11},{10,... | collective-permute-start | bytes 3145736 | tf_op jit(solution)/shard_map/ppermute | solution.py:75
  3.6 26.6 %collective-permute-start.3 = (bf16[512,1024]{1,0:T(8,128)(2,1)}, bf16[512,1024]{1,0:T(8,128)(2,1)S(1)}, u32[]{:S(2)}, u32[]{:S(2)}) collective-permute-start(bf16[512,1024]{1,0:T(8,128)(2,1)} %bitcast.68), channel_id=1, source_target_pairs={{2,4},{3,5},{4,2},{5,3},{10,12},{11,13},{12,10},{13,11},{18,20},{1... | collective-permute-start | bytes 3145736 | tf_op jit(solution)/shard_map/ppermute | solution.py:75
  5.9 1.5 collective-permute-start.1
  7.3 22.9 %collective-permute-start.2 = (f32[512]{0:T(512)S(1)}, f32[512]{0:T(512)S(1)}, u32[]{:S(2)}, u32[]{:S(2)}) collective-permute-start(f32[512]{0:T(512)S(1)} %add.21), channel_id=1, source_target_pairs={{0,2},{1,3},{2,0},{3,1},{4,6},{5,7},{6,4},{7,5},{8,10},{9,11},{10,... | collective-permute-start | bytes 6152 | tf_op jit(solution)/shard_map/ppermute | solution.py:321
  10.1 20.1 %collective-permute-start.5 = (f32[512]{0:T(512)S(1)}, f32[512]{0:T(512)S(1)}, u32[]{:S(2)}, u32[]{:S(2)}) collective-permute-start(f32[512]{0:T(512)S(1)} %add.21), channel_id=1, source_target_pairs={{0,6},{1,7},{2,4},{3,5},{4,2},{5,3},{6,0},{7,1},{8,14},{9,15},{10,... | collective-permute-start | bytes 6152 | tf_op jit(solution)/shard_map/ppermute | solution.py:335
  13.1 2.6 copy-start.4
  13.1 2.8 copy-start.5
  15.9 3.3 %copy-start = (f32[1,2048,512]{2,1,0:T(8,128)S(1)}, f32[1,2048,512]{2,1,0:T(8,128)}, u32[]{:S(2)}) copy-start(f32[1,2048,512]{2,1,0:T(8,128)} %param.14) | copy-start | bytes 12582916
  15.9 14.3 %collective-permute-start.4 = (f32[1024]{0:T(1024)S(1)}, f32[1024]{0:T(1024)S(1)}, u32[]{:S(2)}, u32[]{:S(2)}) collective-permute-start(f32[1024]{0:T(1024)S(1)} %pad_maximum_fusion.8), channel_id=1, source_target_pairs={{0,4},{4,0},{1,5},{5,1},{2,6},{6,2},{3,7},{7,3},{8,12},{12,8},{9,1... | collective-permute-start | bytes 12296 | tf_op jit(solution)/shard_map/ppermute | solution.py:45
  19.2 11.0 %copy-start.8 = (bf16[1,2,256,1024]{3,2,1,0:T(8,128)(2,1)S(1)}, bf16[1,2,256,1024]{3,2,1,0:T(8,128)(2,1)}, u32[]{:S(2)}) copy-start(bf16[1,2,256,1024]{3,2,1,0:T(8,128)(2,1)} %param.8) | copy-start | bytes 3145732
  31.1 5.1 %collective-permute-start.6 = (bf16[2,512,1024]{2,1,0:T(8,128)(2,1)S(1)}, bf16[2,512,1024]{2,1,0:T(8,128)(2,1)}, u32[]{:S(2)}, u32[]{:S(2)}) collective-permute-start(bf16[2,512,1024]{2,1,0:T(8,128)(2,1)S(1)} %pad_maximum_fusion.1.refs_0_), channel_id=1, source_target_pairs={{0,1},{1,0},{2,3},{3,2},{4,5},{5,4},{6,7},{7,6},{8,9},{9,8},{10,11... | collective-permute-start | bytes 6291464 | tf_op jit(solution)/shard_map/ppermute | solution.py:79
  31.1 26.3 %collective-permute-start.8 = (bf16[512,1024]{1,0:T(8,128)(2,1)}, bf16[512,1024]{1,0:T(8,128)(2,1)}, u32[]{:S(2)}, u32[]{:S(2)}) collective-permute-start(bf16[512,1024]{1,0:T(8,128)(2,1)} %bitcast.8), channel_id=1, source_target_pairs={{0,2},{1,3},{2,6},{3,7},{4,0},{5,1},{6,4},{7,5},{8,10},{9,11},{10,... | collective-permute-start | bytes 3145736 | tf_op jit(solution)/shard_map/ppermute | solution.py:75
  33.8 23.6 %collective-permute-start.9 = (bf16[512,1024]{1,0:T(8,128)(2,1)}, bf16[512,1024]{1,0:T(8,128)(2,1)}, u32[]{:S(2)}, u32[]{:S(2)}) collective-permute-start(bf16[512,1024]{1,0:T(8,128)(2,1)} %bitcast.8), channel_id=1, source_target_pairs={{2,4},{3,5},{4,2},{5,3},{10,12},{11,13},{12,10},{13,11},{18,20},{1... | collective-permute-start | bytes 3145736 | tf_op jit(solution)/shard_map/ppermute | solution.py:75
  36.2 1.9 copy-start.3
  42.1 33.7 %collective-permute-start.14 = (bf16[2,512,384]{2,1,0:T(8,128)(2,1)S(1)}, bf16[2,512,384]{2,1,0:T(8,128)(2,1)S(1)}, u32[]{:S(2)}, u32[]{:S(2)}) collective-permute-start(bf16[2,512,384]{2,1,0:T(8,128)(2,1)S(1)} %get-tuple-element.106), channel_id=1, source_target_pairs={{0,4},{4,0},{1,5},{5,1},{2,6},{6,2},{3,7},{7,3},{8,12},{12,8},{9,1... | collective-permute-start | bytes 2359304 | tf_op jit(solution)/shard_map/ppermute | solution.py:45
  48.5 5.6 %collective-permute-start.7 = (f32[1]{0:T(128)}, f32[1]{0:T(128)}, u32[]{:S(2)}, u32[]{:S(2)}) collective-permute-start(f32[1]{0:T(128)} %param.15), channel_id=1, source_target_pairs={{0,8},{8,16},{16,24},{24,0},{1,9},{9,17},{17,25},{25,1},{2,10},{10... | collective-permute-start | bytes 20 | tf_op jit(solution)/shard_map/ppermute | solution.py:45
  59.6 20.9 %copy-start.1 = (f32[1,2048,512]{2,1,0:T(8,128)S(1)}, f32[1,2048,512]{2,1,0:T(8,128)}, u32[]{:S(2)}) copy-start(f32[1,2048,512]{2,1,0:T(8,128)} %param.14) | copy-start | bytes 12582916
  59.7 20.7 %collective-permute-start.13 = (bf16[2,128,1024]{2,1,0:T(8,128)(2,1)S(1)}, bf16[2,128,1024]{2,1,0:T(8,128)(2,1)S(1)}, u32[]{:S(2)}, u32[]{:S(2)}) collective-permute-start(bf16[2,128,1024]{2,1,0:T(8,128)(2,1)S(1)} %pad_maximum_fusion.5.refs_6_), channel_id=1, source_target_pairs={{0,1},{1,0},{2,3},{3,2},{4,5},{5,4},{6,7},{7,6},{8,9},{9,8},{10,11... | collective-permute-start | bytes 1572872 | tf_op jit(solution)/shard_map/ppermute | solution.py:79
  59.8 20.7 %collective-permute-start.12 = (bf16[2,128,1024]{2,1,0:T(8,128)(2,1)S(1)}, bf16[2,128,1024]{2,1,0:T(8,128)(2,1)S(1)}, u32[]{:S(2)}, u32[]{:S(2)}) collective-permute-start(bf16[2,128,1024]{2,1,0:T(8,128)(2,1)S(1)} %pad_maximum_fusion.4.refs_4_), channel_id=1, source_target_pairs={{0,1},{1,0},{2,3},{3,2},{4,5},{5,4},{6,7},{7,6},{8,9},{9,8},{10,11... | collective-permute-start | bytes 1572872 | tf_op jit(solution)/shard_map/ppermute | solution.py:79
  60.3 20.2 %collective-permute-start.11 = (bf16[2,128,1024]{2,1,0:T(8,128)(2,1)S(1)}, bf16[2,128,1024]{2,1,0:T(8,128)(2,1)S(1)}, u32[]{:S(2)}, u32[]{:S(2)}) collective-permute-start(bf16[2,128,1024]{2,1,0:T(8,128)(2,1)S(1)} %pad_maximum_fusion.3.refs_2_), channel_id=1, source_target_pairs={{0,1},{1,0},{2,3},{3,2},{4,5},{5,4},{6,7},{7,6},{8,9},{9,8},{10,11... | collective-permute-start | bytes 1572872 | tf_op jit(solution)/shard_map/ppermute | solution.py:79
  60.4 20.1 %collective-permute-start.10 = (bf16[2,128,1024]{2,1,0:T(8,128)(2,1)S(1)}, bf16[2,128,1024]{2,1,0:T(8,128)(2,1)S(1)}, u32[]{:S(2)}, u32[]{:S(2)}) collective-permute-start(bf16[2,128,1024]{2,1,0:T(8,128)(2,1)S(1)} %pad_maximum_fusion.2.refs_0_), channel_id=1, source_target_pairs={{0,1},{1,0},{2,3},{3,2},{4,5},{5,4},{6,7},{7,6},{8,9},{9,8},{10,11... | collective-permute-start | bytes 1572872 | tf_op jit(solution)/shard_map/ppermute | solution.py:79
  77.9 20.3 %collective-permute-start.15 = (bf16[2,512,384]{2,1,0:T(8,128)(2,1)S(1)}, bf16[2,512,384]{2,1,0:T(8,128)(2,1)S(1)}, u32[]{:S(2)}, u32[]{:S(2)}) collective-permute-start(bf16[2,512,384]{2,1,0:T(8,128)(2,1)S(1)} %get-tuple-element.135), channel_id=1, source_target_pairs={{0,4},{4,0},{1,5},{5,1},{2,6},{6,2},{3,7},{7,3},{8,12},{12,8},{9,1... | collective-permute-start | bytes 2359304 | tf_op jit(solution)/shard_map/ppermute | solution.py:45
  82.0 11.1 %collective-permute-start.16 = (bf16[2,512,128]{2,1,0:T(8,128)(2,1)S(1)}, bf16[2,512,128]{2,1,0:T(8,128)(2,1)S(1)}, u32[]{:S(2)}, u32[]{:S(2)}) collective-permute-start(bf16[2,512,128]{2,1,0:T(8,128)(2,1)S(1)} %get-tuple-element.136), channel_id=1, source_target_pairs={{0,8},{8,16},{16,24},{24,0},{1,9},{9,17},{17,25},{25,1},{2,10},{10... | collective-permute-start | bytes 786440 | tf_op jit(solution)/shard_map/ppermute | solution.py:45
  83.8 13.3 %collective-permute-start.17 = (bf16[2,512,128]{2,1,0:T(8,128)(2,1)S(1)}, bf16[2,512,128]{2,1,0:T(8,128)(2,1)S(1)}, u32[]{:S(2)}, u32[]{:S(2)}) collective-permute-start(bf16[2,512,128]{2,1,0:T(8,128)(2,1)S(1)} %get-tuple-element.136), channel_id=1, source_target_pairs={{0,24},{8,0},{16,8},{24,16},{1,25},{9,1},{17,9},{25,17},{2,26},{10... | collective-permute-start | bytes 786440 | tf_op jit(solution)/shard_map/ppermute | solution.py:45
  85.9 1.6 copy-start.7
  98.2 36.6 %collective-permute-start.18 = (bf16[2,512,512]{2,1,0:T(8,128)(2,1)S(1)}, bf16[2,512,512]{2,1,0:T(8,128)(2,1)S(1)}, u32[]{:S(2)}, u32[]{:S(2)}) collective-permute-start(bf16[2,512,512]{2,1,0:T(8,128)(2,1)S(1)} %get-tuple-element.138), channel_id=1, source_target_pairs={{0,4},{4,0},{1,5},{5,1},{2,6},{6,2},{3,7},{7,3},{8,12},{12,8},{9,1... | collective-permute-start | bytes 3145736 | tf_op jit(solution)/shard_map/ppermute | solution.py:45
  99.9 14.2 %collective-permute-start.19 = (bf16[2,512,128]{2,1,0:T(8,128)(2,1)S(1)}, bf16[2,512,128]{2,1,0:T(8,128)(2,1)S(1)}, u32[]{:S(2)}, u32[]{:S(2)}) collective-permute-start(bf16[2,512,128]{2,1,0:T(8,128)(2,1)S(1)} %get-tuple-element.145), channel_id=1, source_target_pairs={{0,8},{8,16},{16,24},{24,0},{1,9},{9,17},{17,25},{25,1},{2,10},{10... | collective-permute-start | bytes 786440 | tf_op jit(solution)/shard_map/ppermute | solution.py:45
  101.7 23.2 %collective-permute-start.20 = (bf16[2,512,128]{2,1,0:T(8,128)(2,1)S(1)}, bf16[2,512,128]{2,1,0:T(8,128)(2,1)S(1)}, u32[]{:S(2)}, u32[]{:S(2)}) collective-permute-start(bf16[2,512,128]{2,1,0:T(8,128)(2,1)S(1)} %get-tuple-element.145), channel_id=1, source_target_pairs={{0,24},{8,0},{16,8},{24,16},{1,25},{9,1},{17,9},{25,17},{2,26},{10... | collective-permute-start | bytes 786440 | tf_op jit(solution)/shard_map/ppermute | solution.py:45
  110.3 32.4 %collective-permute-start.37 = (bf16[2,1024,128]{2,1,0:T(8,128)(2,1)S(1)}, bf16[2,1024,128]{2,1,0:T(8,128)(2,1)S(1)}, u32[]{:S(2)}, u32[]{:S(2)}) collective-permute-start(bf16[2,1024,128]{2,1,0:T(8,128)(2,1)S(1)} %get-tuple-element.173), channel_id=1, source_target_pairs={{0,8},{8,16},{16,24},{24,0},{1,9},{9,17},{17,25},{25,1},{2,10},{10... | collective-permute-start | bytes 1572872 | tf_op jit(solution)/shard_map/ppermute | solution.py:45
  110.3 40.2 %collective-permute-start.38 = (bf16[2,1024,128]{2,1,0:T(8,128)(2,1)S(1)}, bf16[2,1024,128]{2,1,0:T(8,128)(2,1)S(1)}, u32[]{:S(2)}, u32[]{:S(2)}) collective-permute-start(bf16[2,1024,128]{2,1,0:T(8,128)(2,1)S(1)} %get-tuple-element.173), channel_id=1, source_target_pairs={{0,24},{8,0},{16,8},{24,16},{1,25},{9,1},{17,9},{25,17},{2,26},{10... | collective-permute-start | bytes 1572872 | tf_op jit(solution)/shard_map/ppermute | solution.py:45
  127.9 22.7 %collective-permute-start.35 = (bf16[2,1024,128]{2,1,0:T(8,128)(2,1)S(1)}, bf16[2,1024,128]{2,1,0:T(8,128)(2,1)S(1)}, u32[]{:S(2)}, u32[]{:S(2)}) collective-permute-start(bf16[2,1024,128]{2,1,0:T(8,128)(2,1)S(1)} %get-tuple-element.172), channel_id=1, source_target_pairs={{0,8},{8,16},{16,24},{24,0},{1,9},{9,17},{17,25},{25,1},{2,10},{10... | collective-permute-start | bytes 1572872 | tf_op jit(solution)/shard_map/ppermute | solution.py:45
  127.9 41.1 %collective-permute-start.36 = (bf16[2,1024,128]{2,1,0:T(8,128)(2,1)S(1)}, bf16[2,1024,128]{2,1,0:T(8,128)(2,1)S(1)}, u32[]{:S(2)}, u32[]{:S(2)}) collective-permute-start(bf16[2,1024,128]{2,1,0:T(8,128)(2,1)S(1)} %get-tuple-element.172), channel_id=1, source_target_pairs={{0,24},{8,0},{16,8},{24,16},{1,25},{9,1},{17,9},{25,17},{2,26},{10... | collective-permute-start | bytes 1572872 | tf_op jit(solution)/shard_map/ppermute | solution.py:45
  134.8 37.7 %collective-permute-start.33 = (bf16[2,1024,128]{2,1,0:T(8,128)(2,1)S(1)}, bf16[2,1024,128]{2,1,0:T(8,128)(2,1)S(1)}, u32[]{:S(2)}, u32[]{:S(2)}) collective-permute-start(bf16[2,1024,128]{2,1,0:T(8,128)(2,1)S(1)} %get-tuple-element.171), channel_id=1, source_target_pairs={{0,8},{8,16},{16,24},{24,0},{1,9},{9,17},{17,25},{25,1},{2,10},{10... | collective-permute-start | bytes 1572872 | tf_op jit(solution)/shard_map/ppermute | solution.py:45
  142.7 18.2 %copy-start.6 = (f32[1,2048,128]{2,1,0:T(8,128)S(1)}, f32[1,2048,128]{2,1,0:T(8,128)}, u32[]{:S(2)}) copy-start(f32[1,2048,128]{2,1,0:T(8,128)} %param.13) | copy-start | bytes 3145732
  142.7 41.0 %collective-permute-start.34 = (bf16[2,1024,128]{2,1,0:T(8,128)(2,1)S(1)}, bf16[2,1024,128]{2,1,0:T(8,128)(2,1)S(1)}, u32[]{:S(2)}, u32[]{:S(2)}) collective-permute-start(bf16[2,1024,128]{2,1,0:T(8,128)(2,1)S(1)} %get-tuple-element.171), channel_id=1, source_target_pairs={{0,24},{8,0},{16,8},{24,16},{1,25},{9,1},{17,9},{25,17},{2,26},{10... | collective-permute-start | bytes 1572872 | tf_op jit(solution)/shard_map/ppermute | solution.py:45
  150.5 44.4 %collective-permute-start.31 = (bf16[2,1024,128]{2,1,0:T(8,128)(2,1)S(1)}, bf16[2,1024,128]{2,1,0:T(8,128)(2,1)S(1)}, u32[]{:S(2)}, u32[]{:S(2)}) collective-permute-start(bf16[2,1024,128]{2,1,0:T(8,128)(2,1)S(1)} %get-tuple-element.170), channel_id=1, source_target_pairs={{0,8},{8,16},{16,24},{24,0},{1,9},{9,17},{17,25},{25,1},{2,10},{10... | collective-permute-start | bytes 1572872 | tf_op jit(solution)/shard_map/ppermute | solution.py:45
  150.6 55.6 %collective-permute-start.32 = (bf16[2,1024,128]{2,1,0:T(8,128)(2,1)S(1)}, bf16[2,1024,128]{2,1,0:T(8,128)(2,1)S(1)}, u32[]{:S(2)}, u32[]{:S(2)}) collective-permute-start(bf16[2,1024,128]{2,1,0:T(8,128)(2,1)S(1)} %get-tuple-element.170), channel_id=1, source_target_pairs={{0,24},{8,0},{16,8},{24,16},{1,25},{9,1},{17,9},{25,17},{2,26},{10... | collective-permute-start | bytes 1572872 | tf_op jit(solution)/shard_map/ppermute | solution.py:45
  160.8 4.1 %copy-start.2 = (f32[1,2048,512]{2,1,0:T(8,128)S(1)}, f32[1,2048,512]{2,1,0:T(8,128)}, u32[]{:S(2)}) copy-start(f32[1,2048,512]{2,1,0:T(8,128)} %param.11) | copy-start | bytes 12582916
  169.0 48.4 %collective-permute-start.29 = (bf16[2,1024,128]{2,1,0:T(8,128)(2,1)S(1)}, bf16[2,1024,128]{2,1,0:T(8,128)(2,1)S(1)}, u32[]{:S(2)}, u32[]{:S(2)}) collective-permute-start(bf16[2,1024,128]{2,1,0:T(8,128)(2,1)S(1)} %get-tuple-element.169), channel_id=1, source_target_pairs={{0,8},{8,16},{16,24},{24,0},{1,9},{9,17},{17,25},{25,1},{2,10},{10... | collective-permute-start | bytes 1572872 | tf_op jit(solution)/shard_map/ppermute | solution.py:45
  172.4 56.2 %collective-permute-start.30 = (bf16[2,1024,128]{2,1,0:T(8,128)(2,1)S(1)}, bf16[2,1024,128]{2,1,0:T(8,128)(2,1)S(1)}, u32[]{:S(2)}, u32[]{:S(2)}) collective-permute-start(bf16[2,1024,128]{2,1,0:T(8,128)(2,1)S(1)} %get-tuple-element.169), channel_id=1, source_target_pairs={{0,24},{8,0},{16,8},{24,16},{1,25},{9,1},{17,9},{25,17},{2,26},{10... | collective-permute-start | bytes 1572872 | tf_op jit(solution)/shard_map/ppermute | solution.py:45
  183.7 56.3 %collective-permute-start.27 = (bf16[2,1024,128]{2,1,0:T(8,128)(2,1)S(1)}, bf16[2,1024,128]{2,1,0:T(8,128)(2,1)S(1)}, u32[]{:S(2)}, u32[]{:S(2)}) collective-permute-start(bf16[2,1024,128]{2,1,0:T(8,128)(2,1)S(1)} %get-tuple-element.168), channel_id=1, source_target_pairs={{0,8},{8,16},{16,24},{24,0},{1,9},{9,17},{17,25},{25,1},{2,10},{10... | collective-permute-start | bytes 1572872 | tf_op jit(solution)/shard_map/ppermute | solution.py:45
  194.9 59.6 %collective-permute-start.28 = (bf16[2,1024,128]{2,1,0:T(8,128)(2,1)S(1)}, bf16[2,1024,128]{2,1,0:T(8,128)(2,1)S(1)}, u32[]{:S(2)}, u32[]{:S(2)}) collective-permute-start(bf16[2,1024,128]{2,1,0:T(8,128)(2,1)S(1)} %get-tuple-element.168), channel_id=1, source_target_pairs={{0,24},{8,0},{16,8},{24,16},{1,25},{9,1},{17,9},{25,17},{2,26},{10... | collective-permute-start | bytes 1572872 | tf_op jit(solution)/shard_map/ppermute | solution.py:45
  206.1 56.3 %collective-permute-start.25 = (bf16[2,1024,128]{2,1,0:T(8,128)(2,1)S(1)}, bf16[2,1024,128]{2,1,0:T(8,128)(2,1)S(1)}, u32[]{:S(2)}, u32[]{:S(2)}) collective-permute-start(bf16[2,1024,128]{2,1,0:T(8,128)(2,1)S(1)} %get-tuple-element.167), channel_id=1, source_target_pairs={{0,8},{8,16},{16,24},{24,0},{1,9},{9,17},{17,25},{25,1},{2,10},{10... | collective-permute-start | bytes 1572872 | tf_op jit(solution)/shard_map/ppermute | solution.py:45
  217.4 68.3 %collective-permute-start.26 = (bf16[2,1024,128]{2,1,0:T(8,128)(2,1)S(1)}, bf16[2,1024,128]{2,1,0:T(8,128)(2,1)S(1)}, u32[]{:S(2)}, u32[]{:S(2)}) collective-permute-start(bf16[2,1024,128]{2,1,0:T(8,128)(2,1)S(1)} %get-tuple-element.167), channel_id=1, source_target_pairs={{0,24},{8,0},{16,8},{24,16},{1,25},{9,1},{17,9},{25,17},{2,26},{10... | collective-permute-start | bytes 1572872 | tf_op jit(solution)/shard_map/ppermute | solution.py:45
  228.6 58.8 %collective-permute-start.23 = (bf16[2,1024,128]{2,1,0:T(8,128)(2,1)S(1)}, bf16[2,1024,128]{2,1,0:T(8,128)(2,1)S(1)}, u32[]{:S(2)}, u32[]{:S(2)}) collective-permute-start(bf16[2,1024,128]{2,1,0:T(8,128)(2,1)S(1)} %get-tuple-element.166), channel_id=1, source_target_pairs={{0,8},{8,16},{16,24},{24,0},{1,9},{9,17},{17,25},{25,1},{2,10},{10... | collective-permute-start | bytes 1572872 | tf_op jit(solution)/shard_map/ppermute | solution.py:45
  240.0 55.9 %collective-permute-start.24 = (bf16[2,1024,128]{2,1,0:T(8,128)(2,1)S(1)}, bf16[2,1024,128]{2,1,0:T(8,128)(2,1)S(1)}, u32[]{:S(2)}, u32[]{:S(2)}) collective-permute-start(bf16[2,1024,128]{2,1,0:T(8,128)(2,1)S(1)} %get-tuple-element.166), channel_id=1, source_target_pairs={{0,24},{8,0},{16,8},{24,16},{1,25},{9,1},{17,9},{25,17},{2,26},{10... | collective-permute-start | bytes 1572872 | tf_op jit(solution)/shard_map/ppermute | solution.py:45
  254.6 52.9 %collective-permute-start.21 = (bf16[2,1024,128]{2,1,0:T(8,128)(2,1)S(1)}, bf16[2,1024,128]{2,1,0:T(8,128)(2,1)S(1)}, u32[]{:S(2)}, u32[]{:S(2)}) collective-permute-start(bf16[2,1024,128]{2,1,0:T(8,128)(2,1)S(1)} %get-tuple-element.165), channel_id=1, source_target_pairs={{0,8},{8,16},{16,24},{24,0},{1,9},{9,17},{17,25},{25,1},{2,10},{10... | collective-permute-start | bytes 1572872 | tf_op jit(solution)/shard_map/ppermute | solution.py:45
  262.5 53.9 %collective-permute-start.22 = (bf16[2,1024,128]{2,1,0:T(8,128)(2,1)S(1)}, bf16[2,1024,128]{2,1,0:T(8,128)(2,1)S(1)}, u32[]{:S(2)}, u32[]{:S(2)}) collective-permute-start(bf16[2,1024,128]{2,1,0:T(8,128)(2,1)S(1)} %get-tuple-element.165), channel_id=1, source_target_pairs={{0,24},{8,0},{16,8},{24,16},{1,25},{9,1},{17,9},{25,17},{2,26},{10... | collective-permute-start | bytes 1572872 | tf_op jit(solution)/shard_map/ppermute | solution.py:45
